TPU v7x, 256 devices: a whole 4x4x8 slice. The times are simulated.
256 devices in a mesh: bfly: 256 (over z, x, y, core).
Axes of the slice: x: 4, y: 4, z: 8, core: 2. Of those that a mesh axis runs over, the one named last changes fastest.
Arguments:
- coeffs: float32 [256, 384, 1024], P('bfly'), may hold values from -6 to 6
- transfers: float32 [256, 8, 2, 384, 384], P('bfly'), may hold values from -0.21875 to 0.21875
Outputs:
- result: float32 [256, 384, 1024], P('bfly')
All inputs are finite; a program needn't handle non-finite values.
Results may differ from a plain program's by a relative error of at most 0.00014.
Values sent between devices are 32-bit elements; how exact they have to be, the bound alone decides.
No kernel may reach another device: no remote copies, remote signals or barrier semaphores. Data moves between devices by JAX's collectives and lax.ppermute only.
A program may use at most 64 MiB of HBM per device.

v0:
```python
import functools
import jax
import jax.numpy as jnp
from jax import lax
from jax.experimental import pallas as pl
from jax.experimental.pallas import tpu as pltpu
from jax.sharding import PartitionSpec as P

LEVELS = 8
WIDTHS = (128, 256, 128, 256, 256)
ORDER = (
    (0, 0), (0, 1), (2, 0), (0, 2), (2, 1), (4, 0), (0, 3), (2, 2), (4, 1), (0, 4), (3, 0), (2, 3),
    (0, 5), (4, 2), (2, 4), (0, 6), (3, 1), (4, 3), (2, 5), (0, 7), (4, 4), (3, 2), (2, 6), (4, 5),
    (3, 3), (1, 0), (2, 7), (1, 1), (3, 4), (4, 6), (2, 8), (1, 2), (3, 5), (1, 3), (4, 7), (0, 8),
    (1, 4), (1, 5), (3, 6), (1, 6), (4, 8), (3, 7), (1, 7), (3, 8), (1, 8),
)
ANY = pl.BlockSpec(memory_space=pl.ANY)
VMEM = pl.BlockSpec(memory_space=pltpu.VMEM)
PARAMS = pltpu.CompilerParams(vmem_limit_bytes=12 << 20)
TOKEN = pltpu.VMEM((8, 128), jnp.float32)
CHEAP = pl.CostEstimate(flops=1 << 33, bytes_accessed=1 << 10, transcendentals=0)


def partner(block, axis, stride):
    count = lax.axis_size(axis)
    route = []
    for low in range(count):
        high = low | 1 << stride
        if high != low and high < count:
            route += [(low, high), (high, low)]
    return lax.ppermute(block, axis, route)


def on_chip(values):
    return pltpu.with_memory_space_constraint(values, pltpu.VMEM)


def split(values):
    high = values.astype(jnp.bfloat16)
    return high, (values - high.astype(jnp.float32)).astype(jnp.bfloat16)


def in_hbm(values):
    return pltpu.with_memory_space_constraint(values, pltpu.HBM)


def split_kernel(token_ref, t_ref, out_ref, next_ref):
    rank = t_ref.shape[-1]
    rows = 16
    for which in range(2):
        @pl.loop(0, rank // rows)
        def _(i):
            here = pl.ds(pl.multiple_of(i * rows, rows), rows)
            there = pl.ds(pl.multiple_of(which * rank + i * rows, rows), rows)
            high, low = split(t_ref[0, 0, which, here])
            out_ref[there, :rank] = high
            out_ref[there, rank:2 * rank] = high
            out_ref[there, 2 * rank:] = low
    next_ref[...] = jnp.zeros_like(next_ref)


def split_matrices(token, transfers, level):
    rank = transfers.shape[-1]
    return pl.pallas_call(
        split_kernel,
        grid=(1,),
        out_shape=(pltpu.VMEM((2 * rank, 3 * rank), jnp.bfloat16), TOKEN),
        in_specs=[VMEM, pl.BlockSpec((1, 1, 2, rank, rank), lambda i: (0, level, 0, 0, 0))],
        out_specs=(VMEM, VMEM),
        cost_estimate=CHEAP,
        compiler_params=PARAMS,
        name="split_matrices",
    )(on_chip(token), in_hbm(transfers))


def multiply(t_ref, part_refs, send_ref, keep_ref, stacked):
    rank = send_ref.shape[0]
    step = 64

    @pl.loop(0, rank // step)
    def _(i):
        here = pl.multiple_of(i * step, step)
        current = part_refs[0][pl.ds(here, step)]
        for part_ref in part_refs[1:]:
            current = current + part_ref[pl.ds(here, step)]
        high, low = split(current)
        stacked[pl.ds(here, step)] = high
        stacked[pl.ds(pl.multiple_of(here + rank, step), step)] = low
        stacked[pl.ds(pl.multiple_of(here + 2 * rank, step), step)] = high

    rows = rank // 2

    @pl.loop(0, 4)
    def _(i):
        source = pl.ds(pl.multiple_of(i * rows, rows), rows)
        product = jnp.dot(t_ref[source], stacked[...], preferred_element_type=jnp.float32)

        @pl.when(i < 2)
        def _():
            keep_ref[source] = product

        @pl.when(i >= 2)
        def _():
            send_ref[pl.ds(pl.multiple_of((i - 2) * rows, rows), rows)] = product


def first_kernel(start, token_ref, t_ref, c_ref, send_ref, keep_ref, next_ref, stacked, block, sem):
    copy = pltpu.make_async_copy(c_ref.at[0, :, pl.ds(start, block.shape[1])], block, sem)
    copy.start()
    copy.wait()
    multiply(t_ref, (block,), send_ref, keep_ref, stacked)
    next_ref[...] = jnp.zeros_like(next_ref)


def level_kernel(token_ref, t_ref, kept_ref, arrived_ref, send_ref, keep_ref, next_ref, stacked):
    multiply(t_ref, (kept_ref, arrived_ref), send_ref, keep_ref, stacked)
    next_ref[...] = jnp.zeros_like(next_ref)


def stage(name, kernel, operands, specs, width, scratch=()):
    rank = operands[1].shape[0] // 2
    block = pltpu.VMEM((rank, width), jnp.float32)
    return pl.pallas_call(
        kernel,
        out_shape=(block, block, TOKEN),
        in_specs=specs,
        out_specs=(VMEM, VMEM, VMEM),
        scratch_shapes=[pltpu.VMEM((3 * rank, width), jnp.bfloat16), *scratch],
        cost_estimate=CHEAP,
        compiler_params=PARAMS,
        name=name,
    )(*operands)


def first_level(token, matrices, coeffs, start, width):
    scratch = (pltpu.VMEM((coeffs.shape[1], width), jnp.float32), pltpu.SemaphoreType.DMA)
    operands = (on_chip(token), on_chip(matrices), in_hbm(coeffs))
    kernel = functools.partial(first_kernel, start)
    return stage("first_level", kernel, operands, [VMEM, VMEM, ANY], width, scratch)


def next_level(token, matrices, kept, arrived):
    operands = tuple(map(on_chip, (token, matrices, kept, arrived)))
    return stage("next_level", level_kernel, operands, [VMEM] * 4, kept.shape[1])


def write_kernel(start, token_ref, kept_ref, arrived_ref, *refs):
    out_ref, next_ref, block, sem = refs[-4:]
    step = 64

    @pl.loop(0, block.shape[0] // step)
    def _(i):
        here = pl.ds(pl.multiple_of(i * step, step), step)
        block[here] = kept_ref[here] + arrived_ref[here]

    copy = pltpu.make_async_copy(block, out_ref.at[0, :, pl.ds(start, block.shape[1])], sem)
    copy.start()
    copy.wait()
    next_ref[...] = jnp.zeros_like(next_ref)


def write_result(token, kept, arrived, start, shape, result):
    parts = tuple(map(on_chip, (token, kept, arrived))) + (() if result is None else (result,))
    return pl.pallas_call(
        functools.partial(write_kernel, start),
        out_shape=(jax.ShapeDtypeStruct(shape, jnp.float32), TOKEN),
        in_specs=[VMEM] * 3 + [ANY] * (len(parts) - 3),
        out_specs=(ANY, VMEM),
        scratch_shapes=[pltpu.VMEM(kept.shape, jnp.float32), pltpu.SemaphoreType.DMA],
        input_output_aliases={} if result is None else {3: 0},
        cost_estimate=CHEAP,
        compiler_params=PARAMS,
        name="write_result",
    )(*parts)


def on_device(coeffs, transfers):
    bit_count = lax.axis_size("bfly").bit_length() - 1
    starts = [sum(WIDTHS[:i]) for i in range(len(WIDTHS))]
    parts = [()] * len(WIDTHS)
    token = jnp.zeros(TOKEN.shape, TOKEN.dtype)
    first, token = split_matrices(token, transfers, 0)
    matrices = [first]
    result = None
    for chunk, level in ORDER:
        if level == LEVELS:
            result, token = write_result(token, *parts[chunk], starts[chunk], coeffs.shape, result)
            continue
        if level == 0:
            stepped = first_level(token, matrices[0], coeffs, starts[chunk], WIDTHS[chunk])
        else:
            stepped = next_level(token, matrices[level], *parts[chunk])
        outgoing, kept, token = stepped
        parts[chunk] = (kept, partner(outgoing, "bfly", level % bit_count))
        if len(matrices) == level + 1 < LEVELS:
            following, token = split_matrices(token, transfers, level + 1)
            matrices.append(following)
    return result


def solution(mesh):
    return jax.shard_map(
        on_device,
        mesh=mesh,
        in_specs=(P("bfly", None, None), P("bfly", None, None, None, None)),
        out_specs=P("bfly", None, None),
        check_vma=False,
    )
```

profile of v0, /device:TPU:10, one launch (start us, length us, event | category | flops | bytes accessed | tf_op | source)
XLA Modules:
  0.0 257.0 jit_solution(4797473542966401989)
XLA Ops:
  0.0 1.7 split_matrices.8
  1.7 2.1 first_level.5
  4.0 1.7 split_matrices.9
  7.5 1.7 split_matrices.10
  9.2 2.1 first_level.6
  11.7 2.7 %collective-permute-done.1.arrived_ref = f32[384,128]{1,0:T(8,128)S(1)} collective-permute-done((f32[384,128]{1,0:T(8,128)S(1)}, f32[384,128]{1,0:T(8,128)S(1)}, u32[]{:S(2)}, u32[]{:S(2)}) %collective-permute-start.1) | collective-permute-done | bytes 196640 | tf_op jit(solution)/shard_map/ppermute | solution.py:31
  15.6 2.4 collective-permute-start.3
  17.9 1.7 split_matrices.11
  20.9 1.4 collective-permute-start.4
  22.4 2.4 first_level.7
  26.7 1.7 split_matrices.12
  29.7 1.6 collective-permute-start.7
  31.3 1.4 next_level.40
  34.7 2.2 collective-permute-start.8
  38.1 1.7 split_matrices.13
  39.8 2.4 first_level.8
  43.5 1.9 collective-permute-start.10
  46.6 2.0 collective-permute-start.11
  48.6 1.7 split_matrices.14
  50.3 1.4 next_level.44
  55.4 3.4 %collective-permute-start.15 = (f32[384,128]{1,0:T(8,128)S(1)}, f32[384,128]{1,0:T(8,128)S(1)}, u32[]{:S(2)}, u32[]{:S(2)}) collective-permute-start(f32[384,128]{1,0:T(8,128)S(1)} %get-tuple-element.216), channel_id=1, source_target_pairs={{0,64},{64,0},{1,65},{65,1},{2,66},{66,2},{3,67},{67,3},{4,68},{68... | collective-permute-start | bytes 589832 | tf_op jit(solution)/shard_map/ppermute | solution.py:31
  59.4 1.7 split_matrices.15
  61.2 1.4 next_level.47
  62.6 2.7 %collective-permute-start.17 = (f32[384,256]{1,0:T(8,128)S(1)}, f32[384,256]{1,0:T(8,128)S(1)}, u32[]{:S(2)}, u32[]{:S(2)}) collective-permute-start(f32[384,256]{1,0:T(8,128)S(1)} %get-tuple-element.222), channel_id=1, source_target_pairs={{0,2},{2,0},{1,3},{3,1},{4,6},{6,4},{5,7},{7,5},{8,10},{10,8},{9,1... | collective-permute-start | bytes 1179656 | tf_op jit(solution)/shard_map/ppermute | solution.py:31
  65.3 7.3 %collective-permute-done.13.arrived_ref = f32[384,256]{1,0:T(8,128)S(1)} collective-permute-done((f32[384,256]{1,0:T(8,128)S(1)}, f32[384,256]{1,0:T(8,128)S(1)}, u32[]{:S(2)}, u32[]{:S(2)}) %collective-permute-start.13) | collective-permute-done | bytes 393248 | tf_op jit(solution)/shard_map/ppermute | solution.py:31
  72.5 1.4 next_level.48
  73.9 1.8 collective-permute-start.16
  78.2 5.3 %collective-permute-start.30 = (f32[384,128]{1,0:T(8,128)S(1)}, f32[384,128]{1,0:T(8,128)S(1)}, u32[]{:S(2)}, u32[]{:S(2)}) collective-permute-start(f32[384,128]{1,0:T(8,128)S(1)} %get-tuple-element.262), channel_id=1, source_target_pairs={{0,128},{128,0},{1,129},{129,1},{2,130},{130,2},{3,131},{131,3},{4... | collective-permute-start | bytes 589832 | tf_op jit(solution)/shard_map/ppermute | solution.py:31
  85.9 1.7 collective-permute-start.19
  87.7 1.4 next_level.52
  89.1 4.8 %collective-permute-done.18.arrived_ref = f32[384,128]{1,0:T(8,128)S(1)} collective-permute-done((f32[384,128]{1,0:T(8,128)S(1)}, f32[384,128]{1,0:T(8,128)S(1)}, u32[]{:S(2)}, u32[]{:S(2)}) %collective-permute-start.18) | collective-permute-done | bytes 196640 | tf_op jit(solution)/shard_map/ppermute | solution.py:31
  95.1 1.8 collective-permute-start.21
  98.0 1.4 next_level.54
  99.7 6.5 %collective-permute-done.20.arrived_ref = f32[384,256]{1,0:T(8,128)S(1)} collective-permute-done((f32[384,256]{1,0:T(8,128)S(1)}, f32[384,256]{1,0:T(8,128)S(1)}, u32[]{:S(2)}, u32[]{:S(2)}) %collective-permute-start.20) | collective-permute-done | bytes 393248 | tf_op jit(solution)/shard_map/ppermute | solution.py:31
  107.6 2.4 first_level.9
  112.4 1.4 next_level.57
  115.0 8.0 %collective-permute-done.23.arrived_ref = f32[384,256]{1,0:T(8,128)S(1)} collective-permute-done((f32[384,256]{1,0:T(8,128)S(1)}, f32[384,256]{1,0:T(8,128)S(1)}, u32[]{:S(2)}, u32[]{:S(2)}) %collective-permute-start.23) | collective-permute-done | bytes 393248 | tf_op jit(solution)/shard_map/ppermute | solution.py:31
  123.0 1.4 next_level.58
  124.5 1.4 next_level.59
  125.9 2.6 collective-permute-start.29
  128.5 2.2 collective-permute-start.27
  131.4 1.4 next_level.60
  133.6 6.5 %collective-permute-done.27.arrived_ref = f32[384,256]{1,0:T(8,128)S(1)} collective-permute-done((f32[384,256]{1,0:T(8,128)S(1)}, f32[384,256]{1,0:T(8,128)S(1)}, u32[]{:S(2)}, u32[]{:S(2)}) %collective-permute-start.27) | collective-permute-done | bytes 393248 | tf_op jit(solution)/shard_map/ppermute | solution.py:31
  140.1 1.4 next_level.61
  141.5 3.0 %collective-permute-done.28.arrived_ref = f32[384,256]{1,0:T(8,128)S(1)} collective-permute-done((f32[384,256]{1,0:T(8,128)S(1)}, f32[384,256]{1,0:T(8,128)S(1)}, u32[]{:S(2)}, u32[]{:S(2)}) %collective-permute-start.28) | collective-permute-done | bytes 393248 | tf_op jit(solution)/shard_map/ppermute | solution.py:31
  144.5 1.4 next_level.62
  145.9 2.1 collective-permute-start.31
  148.0 1.4 next_level.63
  150.2 5.0 %collective-permute-done.31.arrived_ref = f32[384,256]{1,0:T(8,128)S(1)} collective-permute-done((f32[384,256]{1,0:T(8,128)S(1)}, f32[384,256]{1,0:T(8,128)S(1)}, u32[]{:S(2)}, u32[]{:S(2)}) %collective-permute-start.31) | collective-permute-done | bytes 393248 | tf_op jit(solution)/shard_map/ppermute | solution.py:31
  155.2 1.4 next_level.64
  157.8 4.3 %collective-permute-start.35 = (f32[384,256]{1,0:T(8,128)S(1)}, f32[384,256]{1,0:T(8,128)S(1)}, u32[]{:S(2)}, u32[]{:S(2)}) collective-permute-start(f32[384,256]{1,0:T(8,128)S(1)} %get-tuple-element.278), channel_id=1, source_target_pairs={{0,128},{128,0},{1,129},{129,1},{2,130},{130,2},{3,131},{131,3},{4... | collective-permute-start | bytes 1179656 | tf_op jit(solution)/shard_map/ppermute | solution.py:31
  162.1 4.4 %collective-permute-done.32.arrived_ref = f32[384,256]{1,0:T(8,128)S(1)} collective-permute-done((f32[384,256]{1,0:T(8,128)S(1)}, f32[384,256]{1,0:T(8,128)S(1)}, u32[]{:S(2)}, u32[]{:S(2)}) %collective-permute-start.32) | collective-permute-done | bytes 393248 | tf_op jit(solution)/shard_map/ppermute | solution.py:31
  166.5 1.4 next_level.65
  168.0 14.4 %collective-permute-done.33.arrived_ref = f32[384,256]{1,0:T(8,128)S(1)} collective-permute-done((f32[384,256]{1,0:T(8,128)S(1)}, f32[384,256]{1,0:T(8,128)S(1)}, u32[]{:S(2)}, u32[]{:S(2)}) %collective-permute-start.33) | collective-permute-done | bytes 393248 | tf_op jit(solution)/shard_map/ppermute | solution.py:31
  182.5 1.4 next_level.66
  184.0 12.3 %collective-permute-done.34.arrived_ref = f32[384,256]{1,0:T(8,128)S(1)} collective-permute-done((f32[384,256]{1,0:T(8,128)S(1)}, f32[384,256]{1,0:T(8,128)S(1)}, u32[]{:S(2)}, u32[]{:S(2)}) %collective-permute-start.34) | collective-permute-done | bytes 393248 | tf_op jit(solution)/shard_map/ppermute | solution.py:31
  198.7 23.1 %collective-permute-done.36.arrived_ref = f32[384,256]{1,0:T(8,128)S(1)} collective-permute-done((f32[384,256]{1,0:T(8,128)S(1)}, f32[384,256]{1,0:T(8,128)S(1)}, u32[]{:S(2)}, u32[]{:S(2)}) %collective-permute-start.36) | collective-permute-done | bytes 393248 | tf_op jit(solution)/shard_map/ppermute | solution.py:31
  221.8 1.4 next_level.68
  223.3 1.7 collective-permute-start.38
  225.0 2.5 collective-permute-done.37.arrived_ref
  227.5 1.4 next_level.69
  228.9 3.6 %collective-permute-start.39 = (f32[384,256]{1,0:T(8,128)S(1)}, f32[384,256]{1,0:T(8,128)S(1)}, u32[]{:S(2)}, u32[]{:S(2)}) collective-permute-start(f32[384,256]{1,0:T(8,128)S(1)} %get-tuple-element.292), channel_id=1, source_target_pairs={{0,128},{128,0},{1,129},{129,1},{2,130},{130,2},{3,131},{131,3},{4... | collective-permute-start | bytes 1179656 | tf_op jit(solution)/shard_map/ppermute | solution.py:31
  232.6 17.9 %collective-permute-done.38.arrived_ref = f32[384,256]{1,0:T(8,128)S(1)} collective-permute-done((f32[384,256]{1,0:T(8,128)S(1)}, f32[384,256]{1,0:T(8,128)S(1)}, u32[]{:S(2)}, u32[]{:S(2)}) %collective-permute-start.38) | collective-permute-done | bytes 393248 | tf_op jit(solution)/shard_map/ppermute | solution.py:31
  251.3 4.2 %collective-permute-done.39.arrived_ref = f32[384,256]{1,0:T(8,128)S(1)} collective-permute-done((f32[384,256]{1,0:T(8,128)S(1)}, f32[384,256]{1,0:T(8,128)S(1)}, u32[]{:S(2)}, u32[]{:S(2)}) %collective-permute-start.39) | collective-permute-done | bytes 393248 | tf_op jit(solution)/shard_map/ppermute | solution.py:31
  (70 shorter events, 38.3 us)
Async XLA Ops:
  3.9 1.8 collective-permute-start
  7.0 7.4 %collective-permute-start.1 = (f32[384,128]{1,0:T(8,128)S(1)}, f32[384,128]{1,0:T(8,128)S(1)}, u32[]{:S(2)}, u32[]{:S(2)}) collective-permute-start(f32[384,128]{1,0:T(8,128)S(1)} %get-tuple-element.162), channel_id=1, source_target_pairs={{0,2},{2,0},{1,3},{3,1},{4,6},{6,4},{5,7},{7,5},{8,10},{10,8},{9,1... | collective-permute-start | bytes 589832 | tf_op jit(solution)/shard_map/ppermute | solution.py:31
  11.4 8.3 %collective-permute-start.2 = (f32[384,128]{1,0:T(8,128)S(1)}, f32[384,128]{1,0:T(8,128)S(1)}, u32[]{:S(2)}, u32[]{:S(2)}) collective-permute-start(f32[384,128]{1,0:T(8,128)S(1)} %get-tuple-element.166), channel_id=1, source_target_pairs={{0,1},{1,0},{2,3},{3,2},{4,5},{5,4},{6,7},{7,6},{8,9},{9,8},{10,11... | collective-permute-start | bytes 589832 | tf_op jit(solution)/shard_map/ppermute | solution.py:31
  15.6 9.3 %collective-permute-start.3 = (f32[384,128]{1,0:T(8,128)S(1)}, f32[384,128]{1,0:T(8,128)S(1)}, u32[]{:S(2)}, u32[]{:S(2)}) collective-permute-start(f32[384,128]{1,0:T(8,128)S(1)} %get-tuple-element.171), channel_id=1, source_target_pairs={{0,4},{4,0},{1,5},{5,1},{2,6},{6,2},{3,7},{7,3},{8,12},{12,8},{9,1... | collective-permute-start | bytes 589832 | tf_op jit(solution)/shard_map/ppermute | solution.py:31
  20.9 7.5 %collective-permute-start.4 = (f32[384,128]{1,0:T(8,128)S(1)}, f32[384,128]{1,0:T(8,128)S(1)}, u32[]{:S(2)}, u32[]{:S(2)}) collective-permute-start(f32[384,128]{1,0:T(8,128)S(1)} %get-tuple-element.175), channel_id=1, source_target_pairs={{0,2},{2,0},{1,3},{3,1},{4,6},{6,4},{5,7},{7,5},{8,10},{10,8},{9,1... | collective-permute-start | bytes 589832 | tf_op jit(solution)/shard_map/ppermute | solution.py:31
  24.8 6.5 %collective-permute-start.5 = (f32[384,256]{1,0:T(8,128)S(1)}, f32[384,256]{1,0:T(8,128)S(1)}, u32[]{:S(2)}, u32[]{:S(2)}) collective-permute-start(f32[384,256]{1,0:T(8,128)S(1)} %get-tuple-element.178), channel_id=1, source_target_pairs={{0,1},{1,0},{2,3},{3,2},{4,5},{5,4},{6,7},{7,6},{8,9},{9,8},{10,11... | collective-permute-start | bytes 1179656 | tf_op jit(solution)/shard_map/ppermute | solution.py:31
  26.1 7.4 %collective-permute-start.6 = (f32[384,128]{1,0:T(8,128)S(1)}, f32[384,128]{1,0:T(8,128)S(1)}, u32[]{:S(2)}, u32[]{:S(2)}) collective-permute-start(f32[384,128]{1,0:T(8,128)S(1)} %get-tuple-element.182), channel_id=1, source_target_pairs={{0,8},{8,0},{1,9},{9,1},{2,10},{10,2},{3,11},{11,3},{4,12},{12,4},... | collective-permute-start | bytes 589832 | tf_op jit(solution)/shard_map/ppermute | solution.py:31
  29.7 12.5 %collective-permute-start.7 = (f32[384,128]{1,0:T(8,128)S(1)}, f32[384,128]{1,0:T(8,128)S(1)}, u32[]{:S(2)}, u32[]{:S(2)}) collective-permute-start(f32[384,128]{1,0:T(8,128)S(1)} %get-tuple-element.187), channel_id=1, source_target_pairs={{0,4},{4,0},{1,5},{5,1},{2,6},{6,2},{3,7},{7,3},{8,12},{12,8},{9,1... | collective-permute-start | bytes 589832 | tf_op jit(solution)/shard_map/ppermute | solution.py:31
  34.7 10.7 %collective-permute-start.8 = (f32[384,128]{1,0:T(8,128)S(1)}, f32[384,128]{1,0:T(8,128)S(1)}, u32[]{:S(2)}, u32[]{:S(2)}) collective-permute-start(f32[384,128]{1,0:T(8,128)S(1)} %get-tuple-element.191), channel_id=1, source_target_pairs={{0,16},{16,0},{1,17},{17,1},{2,18},{18,2},{3,19},{19,3},{4,20},{20... | collective-permute-start | bytes 589832 | tf_op jit(solution)/shard_map/ppermute | solution.py:31
  36.9 13.4 %collective-permute-start.9 = (f32[384,256]{1,0:T(8,128)S(1)}, f32[384,256]{1,0:T(8,128)S(1)}, u32[]{:S(2)}, u32[]{:S(2)}) collective-permute-start(f32[384,256]{1,0:T(8,128)S(1)} %get-tuple-element.195), channel_id=1, source_target_pairs={{0,2},{2,0},{1,3},{3,1},{4,6},{6,4},{5,7},{7,5},{8,10},{10,8},{9,1... | collective-permute-start | bytes 1179656 | tf_op jit(solution)/shard_map/ppermute | solution.py:31
  43.5 8.3 %collective-permute-start.10 = (f32[384,128]{1,0:T(8,128)S(1)}, f32[384,128]{1,0:T(8,128)S(1)}, u32[]{:S(2)}, u32[]{:S(2)}) collective-permute-start(f32[384,128]{1,0:T(8,128)S(1)} %get-tuple-element.198), channel_id=1, source_target_pairs={{0,8},{8,0},{1,9},{9,1},{2,10},{10,2},{3,11},{11,3},{4,12},{12,4},... | collective-permute-start | bytes 589832 | tf_op jit(solution)/shard_map/ppermute | solution.py:31
  45.4 15.8 %collective-permute-start.12 = (f32[384,256]{1,0:T(8,128)S(1)}, f32[384,256]{1,0:T(8,128)S(1)}, u32[]{:S(2)}, u32[]{:S(2)}) collective-permute-start(f32[384,256]{1,0:T(8,128)S(1)} %get-tuple-element.206), channel_id=1, source_target_pairs={{0,1},{1,0},{2,3},{3,2},{4,5},{5,4},{6,7},{7,6},{8,9},{9,8},{10,11... | collective-permute-start | bytes 1179656 | tf_op jit(solution)/shard_map/ppermute | solution.py:31
  46.6 7.6 %collective-permute-start.11 = (f32[384,128]{1,0:T(8,128)S(1)}, f32[384,128]{1,0:T(8,128)S(1)}, u32[]{:S(2)}, u32[]{:S(2)}) collective-permute-start(f32[384,128]{1,0:T(8,128)S(1)} %get-tuple-element.202), channel_id=1, source_target_pairs={{0,32},{32,0},{1,33},{33,1},{2,34},{34,2},{3,35},{35,3},{4,36},{36... | collective-permute-start | bytes 589832 | tf_op jit(solution)/shard_map/ppermute | solution.py:31
  55.4 21.6 %collective-permute-start.15 = (f32[384,128]{1,0:T(8,128)S(1)}, f32[384,128]{1,0:T(8,128)S(1)}, u32[]{:S(2)}, u32[]{:S(2)}) collective-permute-start(f32[384,128]{1,0:T(8,128)S(1)} %get-tuple-element.216), channel_id=1, source_target_pairs={{0,64},{64,0},{1,65},{65,1},{2,66},{66,2},{3,67},{67,3},{4,68},{68... | collective-permute-start | bytes 589832 | tf_op jit(solution)/shard_map/ppermute | solution.py:31
  58.7 17.0 %collective-permute-start.14 = (f32[384,128]{1,0:T(8,128)S(1)}, f32[384,128]{1,0:T(8,128)S(1)}, u32[]{:S(2)}, u32[]{:S(2)}) collective-permute-start(f32[384,128]{1,0:T(8,128)S(1)} %get-tuple-element.212), channel_id=1, source_target_pairs={{0,16},{16,0},{1,17},{17,1},{2,18},{18,2},{3,19},{19,3},{4,20},{20... | collective-permute-start | bytes 589832 | tf_op jit(solution)/shard_map/ppermute | solution.py:31
  58.9 13.6 %collective-permute-start.13 = (f32[384,256]{1,0:T(8,128)S(1)}, f32[384,256]{1,0:T(8,128)S(1)}, u32[]{:S(2)}, u32[]{:S(2)}) collective-permute-start(f32[384,256]{1,0:T(8,128)S(1)} %get-tuple-element.209), channel_id=1, source_target_pairs={{0,4},{4,0},{1,5},{5,1},{2,6},{6,2},{3,7},{7,3},{8,12},{12,8},{9,1... | collective-permute-start | bytes 1179656 | tf_op jit(solution)/shard_map/ppermute | solution.py:31
  62.6 25.1 %collective-permute-start.17 = (f32[384,256]{1,0:T(8,128)S(1)}, f32[384,256]{1,0:T(8,128)S(1)}, u32[]{:S(2)}, u32[]{:S(2)}) collective-permute-start(f32[384,256]{1,0:T(8,128)S(1)} %get-tuple-element.222), channel_id=1, source_target_pairs={{0,2},{2,0},{1,3},{3,1},{4,6},{6,4},{5,7},{7,5},{8,10},{10,8},{9,1... | collective-permute-start | bytes 1179656 | tf_op jit(solution)/shard_map/ppermute | solution.py:31
  73.9 10.6 %collective-permute-start.16 = (f32[384,256]{1,0:T(8,128)S(1)}, f32[384,256]{1,0:T(8,128)S(1)}, u32[]{:S(2)}, u32[]{:S(2)}) collective-permute-start(f32[384,256]{1,0:T(8,128)S(1)} %get-tuple-element.219), channel_id=1, source_target_pairs={{0,8},{8,0},{1,9},{9,1},{2,10},{10,2},{3,11},{11,3},{4,12},{12,4},... | collective-permute-start | bytes 1179656 | tf_op jit(solution)/shard_map/ppermute | solution.py:31
  78.2 71.2 %collective-permute-start.30 = (f32[384,128]{1,0:T(8,128)S(1)}, f32[384,128]{1,0:T(8,128)S(1)}, u32[]{:S(2)}, u32[]{:S(2)}) collective-permute-start(f32[384,128]{1,0:T(8,128)S(1)} %get-tuple-element.262), channel_id=1, source_target_pairs={{0,128},{128,0},{1,129},{129,1},{2,130},{130,2},{3,131},{131,3},{4... | collective-permute-start | bytes 589832 | tf_op jit(solution)/shard_map/ppermute | solution.py:31
  83.5 10.3 %collective-permute-start.18 = (f32[384,128]{1,0:T(8,128)S(1)}, f32[384,128]{1,0:T(8,128)S(1)}, u32[]{:S(2)}, u32[]{:S(2)}) collective-permute-start(f32[384,128]{1,0:T(8,128)S(1)} %get-tuple-element.225), channel_id=1, source_target_pairs={{0,32},{32,0},{1,33},{33,1},{2,34},{34,2},{3,35},{35,3},{4,36},{36... | collective-permute-start | bytes 589832 | tf_op jit(solution)/shard_map/ppermute | solution.py:31
  85.9 12.0 %collective-permute-start.19 = (f32[384,256]{1,0:T(8,128)S(1)}, f32[384,256]{1,0:T(8,128)S(1)}, u32[]{:S(2)}, u32[]{:S(2)}) collective-permute-start(f32[384,256]{1,0:T(8,128)S(1)} %get-tuple-element.228), channel_id=1, source_target_pairs={{0,16},{16,0},{1,17},{17,1},{2,18},{18,2},{3,19},{19,3},{4,20},{20... | collective-permute-start | bytes 1179656 | tf_op jit(solution)/shard_map/ppermute | solution.py:31
  95.1 15.0 %collective-permute-start.21 = (f32[384,128]{1,0:T(8,128)S(1)}, f32[384,128]{1,0:T(8,128)S(1)}, u32[]{:S(2)}, u32[]{:S(2)}) collective-permute-start(f32[384,128]{1,0:T(8,128)S(1)} %get-tuple-element.235), channel_id=1, source_target_pairs={{0,64},{64,0},{1,65},{65,1},{2,66},{66,2},{3,67},{67,3},{4,68},{68... | collective-permute-start | bytes 589832 | tf_op jit(solution)/shard_map/ppermute | solution.py:31
  96.9 9.3 %collective-permute-start.20 = (f32[384,256]{1,0:T(8,128)S(1)}, f32[384,256]{1,0:T(8,128)S(1)}, u32[]{:S(2)}, u32[]{:S(2)}) collective-permute-start(f32[384,256]{1,0:T(8,128)S(1)} %get-tuple-element.231), channel_id=1, source_target_pairs={{0,4},{4,0},{1,5},{5,1},{2,6},{6,2},{3,7},{7,3},{8,12},{12,8},{9,1... | collective-permute-start | bytes 1179656 | tf_op jit(solution)/shard_map/ppermute | solution.py:31
  99.4 25.1 %collective-permute-start.24 = (f32[384,256]{1,0:T(8,128)S(1)}, f32[384,256]{1,0:T(8,128)S(1)}, u32[]{:S(2)}, u32[]{:S(2)}) collective-permute-start(f32[384,256]{1,0:T(8,128)S(1)} %get-tuple-element.244), channel_id=1, source_target_pairs={{0,32},{32,0},{1,33},{33,1},{2,34},{34,2},{3,35},{35,3},{4,36},{36... | collective-permute-start | bytes 1179656 | tf_op jit(solution)/shard_map/ppermute | solution.py:31
  110.0 2.4 collective-permute-start.22
  111.3 19.3 %collective-permute-start.25 = (f32[384,128]{1,0:T(8,128)S(1)}, f32[384,128]{1,0:T(8,128)S(1)}, u32[]{:S(2)}, u32[]{:S(2)}) collective-permute-start(f32[384,128]{1,0:T(8,128)S(1)} %get-tuple-element.247), channel_id=1, source_target_pairs={{0,128},{128,0},{1,129},{129,1},{2,130},{130,2},{3,131},{131,3},{4... | collective-permute-start | bytes 589832 | tf_op jit(solution)/shard_map/ppermute | solution.py:31
  111.8 11.3 %collective-permute-start.23 = (f32[384,256]{1,0:T(8,128)S(1)}, f32[384,256]{1,0:T(8,128)S(1)}, u32[]{:S(2)}, u32[]{:S(2)}) collective-permute-start(f32[384,256]{1,0:T(8,128)S(1)} %get-tuple-element.241), channel_id=1, source_target_pairs={{0,8},{8,0},{1,9},{9,1},{2,10},{10,2},{3,11},{11,3},{4,12},{12,4},... | collective-permute-start | bytes 1179656 | tf_op jit(solution)/shard_map/ppermute | solution.py:31
  113.8 17.6 %collective-permute-start.26 = (f32[384,256]{1,0:T(8,128)S(1)}, f32[384,256]{1,0:T(8,128)S(1)}, u32[]{:S(2)}, u32[]{:S(2)}) collective-permute-start(f32[384,256]{1,0:T(8,128)S(1)} %get-tuple-element.250), channel_id=1, source_target_pairs={{0,2},{2,0},{1,3},{3,1},{4,6},{6,4},{5,7},{7,5},{8,10},{10,8},{9,1... | collective-permute-start | bytes 1179656 | tf_op jit(solution)/shard_map/ppermute | solution.py:31
  125.9 22.1 %collective-permute-start.29 = (f32[384,256]{1,0:T(8,128)S(1)}, f32[384,256]{1,0:T(8,128)S(1)}, u32[]{:S(2)}, u32[]{:S(2)}) collective-permute-start(f32[384,256]{1,0:T(8,128)S(1)} %get-tuple-element.259), channel_id=1, source_target_pairs={{0,64},{64,0},{1,65},{65,1},{2,66},{66,2},{3,67},{67,3},{4,68},{68... | collective-permute-start | bytes 1179656 | tf_op jit(solution)/shard_map/ppermute | solution.py:31
  128.5 11.6 %collective-permute-start.27 = (f32[384,256]{1,0:T(8,128)S(1)}, f32[384,256]{1,0:T(8,128)S(1)}, u32[]{:S(2)}, u32[]{:S(2)}) collective-permute-start(f32[384,256]{1,0:T(8,128)S(1)} %get-tuple-element.253), channel_id=1, source_target_pairs={{0,16},{16,0},{1,17},{17,1},{2,18},{18,2},{3,19},{19,3},{4,20},{20... | collective-permute-start | bytes 1179656 | tf_op jit(solution)/shard_map/ppermute | solution.py:31
  132.8 11.6 %collective-permute-start.28 = (f32[384,256]{1,0:T(8,128)S(1)}, f32[384,256]{1,0:T(8,128)S(1)}, u32[]{:S(2)}, u32[]{:S(2)}) collective-permute-start(f32[384,256]{1,0:T(8,128)S(1)} %get-tuple-element.256), channel_id=1, source_target_pairs={{0,4},{4,0},{1,5},{5,1},{2,6},{6,2},{3,7},{7,3},{8,12},{12,8},{9,1... | collective-permute-start | bytes 1179656 | tf_op jit(solution)/shard_map/ppermute | solution.py:31
  145.9 9.3 %collective-permute-start.31 = (f32[384,256]{1,0:T(8,128)S(1)}, f32[384,256]{1,0:T(8,128)S(1)}, u32[]{:S(2)}, u32[]{:S(2)}) collective-permute-start(f32[384,256]{1,0:T(8,128)S(1)} %get-tuple-element.266), channel_id=1, source_target_pairs={{0,8},{8,0},{1,9},{9,1},{2,10},{10,2},{3,11},{11,3},{4,12},{12,4},... | collective-permute-start | bytes 1179656 | tf_op jit(solution)/shard_map/ppermute | solution.py:31
  156.6 9.9 %collective-permute-start.32 = (f32[384,256]{1,0:T(8,128)S(1)}, f32[384,256]{1,0:T(8,128)S(1)}, u32[]{:S(2)}, u32[]{:S(2)}) collective-permute-start(f32[384,256]{1,0:T(8,128)S(1)} %get-tuple-element.269), channel_id=1, source_target_pairs={{0,16},{16,0},{1,17},{17,1},{2,18},{18,2},{3,19},{19,3},{4,20},{20... | collective-permute-start | bytes 1179656 | tf_op jit(solution)/shard_map/ppermute | solution.py:31
  157.8 24.7 %collective-permute-start.33 = (f32[384,256]{1,0:T(8,128)S(1)}, f32[384,256]{1,0:T(8,128)S(1)}, u32[]{:S(2)}, u32[]{:S(2)}) collective-permute-start(f32[384,256]{1,0:T(8,128)S(1)} %get-tuple-element.272), channel_id=1, source_target_pairs={{0,32},{32,0},{1,33},{33,1},{2,34},{34,2},{3,35},{35,3},{4,36},{36... | collective-permute-start | bytes 1179656 | tf_op jit(solution)/shard_map/ppermute | solution.py:31
  157.8 40.1 %collective-permute-start.35 = (f32[384,256]{1,0:T(8,128)S(1)}, f32[384,256]{1,0:T(8,128)S(1)}, u32[]{:S(2)}, u32[]{:S(2)}) collective-permute-start(f32[384,256]{1,0:T(8,128)S(1)} %get-tuple-element.278), channel_id=1, source_target_pairs={{0,128},{128,0},{1,129},{129,1},{2,130},{130,2},{3,131},{131,3},{4... | collective-permute-start | bytes 1179656 | tf_op jit(solution)/shard_map/ppermute | solution.py:31
  167.9 28.4 %collective-permute-start.34 = (f32[384,256]{1,0:T(8,128)S(1)}, f32[384,256]{1,0:T(8,128)S(1)}, u32[]{:S(2)}, u32[]{:S(2)}) collective-permute-start(f32[384,256]{1,0:T(8,128)S(1)} %get-tuple-element.275), channel_id=1, source_target_pairs={{0,32},{32,0},{1,33},{33,1},{2,34},{34,2},{3,35},{35,3},{4,36},{36... | collective-permute-start | bytes 1179656 | tf_op jit(solution)/shard_map/ppermute | solution.py:31
  183.9 37.9 %collective-permute-start.36 = (f32[384,256]{1,0:T(8,128)S(1)}, f32[384,256]{1,0:T(8,128)S(1)}, u32[]{:S(2)}, u32[]{:S(2)}) collective-permute-start(f32[384,256]{1,0:T(8,128)S(1)} %get-tuple-element.282), channel_id=1, source_target_pairs={{0,64},{64,0},{1,65},{65,1},{2,66},{66,2},{3,67},{67,3},{4,68},{68... | collective-permute-start | bytes 1179656 | tf_op jit(solution)/shard_map/ppermute | solution.py:31
  197.7 29.8 %collective-permute-start.37 = (f32[384,256]{1,0:T(8,128)S(1)}, f32[384,256]{1,0:T(8,128)S(1)}, u32[]{:S(2)}, u32[]{:S(2)}) collective-permute-start(f32[384,256]{1,0:T(8,128)S(1)} %get-tuple-element.285), channel_id=1, source_target_pairs={{0,64},{64,0},{1,65},{65,1},{2,66},{66,2},{3,67},{67,3},{4,68},{68... | collective-permute-start | bytes 1179656 | tf_op jit(solution)/shard_map/ppermute | solution.py:31
  223.3 27.2 %collective-permute-start.38 = (f32[384,256]{1,0:T(8,128)S(1)}, f32[384,256]{1,0:T(8,128)S(1)}, u32[]{:S(2)}, u32[]{:S(2)}) collective-permute-start(f32[384,256]{1,0:T(8,128)S(1)} %get-tuple-element.288), channel_id=1, source_target_pairs={{0,128},{128,0},{1,129},{129,1},{2,130},{130,2},{3,131},{131,3},{4... | collective-permute-start | bytes 1179656 | tf_op jit(solution)/shard_map/ppermute | solution.py:31
  228.9 26.5 %collective-permute-start.39 = (f32[384,256]{1,0:T(8,128)S(1)}, f32[384,256]{1,0:T(8,128)S(1)}, u32[]{:S(2)}, u32[]{:S(2)}) collective-permute-start(f32[384,256]{1,0:T(8,128)S(1)} %get-tuple-element.292), channel_id=1, source_target_pairs={{0,128},{128,0},{1,129},{129,1},{2,130},{130,2},{3,131},{131,3},{4... | collective-permute-start | bytes 1179656 | tf_op jit(solution)/shard_map/ppermute | solution.py:31
where the time goes:
time: 260 us; the launch traced here: 257 us
  waiting for transfers between devices  124 us (48%)
  Pallas kernels  76.6 us (29%)
  starting transfers between devices  55.2 us (21%)
    ppermute x40, waiting for transfers between devices, partner(): return lax.ppermute(block, axis, route)  124 us
    pallas_call x40, Pallas kernels, stage(): pl.pallas_call(kernel, out_shape=(block, block, TOKEN), in_specs=specs, o...  58.3 us
    ppermute x40, starting transfers between devices, partner(): return lax.ppermute(block, axis, route)  55.2 us
    pallas_call x8, Pallas kernels, split_matrices(): pl.pallas_call(split_kernel, grid=(1,), out_shape=(pltpu.VMEM((2 * rank,...  13.8 us
  transfers between devices with their start and end apart: 40, of which 17 were waited for; matrix products, arithmetic and copies ran while one was open for 0% of the time, Pallas kernels for 27%

commit v1 on v0

--- a/solution.py
+++ b/solution.py
@@ -7,18 +7,18 @@
 from jax.sharding import PartitionSpec as P
 
 LEVELS = 8
-WIDTHS = (128, 256, 128, 256, 256)
+WIDTHS = (128, 128, 256, 256, 256)
 ORDER = (
-    (0, 0), (0, 1), (2, 0), (0, 2), (2, 1), (4, 0), (0, 3), (2, 2), (4, 1), (0, 4), (3, 0), (2, 3),
-    (0, 5), (4, 2), (2, 4), (0, 6), (3, 1), (4, 3), (2, 5), (0, 7), (4, 4), (3, 2), (2, 6), (4, 5),
-    (3, 3), (1, 0), (2, 7), (1, 1), (3, 4), (4, 6), (2, 8), (1, 2), (3, 5), (1, 3), (4, 7), (0, 8),
-    (1, 4), (1, 5), (3, 6), (1, 6), (4, 8), (3, 7), (1, 7), (3, 8), (1, 8),
+    (3, 0), (3, 1), (0, 0), (3, 2), (1, 0), (2, 0), (0, 1), (3, 3), (0, 2), (1, 1), (3, 4), (4, 0),
+    (1, 2), (0, 3), (3, 5), (0, 4), (1, 3), (4, 1), (3, 6), (0, 5), (1, 4), (4, 2), (1, 5), (0, 6),
+    (4, 3), (3, 7), (2, 1), (4, 4), (2, 2), (4, 5), (1, 6), (2, 3), (1, 7), (2, 4), (0, 7), (1, 8),
+    (2, 5), (4, 6), (2, 6), (3, 8), (4, 7), (2, 7), (0, 8), (4, 8), (2, 8),
 )
 ANY = pl.BlockSpec(memory_space=pl.ANY)
 VMEM = pl.BlockSpec(memory_space=pltpu.VMEM)
 PARAMS = pltpu.CompilerParams(vmem_limit_bytes=12 << 20)
 TOKEN = pltpu.VMEM((8, 128), jnp.float32)
-CHEAP = pl.CostEstimate(flops=1 << 33, bytes_accessed=1 << 10, transcendentals=0)
+COST = pl.CostEstimate(flops=1 << 33, bytes_accessed=1 << 10, transcendentals=0)
 
 
 def partner(block, axis, stride):
@@ -67,15 +67,15 @@
         out_shape=(pltpu.VMEM((2 * rank, 3 * rank), jnp.bfloat16), TOKEN),
         in_specs=[VMEM, pl.BlockSpec((1, 1, 2, rank, rank), lambda i: (0, level, 0, 0, 0))],
         out_specs=(VMEM, VMEM),
-        cost_estimate=CHEAP,
+        cost_estimate=COST,
         compiler_params=PARAMS,
         name="split_matrices",
     )(on_chip(token), in_hbm(transfers))
 
 
-def multiply(t_ref, part_refs, send_ref, keep_ref, stacked):
+def multiply(blocks, t_ref, part_refs, send_ref, keep_ref, stacked):
     rank = send_ref.shape[0]
-    step = 64
+    step = 48
 
     @pl.loop(0, rank // step)
     def _(i):
@@ -88,32 +88,32 @@
         stacked[pl.ds(pl.multiple_of(here + rank, step), step)] = low
         stacked[pl.ds(pl.multiple_of(here + 2 * rank, step), step)] = high
 
-    rows = rank // 2
-
-    @pl.loop(0, 4)
+    rows = rank // blocks
+
+    @pl.loop(0, 2 * blocks)
     def _(i):
         source = pl.ds(pl.multiple_of(i * rows, rows), rows)
         product = jnp.dot(t_ref[source], stacked[...], preferred_element_type=jnp.float32)
 
-        @pl.when(i < 2)
+        @pl.when(i < blocks)
         def _():
             keep_ref[source] = product
 
-        @pl.when(i >= 2)
+        @pl.when(i >= blocks)
         def _():
-            send_ref[pl.ds(pl.multiple_of((i - 2) * rows, rows), rows)] = product
+            send_ref[pl.ds(pl.multiple_of((i - blocks) * rows, rows), rows)] = product
 
 
 def first_kernel(start, token_ref, t_ref, c_ref, send_ref, keep_ref, next_ref, stacked, block, sem):
     copy = pltpu.make_async_copy(c_ref.at[0, :, pl.ds(start, block.shape[1])], block, sem)
     copy.start()
     copy.wait()
-    multiply(t_ref, (block,), send_ref, keep_ref, stacked)
+    multiply(2, t_ref, (block,), send_ref, keep_ref, stacked)
     next_ref[...] = jnp.zeros_like(next_ref)
 
 
 def level_kernel(token_ref, t_ref, kept_ref, arrived_ref, send_ref, keep_ref, next_ref, stacked):
-    multiply(t_ref, (kept_ref, arrived_ref), send_ref, keep_ref, stacked)
+    multiply(1, t_ref, (kept_ref, arrived_ref), send_ref, keep_ref, stacked)
     next_ref[...] = jnp.zeros_like(next_ref)
 
 
@@ -126,7 +126,7 @@
         in_specs=specs,
         out_specs=(VMEM, VMEM, VMEM),
         scratch_shapes=[pltpu.VMEM((3 * rank, width), jnp.bfloat16), *scratch],
-        cost_estimate=CHEAP,
+        cost_estimate=COST,
         compiler_params=PARAMS,
         name=name,
     )(*operands)
@@ -146,7 +146,7 @@
 
 def write_kernel(start, token_ref, kept_ref, arrived_ref, *refs):
     out_ref, next_ref, block, sem = refs[-4:]
-    step = 64
+    step = 48
 
     @pl.loop(0, block.shape[0] // step)
     def _(i):
@@ -168,7 +168,7 @@
         out_specs=(ANY, VMEM),
         scratch_shapes=[pltpu.VMEM(kept.shape, jnp.float32), pltpu.SemaphoreType.DMA],
         input_output_aliases={} if result is None else {3: 0},
-        cost_estimate=CHEAP,
+        cost_estimate=COST,
         compiler_params=PARAMS,
         name="write_result",
     )(*parts)

time: 260 us -> 243 us (0.935)
  the two profiles are of different devices: /device:TPU:10 before, /device:TPU:18 now
where the time goes in v1:
time: 243 us; the launch traced here: 242 us
  waiting for transfers between devices  108 us (44%)
  starting transfers between devices  67.7 us (28%)
  Pallas kernels  66.4 us (27%)
    ppermute x40, waiting for transfers between devices, partner(): return lax.ppermute(block, axis, route)  108 us
    ppermute x40, starting transfers between devices, partner(): return lax.ppermute(block, axis, route)  67.7 us
    pallas_call x40, Pallas kernels, stage(): pl.pallas_call(kernel, out_shape=(block, block, TOKEN), in_specs=specs, o...  48.1 us
    pallas_call x8, Pallas kernels, split_matrices(): pl.pallas_call(split_kernel, grid=(1,), out_shape=(pltpu.VMEM((2 * rank,...  13.8 us
  transfers between devices with their start and end apart: 40, of which 15 were waited for; matrix products, arithmetic and copies ran while one was open for 0% of the time, Pallas kernels for 25%

profile of v1, /device:TPU:18, one launch (start us, length us, event | category | flops | bytes accessed | tf_op | source)
XLA Modules:
  0.0 242.5 jit_solution(16938132200026151675)
XLA Ops:
  0.0 1.7 split_matrices.8
  1.7 2.4 first_level.5
  4.2 1.7 split_matrices.9
  7.0 1.4 collective-permute-start.1
  8.4 1.7 split_matrices.10
  10.2 2.1 first_level.6
  12.6 6.0 %collective-permute-done.1.arrived_ref = f32[384,256]{1,0:T(8,128)S(1)} collective-permute-done((f32[384,256]{1,0:T(8,128)S(1)}, f32[384,256]{1,0:T(8,128)S(1)}, u32[]{:S(2)}, u32[]{:S(2)}) %collective-permute-start.1) | collective-permute-done | bytes 393248 | tf_op jit(solution)/shard_map/ppermute | solution.py:31
  20.1 1.7 split_matrices.11
  21.9 2.1 first_level.7
  24.1 3.2 %first_level.8 = (f32[384,256]{1,0:T(8,128)}, f32[384,256]{1,0:T(8,128)S(1)}, f32[8,128]{1,0:T(8,128)S(1)}) custom-call(f32[8,128]{1,0:T(8,128)S(1)} %get-tuple-element.165.token_ref, bf16[768,1152]{1,0:T(8,128)(2,1)S(1)} %get-tuple-element.151.t_ref, f32[1,384,1024]{2,1,0:T(8,128)} %c_ref.9), custom_call_target="tpu_custom_call" | custom-call | flops 8589934592 | bytes 1024 | tf_op jit(solution)/shard_map/first_level/pallas_call | solution.py:123
  28.2 2.3 collective-permute-start.4
  30.7 1.3 collective-permute-done.3.arrived_ref
  32.0 1.0 next_level.38
  33.7 1.7 split_matrices.12
  37.9 1.8 collective-permute-start.7
  39.8 1.7 collective-permute-start.8
  41.4 1.7 collective-permute-done.6.arrived_ref
  43.2 1.0 next_level.41
  44.2 2.2 collective-permute-start.9
  46.4 1.7 split_matrices.13
  48.2 2.4 first_level.9
  52.5 1.5 collective-permute-start.10
  54.0 1.7 collective-permute-start.11
  57.3 2.0 collective-permute-start.13
  59.3 1.7 split_matrices.14
  63.2 3.4 %collective-permute-start.14 = (f32[384,128]{1,0:T(8,128)S(1)}, f32[384,128]{1,0:T(8,128)S(1)}, u32[]{:S(2)}, u32[]{:S(2)}) collective-permute-start(f32[384,128]{1,0:T(8,128)S(1)} %get-tuple-element.213), channel_id=1, source_target_pairs={{0,16},{16,0},{1,17},{17,1},{2,18},{18,2},{3,19},{19,3},{4,20},{20... | collective-permute-start | bytes 589832 | tf_op jit(solution)/shard_map/ppermute | solution.py:31
  66.6 1.0 next_level.47
  67.6 1.1 collective-permute-start.16
  69.8 3.4 %collective-permute-start.20 = (f32[384,256]{1,0:T(8,128)S(1)}, f32[384,256]{1,0:T(8,128)S(1)}, u32[]{:S(2)}, u32[]{:S(2)}) collective-permute-start(f32[384,256]{1,0:T(8,128)S(1)} %get-tuple-element.232), channel_id=1, source_target_pairs={{0,64},{64,0},{1,65},{65,1},{2,66},{66,2},{3,67},{67,3},{4,68},{68... | collective-permute-start | bytes 1179656 | tf_op jit(solution)/shard_map/ppermute | solution.py:31
  73.2 1.7 split_matrices.15
  79.7 2.4 collective-permute-start.19
  82.1 2.0 collective-permute-done.17.arrived_ref
  85.0 1.6 collective-permute-start.25
  86.6 6.4 %collective-permute-done.18.arrived_ref = f32[384,128]{1,0:T(8,128)S(1)} collective-permute-done((f32[384,128]{1,0:T(8,128)S(1)}, f32[384,128]{1,0:T(8,128)S(1)}, u32[]{:S(2)}, u32[]{:S(2)}) %collective-permute-start.18) | collective-permute-done | bytes 196640 | tf_op jit(solution)/shard_map/ppermute | solution.py:31
  93.9 3.5 %collective-permute-start.29 = (f32[384,128]{1,0:T(8,128)S(1)}, f32[384,128]{1,0:T(8,128)S(1)}, u32[]{:S(2)}, u32[]{:S(2)}) collective-permute-start(f32[384,128]{1,0:T(8,128)S(1)} %get-tuple-element.259), channel_id=1, source_target_pairs={{0,64},{64,0},{1,65},{65,1},{2,66},{66,2},{3,67},{67,3},{4,68},{68... | collective-permute-start | bytes 589832 | tf_op jit(solution)/shard_map/ppermute | solution.py:31
  97.5 1.0 next_level.54
  98.6 1.0 next_level.55
  99.7 2.0 next_level.56
  101.7 1.6 collective-permute-start.23
  103.3 4.9 %collective-permute-start.34 = (f32[384,256]{1,0:T(8,128)S(1)}, f32[384,256]{1,0:T(8,128)S(1)}, u32[]{:S(2)}, u32[]{:S(2)}) collective-permute-start(f32[384,256]{1,0:T(8,128)S(1)} %get-tuple-element.274), channel_id=1, source_target_pairs={{0,128},{128,0},{1,129},{129,1},{2,130},{130,2},{3,131},{131,3},{4... | collective-permute-start | bytes 1179656 | tf_op jit(solution)/shard_map/ppermute | solution.py:31
  109.2 2.3 collective-permute-start.24
  112.7 5.9 %collective-permute-done.24.arrived_ref = f32[384,256]{1,0:T(8,128)S(1)} collective-permute-done((f32[384,256]{1,0:T(8,128)S(1)}, f32[384,256]{1,0:T(8,128)S(1)}, u32[]{:S(2)}, u32[]{:S(2)}) %collective-permute-start.24) | collective-permute-done | bytes 393248 | tf_op jit(solution)/shard_map/ppermute | solution.py:31
  118.6 1.0 next_level.59
  120.6 3.0 %collective-permute-start.27 = (f32[384,128]{1,0:T(8,128)S(1)}, f32[384,128]{1,0:T(8,128)S(1)}, u32[]{:S(2)}, u32[]{:S(2)}) collective-permute-start(f32[384,128]{1,0:T(8,128)S(1)} %get-tuple-element.253), channel_id=1, source_target_pairs={{0,64},{64,0},{1,65},{65,1},{2,66},{66,2},{3,67},{67,3},{4,68},{68... | collective-permute-start | bytes 589832 | tf_op jit(solution)/shard_map/ppermute | solution.py:31
  123.5 1.0 next_level.61
  125.1 2.6 %collective-permute-start.32 = (f32[384,256]{1,0:T(8,128)S(1)}, f32[384,256]{1,0:T(8,128)S(1)}, u32[]{:S(2)}, u32[]{:S(2)}) collective-permute-start(f32[384,256]{1,0:T(8,128)S(1)} %get-tuple-element.268), channel_id=1, source_target_pairs={{0,32},{32,0},{1,33},{33,1},{2,34},{34,2},{3,35},{35,3},{4,36},{36... | collective-permute-start | bytes 1179656 | tf_op jit(solution)/shard_map/ppermute | solution.py:31
  127.7 4.8 %collective-permute-done.27.arrived_ref = f32[384,128]{1,0:T(8,128)S(1)} collective-permute-done((f32[384,128]{1,0:T(8,128)S(1)}, f32[384,128]{1,0:T(8,128)S(1)}, u32[]{:S(2)}, u32[]{:S(2)}) %collective-permute-start.27) | collective-permute-done | bytes 196640 | tf_op jit(solution)/shard_map/ppermute | solution.py:31
  133.4 3.6 %collective-permute-start.30 = (f32[384,128]{1,0:T(8,128)S(1)}, f32[384,128]{1,0:T(8,128)S(1)}, u32[]{:S(2)}, u32[]{:S(2)}) collective-permute-start(f32[384,128]{1,0:T(8,128)S(1)} %get-tuple-element.262), channel_id=1, source_target_pairs={{0,128},{128,0},{1,129},{129,1},{2,130},{130,2},{3,131},{131,3},{4... | collective-permute-start | bytes 589832 | tf_op jit(solution)/shard_map/ppermute | solution.py:31
  137.1 1.0 next_level.63
  139.1 2.5 %collective-permute-start.37 = (f32[384,128]{1,0:T(8,128)S(1)}, f32[384,128]{1,0:T(8,128)S(1)}, u32[]{:S(2)}, u32[]{:S(2)}) collective-permute-start(f32[384,128]{1,0:T(8,128)S(1)} %get-tuple-element.284), channel_id=1, source_target_pairs={{0,128},{128,0},{1,129},{129,1},{2,130},{130,2},{3,131},{131,3},{4... | collective-permute-start | bytes 589832 | tf_op jit(solution)/shard_map/ppermute | solution.py:31
  141.5 3.3 %collective-permute-start.31 = (f32[384,256]{1,0:T(8,128)S(1)}, f32[384,256]{1,0:T(8,128)S(1)}, u32[]{:S(2)}, u32[]{:S(2)}) collective-permute-start(f32[384,256]{1,0:T(8,128)S(1)} %get-tuple-element.265), channel_id=1, source_target_pairs={{0,16},{16,0},{1,17},{17,1},{2,18},{18,2},{3,19},{19,3},{4,20},{20... | collective-permute-start | bytes 1179656 | tf_op jit(solution)/shard_map/ppermute | solution.py:31
  144.9 8.0 %collective-permute-done.30.arrived_ref = f32[384,128]{1,0:T(8,128)S(1)} collective-permute-done((f32[384,128]{1,0:T(8,128)S(1)}, f32[384,128]{1,0:T(8,128)S(1)}, u32[]{:S(2)}, u32[]{:S(2)}) %collective-permute-start.30) | collective-permute-done | bytes 196640 | tf_op jit(solution)/shard_map/ppermute | solution.py:31
  154.8 1.1 next_level.66
  155.8 2.4 %collective-permute-start.35 = (f32[384,256]{1,0:T(8,128)S(1)}, f32[384,256]{1,0:T(8,128)S(1)}, u32[]{:S(2)}, u32[]{:S(2)}) collective-permute-start(f32[384,256]{1,0:T(8,128)S(1)} %get-tuple-element.278), channel_id=1, source_target_pairs={{0,64},{64,0},{1,65},{65,1},{2,66},{66,2},{3,67},{67,3},{4,68},{68... | collective-permute-start | bytes 1179656 | tf_op jit(solution)/shard_map/ppermute | solution.py:31
  158.3 12.5 %collective-permute-done.33.arrived_ref = f32[384,256]{1,0:T(8,128)S(1)} collective-permute-done((f32[384,256]{1,0:T(8,128)S(1)}, f32[384,256]{1,0:T(8,128)S(1)}, u32[]{:S(2)}, u32[]{:S(2)}) %collective-permute-start.33) | collective-permute-done | bytes 393248 | tf_op jit(solution)/shard_map/ppermute | solution.py:31
  173.3 33.8 %collective-permute-done.35.arrived_ref = f32[384,256]{1,0:T(8,128)S(1)} collective-permute-done((f32[384,256]{1,0:T(8,128)S(1)}, f32[384,256]{1,0:T(8,128)S(1)}, u32[]{:S(2)}, u32[]{:S(2)}) %collective-permute-start.35) | collective-permute-done | bytes 393248 | tf_op jit(solution)/shard_map/ppermute | solution.py:31
  207.1 1.0 next_level.68
  208.2 3.3 %collective-permute-start.38 = (f32[384,256]{1,0:T(8,128)S(1)}, f32[384,256]{1,0:T(8,128)S(1)}, u32[]{:S(2)}, u32[]{:S(2)}) collective-permute-start(f32[384,256]{1,0:T(8,128)S(1)} %get-tuple-element.288), channel_id=1, source_target_pairs={{0,128},{128,0},{1,129},{129,1},{2,130},{130,2},{3,131},{131,3},{4... | collective-permute-start | bytes 1179656 | tf_op jit(solution)/shard_map/ppermute | solution.py:31
  211.5 2.8 %collective-permute-done.36.arrived_ref = f32[384,256]{1,0:T(8,128)S(1)} collective-permute-done((f32[384,256]{1,0:T(8,128)S(1)}, f32[384,256]{1,0:T(8,128)S(1)}, u32[]{:S(2)}, u32[]{:S(2)}) %collective-permute-start.36) | collective-permute-done | bytes 393248 | tf_op jit(solution)/shard_map/ppermute | solution.py:31
  214.3 1.0 next_level.69
  215.4 2.9 %collective-permute-start.39 = (f32[384,256]{1,0:T(8,128)S(1)}, f32[384,256]{1,0:T(8,128)S(1)}, u32[]{:S(2)}, u32[]{:S(2)}) collective-permute-start(f32[384,256]{1,0:T(8,128)S(1)} %get-tuple-element.292), channel_id=1, source_target_pairs={{0,128},{128,0},{1,129},{129,1},{2,130},{130,2},{3,131},{131,3},{4... | collective-permute-start | bytes 1179656 | tf_op jit(solution)/shard_map/ppermute | solution.py:31
  219.0 17.5 %collective-permute-done.38.arrived_ref = f32[384,256]{1,0:T(8,128)S(1)} collective-permute-done((f32[384,256]{1,0:T(8,128)S(1)}, f32[384,256]{1,0:T(8,128)S(1)}, u32[]{:S(2)}, u32[]{:S(2)}) %collective-permute-start.38) | collective-permute-done | bytes 393248 | tf_op jit(solution)/shard_map/ppermute | solution.py:31
  237.4 3.5 %collective-permute-done.39.arrived_ref = f32[384,256]{1,0:T(8,128)S(1)} collective-permute-done((f32[384,256]{1,0:T(8,128)S(1)}, f32[384,256]{1,0:T(8,128)S(1)}, u32[]{:S(2)}, u32[]{:S(2)}) %collective-permute-start.39) | collective-permute-done | bytes 393248 | tf_op jit(solution)/shard_map/ppermute | solution.py:31
  240.9 1.4 write_result.9
  (70 shorter events, 32.0 us)
Async XLA Ops:
  4.1 1.8 collective-permute-start
  7.0 11.6 %collective-permute-start.1 = (f32[384,256]{1,0:T(8,128)S(1)}, f32[384,256]{1,0:T(8,128)S(1)}, u32[]{:S(2)}, u32[]{:S(2)}) collective-permute-start(f32[384,256]{1,0:T(8,128)S(1)} %get-tuple-element.162), channel_id=1, source_target_pairs={{0,2},{2,0},{1,3},{3,1},{4,6},{6,4},{5,7},{7,5},{8,10},{10,8},{9,1... | collective-permute-start | bytes 1179656 | tf_op jit(solution)/shard_map/ppermute | solution.py:31
  12.3 15.0 %collective-permute-start.2 = (f32[384,128]{1,0:T(8,128)S(1)}, f32[384,128]{1,0:T(8,128)S(1)}, u32[]{:S(2)}, u32[]{:S(2)}) collective-permute-start(f32[384,128]{1,0:T(8,128)S(1)} %get-tuple-element.168), channel_id=1, source_target_pairs={{0,1},{1,0},{2,3},{3,2},{4,5},{5,4},{6,7},{7,6},{8,9},{9,8},{10,11... | collective-permute-start | bytes 589832 | tf_op jit(solution)/shard_map/ppermute | solution.py:31
  19.7 12.3 %collective-permute-start.3 = (f32[384,256]{1,0:T(8,128)S(1)}, f32[384,256]{1,0:T(8,128)S(1)}, u32[]{:S(2)}, u32[]{:S(2)}) collective-permute-start(f32[384,256]{1,0:T(8,128)S(1)} %get-tuple-element.172), channel_id=1, source_target_pairs={{0,4},{4,0},{1,5},{5,1},{2,6},{6,2},{3,7},{7,3},{8,12},{12,8},{9,1... | collective-permute-start | bytes 1179656 | tf_op jit(solution)/shard_map/ppermute | solution.py:31
  24.0 13.0 %collective-permute-start.5 = (f32[384,128]{1,0:T(8,128)S(1)}, f32[384,128]{1,0:T(8,128)S(1)}, u32[]{:S(2)}, u32[]{:S(2)}) collective-permute-start(f32[384,128]{1,0:T(8,128)S(1)} %get-tuple-element.179), channel_id=1, source_target_pairs={{0,1},{1,0},{2,3},{3,2},{4,5},{5,4},{6,7},{7,6},{8,9},{9,8},{10,11... | collective-permute-start | bytes 589832 | tf_op jit(solution)/shard_map/ppermute | solution.py:31
  28.2 7.8 %collective-permute-start.4 = (f32[384,128]{1,0:T(8,128)S(1)}, f32[384,128]{1,0:T(8,128)S(1)}, u32[]{:S(2)}, u32[]{:S(2)}) collective-permute-start(f32[384,128]{1,0:T(8,128)S(1)} %get-tuple-element.176), channel_id=1, source_target_pairs={{0,2},{2,0},{1,3},{3,1},{4,6},{6,4},{5,7},{7,5},{8,10},{10,8},{9,1... | collective-permute-start | bytes 589832 | tf_op jit(solution)/shard_map/ppermute | solution.py:31
  30.5 69.2 %collective-permute-start.21 = (f32[384,256]{1,0:T(8,128)}, f32[384,256]{1,0:T(8,128)}, u32[]{:S(2)}, u32[]{:S(2)}) collective-permute-start(f32[384,256]{1,0:T(8,128)} %get-tuple-element.235), channel_id=1, source_target_pairs={{0,1},{1,0},{2,3},{3,2},{4,5},{5,4},{6,7},{7,6},{8,9},{9,8},{10,11... | collective-permute-start | bytes 1179656 | tf_op jit(solution)/shard_map/ppermute | solution.py:31
  33.1 10.1 %collective-permute-start.6 = (f32[384,256]{1,0:T(8,128)S(1)}, f32[384,256]{1,0:T(8,128)S(1)}, u32[]{:S(2)}, u32[]{:S(2)}) collective-permute-start(f32[384,256]{1,0:T(8,128)S(1)} %get-tuple-element.183), channel_id=1, source_target_pairs={{0,8},{8,0},{1,9},{9,1},{2,10},{10,2},{3,11},{11,3},{4,12},{12,4},... | collective-permute-start | bytes 1179656 | tf_op jit(solution)/shard_map/ppermute | solution.py:31
  37.9 12.7 %collective-permute-start.7 = (f32[384,128]{1,0:T(8,128)S(1)}, f32[384,128]{1,0:T(8,128)S(1)}, u32[]{:S(2)}, u32[]{:S(2)}) collective-permute-start(f32[384,128]{1,0:T(8,128)S(1)} %get-tuple-element.188), channel_id=1, source_target_pairs={{0,2},{2,0},{1,3},{3,1},{4,6},{6,4},{5,7},{7,5},{8,10},{10,8},{9,1... | collective-permute-start | bytes 589832 | tf_op jit(solution)/shard_map/ppermute | solution.py:31
  39.8 11.8 %collective-permute-start.8 = (f32[384,128]{1,0:T(8,128)S(1)}, f32[384,128]{1,0:T(8,128)S(1)}, u32[]{:S(2)}, u32[]{:S(2)}) collective-permute-start(f32[384,128]{1,0:T(8,128)S(1)} %get-tuple-element.191), channel_id=1, source_target_pairs={{0,4},{4,0},{1,5},{5,1},{2,6},{6,2},{3,7},{7,3},{8,12},{12,8},{9,1... | collective-permute-start | bytes 589832 | tf_op jit(solution)/shard_map/ppermute | solution.py:31
  44.2 12.0 %collective-permute-start.9 = (f32[384,256]{1,0:T(8,128)S(1)}, f32[384,256]{1,0:T(8,128)S(1)}, u32[]{:S(2)}, u32[]{:S(2)}) collective-permute-start(f32[384,256]{1,0:T(8,128)S(1)} %get-tuple-element.195), channel_id=1, source_target_pairs={{0,16},{16,0},{1,17},{17,1},{2,18},{18,2},{3,19},{19,3},{4,20},{20... | collective-permute-start | bytes 1179656 | tf_op jit(solution)/shard_map/ppermute | solution.py:31
  52.5 8.6 %collective-permute-start.10 = (f32[384,128]{1,0:T(8,128)S(1)}, f32[384,128]{1,0:T(8,128)S(1)}, u32[]{:S(2)}, u32[]{:S(2)}) collective-permute-start(f32[384,128]{1,0:T(8,128)S(1)} %get-tuple-element.199), channel_id=1, source_target_pairs={{0,8},{8,0},{1,9},{9,1},{2,10},{10,2},{3,11},{11,3},{4,12},{12,4},... | collective-permute-start | bytes 589832 | tf_op jit(solution)/shard_map/ppermute | solution.py:31
  54.0 8.0 %collective-permute-start.11 = (f32[384,128]{1,0:T(8,128)S(1)}, f32[384,128]{1,0:T(8,128)S(1)}, u32[]{:S(2)}, u32[]{:S(2)}) collective-permute-start(f32[384,128]{1,0:T(8,128)S(1)} %get-tuple-element.202), channel_id=1, source_target_pairs={{0,4},{4,0},{1,5},{5,1},{2,6},{6,2},{3,7},{7,3},{8,12},{12,8},{9,1... | collective-permute-start | bytes 589832 | tf_op jit(solution)/shard_map/ppermute | solution.py:31
  55.7 10.9 %collective-permute-start.12 = (f32[384,256]{1,0:T(8,128)S(1)}, f32[384,256]{1,0:T(8,128)S(1)}, u32[]{:S(2)}, u32[]{:S(2)}) collective-permute-start(f32[384,256]{1,0:T(8,128)S(1)} %get-tuple-element.205), channel_id=1, source_target_pairs={{0,1},{1,0},{2,3},{3,2},{4,5},{5,4},{6,7},{7,6},{8,9},{9,8},{10,11... | collective-permute-start | bytes 1179656 | tf_op jit(solution)/shard_map/ppermute | solution.py:31
  57.3 11.4 %collective-permute-start.13 = (f32[384,256]{1,0:T(8,128)S(1)}, f32[384,256]{1,0:T(8,128)S(1)}, u32[]{:S(2)}, u32[]{:S(2)}) collective-permute-start(f32[384,256]{1,0:T(8,128)S(1)} %get-tuple-element.209), channel_id=1, source_target_pairs={{0,32},{32,0},{1,33},{33,1},{2,34},{34,2},{3,35},{35,3},{4,36},{36... | collective-permute-start | bytes 1179656 | tf_op jit(solution)/shard_map/ppermute | solution.py:31
  63.0 12.9 %collective-permute-start.15 = (f32[384,128]{1,0:T(8,128)S(1)}, f32[384,128]{1,0:T(8,128)S(1)}, u32[]{:S(2)}, u32[]{:S(2)}) collective-permute-start(f32[384,128]{1,0:T(8,128)S(1)} %get-tuple-element.216), channel_id=1, source_target_pairs={{0,8},{8,0},{1,9},{9,1},{2,10},{10,2},{3,11},{11,3},{4,12},{12,4},... | collective-permute-start | bytes 589832 | tf_op jit(solution)/shard_map/ppermute | solution.py:31
  63.2 11.7 %collective-permute-start.14 = (f32[384,128]{1,0:T(8,128)S(1)}, f32[384,128]{1,0:T(8,128)S(1)}, u32[]{:S(2)}, u32[]{:S(2)}) collective-permute-start(f32[384,128]{1,0:T(8,128)S(1)} %get-tuple-element.213), channel_id=1, source_target_pairs={{0,16},{16,0},{1,17},{17,1},{2,18},{18,2},{3,19},{19,3},{4,20},{20... | collective-permute-start | bytes 589832 | tf_op jit(solution)/shard_map/ppermute | solution.py:31
  67.6 11.0 %collective-permute-start.16 = (f32[384,256]{1,0:T(8,128)S(1)}, f32[384,256]{1,0:T(8,128)S(1)}, u32[]{:S(2)}, u32[]{:S(2)}) collective-permute-start(f32[384,256]{1,0:T(8,128)S(1)} %get-tuple-element.219), channel_id=1, source_target_pairs={{0,2},{2,0},{1,3},{3,1},{4,6},{6,4},{5,7},{7,5},{8,10},{10,8},{9,1... | collective-permute-start | bytes 1179656 | tf_op jit(solution)/shard_map/ppermute | solution.py:31
  69.8 28.9 %collective-permute-start.20 = (f32[384,256]{1,0:T(8,128)S(1)}, f32[384,256]{1,0:T(8,128)S(1)}, u32[]{:S(2)}, u32[]{:S(2)}) collective-permute-start(f32[384,256]{1,0:T(8,128)S(1)} %get-tuple-element.232), channel_id=1, source_target_pairs={{0,64},{64,0},{1,65},{65,1},{2,66},{66,2},{3,67},{67,3},{4,68},{68... | collective-permute-start | bytes 1179656 | tf_op jit(solution)/shard_map/ppermute | solution.py:31
  76.8 7.3 %collective-permute-start.17 = (f32[384,128]{1,0:T(8,128)S(1)}, f32[384,128]{1,0:T(8,128)S(1)}, u32[]{:S(2)}, u32[]{:S(2)}) collective-permute-start(f32[384,128]{1,0:T(8,128)S(1)} %get-tuple-element.222), channel_id=1, source_target_pairs={{0,16},{16,0},{1,17},{17,1},{2,18},{18,2},{3,19},{19,3},{4,20},{20... | collective-permute-start | bytes 589832 | tf_op jit(solution)/shard_map/ppermute | solution.py:31
  77.8 15.2 %collective-permute-start.18 = (f32[384,128]{1,0:T(8,128)S(1)}, f32[384,128]{1,0:T(8,128)S(1)}, u32[]{:S(2)}, u32[]{:S(2)}) collective-permute-start(f32[384,128]{1,0:T(8,128)S(1)} %get-tuple-element.225), channel_id=1, source_target_pairs={{0,32},{32,0},{1,33},{33,1},{2,34},{34,2},{3,35},{35,3},{4,36},{36... | collective-permute-start | bytes 589832 | tf_op jit(solution)/shard_map/ppermute | solution.py:31
  79.7 17.8 %collective-permute-start.19 = (f32[384,256]{1,0:T(8,128)S(1)}, f32[384,256]{1,0:T(8,128)S(1)}, u32[]{:S(2)}, u32[]{:S(2)}) collective-permute-start(f32[384,256]{1,0:T(8,128)S(1)} %get-tuple-element.228), channel_id=1, source_target_pairs={{0,4},{4,0},{1,5},{5,1},{2,6},{6,2},{3,7},{7,3},{8,12},{12,8},{9,1... | collective-permute-start | bytes 1179656 | tf_op jit(solution)/shard_map/ppermute | solution.py:31
  85.0 34.6 %collective-permute-start.25 = (f32[384,128]{1,0:T(8,128)S(1)}, f32[384,128]{1,0:T(8,128)S(1)}, u32[]{:S(2)}, u32[]{:S(2)}) collective-permute-start(f32[384,128]{1,0:T(8,128)S(1)} %get-tuple-element.247), channel_id=1, source_target_pairs={{0,32},{32,0},{1,33},{33,1},{2,34},{34,2},{3,35},{35,3},{4,36},{36... | collective-permute-start | bytes 589832 | tf_op jit(solution)/shard_map/ppermute | solution.py:31
  93.9 44.2 %collective-permute-start.29 = (f32[384,128]{1,0:T(8,128)S(1)}, f32[384,128]{1,0:T(8,128)S(1)}, u32[]{:S(2)}, u32[]{:S(2)}) collective-permute-start(f32[384,128]{1,0:T(8,128)S(1)} %get-tuple-element.259), channel_id=1, source_target_pairs={{0,64},{64,0},{1,65},{65,1},{2,66},{66,2},{3,67},{67,3},{4,68},{68... | collective-permute-start | bytes 589832 | tf_op jit(solution)/shard_map/ppermute | solution.py:31
  98.5 9.7 %collective-permute-start.22 = (f32[384,256]{1,0:T(8,128)S(1)}, f32[384,256]{1,0:T(8,128)S(1)}, u32[]{:S(2)}, u32[]{:S(2)}) collective-permute-start(f32[384,256]{1,0:T(8,128)S(1)} %get-tuple-element.238), channel_id=1, source_target_pairs={{0,8},{8,0},{1,9},{9,1},{2,10},{10,2},{3,11},{11,3},{4,12},{12,4},... | collective-permute-start | bytes 1179656 | tf_op jit(solution)/shard_map/ppermute | solution.py:31
  101.7 9.8 %collective-permute-start.23 = (f32[384,256]{1,0:T(8,128)S(1)}, f32[384,256]{1,0:T(8,128)S(1)}, u32[]{:S(2)}, u32[]{:S(2)}) collective-permute-start(f32[384,256]{1,0:T(8,128)S(1)} %get-tuple-element.241), channel_id=1, source_target_pairs={{0,2},{2,0},{1,3},{3,1},{4,6},{6,4},{5,7},{7,5},{8,10},{10,8},{9,1... | collective-permute-start | bytes 1179656 | tf_op jit(solution)/shard_map/ppermute | solution.py:31
  103.3 69.2 %collective-permute-start.34 = (f32[384,256]{1,0:T(8,128)S(1)}, f32[384,256]{1,0:T(8,128)S(1)}, u32[]{:S(2)}, u32[]{:S(2)}) collective-permute-start(f32[384,256]{1,0:T(8,128)S(1)} %get-tuple-element.274), channel_id=1, source_target_pairs={{0,128},{128,0},{1,129},{129,1},{2,130},{130,2},{3,131},{131,3},{4... | collective-permute-start | bytes 1179656 | tf_op jit(solution)/shard_map/ppermute | solution.py:31
  109.2 9.4 %collective-permute-start.24 = (f32[384,256]{1,0:T(8,128)S(1)}, f32[384,256]{1,0:T(8,128)S(1)}, u32[]{:S(2)}, u32[]{:S(2)}) collective-permute-start(f32[384,256]{1,0:T(8,128)S(1)} %get-tuple-element.244), channel_id=1, source_target_pairs={{0,16},{16,0},{1,17},{17,1},{2,18},{18,2},{3,19},{19,3},{4,20},{20... | collective-permute-start | bytes 1179656 | tf_op jit(solution)/shard_map/ppermute | solution.py:31
  112.6 10.9 %collective-permute-start.26 = (f32[384,256]{1,0:T(8,128)S(1)}, f32[384,256]{1,0:T(8,128)S(1)}, u32[]{:S(2)}, u32[]{:S(2)}) collective-permute-start(f32[384,256]{1,0:T(8,128)S(1)} %get-tuple-element.250), channel_id=1, source_target_pairs={{0,4},{4,0},{1,5},{5,1},{2,6},{6,2},{3,7},{7,3},{8,12},{12,8},{9,1... | collective-permute-start | bytes 1179656 | tf_op jit(solution)/shard_map/ppermute | solution.py:31
  120.6 11.9 %collective-permute-start.27 = (f32[384,128]{1,0:T(8,128)S(1)}, f32[384,128]{1,0:T(8,128)S(1)}, u32[]{:S(2)}, u32[]{:S(2)}) collective-permute-start(f32[384,128]{1,0:T(8,128)S(1)} %get-tuple-element.253), channel_id=1, source_target_pairs={{0,64},{64,0},{1,65},{65,1},{2,66},{66,2},{3,67},{67,3},{4,68},{68... | collective-permute-start | bytes 589832 | tf_op jit(solution)/shard_map/ppermute | solution.py:31
  124.6 12.5 %collective-permute-start.28 = (f32[384,256]{1,0:T(8,128)S(1)}, f32[384,256]{1,0:T(8,128)S(1)}, u32[]{:S(2)}, u32[]{:S(2)}) collective-permute-start(f32[384,256]{1,0:T(8,128)S(1)} %get-tuple-element.256), channel_id=1, source_target_pairs={{0,8},{8,0},{1,9},{9,1},{2,10},{10,2},{3,11},{11,3},{4,12},{12,4},... | collective-permute-start | bytes 1179656 | tf_op jit(solution)/shard_map/ppermute | solution.py:31
  125.1 29.6 %collective-permute-start.32 = (f32[384,256]{1,0:T(8,128)S(1)}, f32[384,256]{1,0:T(8,128)S(1)}, u32[]{:S(2)}, u32[]{:S(2)}) collective-permute-start(f32[384,256]{1,0:T(8,128)S(1)} %get-tuple-element.268), channel_id=1, source_target_pairs={{0,32},{32,0},{1,33},{33,1},{2,34},{34,2},{3,35},{35,3},{4,36},{36... | collective-permute-start | bytes 1179656 | tf_op jit(solution)/shard_map/ppermute | solution.py:31
  133.4 19.4 %collective-permute-start.30 = (f32[384,128]{1,0:T(8,128)S(1)}, f32[384,128]{1,0:T(8,128)S(1)}, u32[]{:S(2)}, u32[]{:S(2)}) collective-permute-start(f32[384,128]{1,0:T(8,128)S(1)} %get-tuple-element.262), channel_id=1, source_target_pairs={{0,128},{128,0},{1,129},{129,1},{2,130},{130,2},{3,131},{131,3},{4... | collective-permute-start | bytes 589832 | tf_op jit(solution)/shard_map/ppermute | solution.py:31
  139.1 79.2 %collective-permute-start.37 = (f32[384,128]{1,0:T(8,128)S(1)}, f32[384,128]{1,0:T(8,128)S(1)}, u32[]{:S(2)}, u32[]{:S(2)}) collective-permute-start(f32[384,128]{1,0:T(8,128)S(1)} %get-tuple-element.284), channel_id=1, source_target_pairs={{0,128},{128,0},{1,129},{129,1},{2,130},{130,2},{3,131},{131,3},{4... | collective-permute-start | bytes 589832 | tf_op jit(solution)/shard_map/ppermute | solution.py:31
  141.5 12.1 %collective-permute-start.31 = (f32[384,256]{1,0:T(8,128)S(1)}, f32[384,256]{1,0:T(8,128)S(1)}, u32[]{:S(2)}, u32[]{:S(2)}) collective-permute-start(f32[384,256]{1,0:T(8,128)S(1)} %get-tuple-element.265), channel_id=1, source_target_pairs={{0,16},{16,0},{1,17},{17,1},{2,18},{18,2},{3,19},{19,3},{4,20},{20... | collective-permute-start | bytes 1179656 | tf_op jit(solution)/shard_map/ppermute | solution.py:31
  154.7 16.1 %collective-permute-start.33 = (f32[384,256]{1,0:T(8,128)S(1)}, f32[384,256]{1,0:T(8,128)S(1)}, u32[]{:S(2)}, u32[]{:S(2)}) collective-permute-start(f32[384,256]{1,0:T(8,128)S(1)} %get-tuple-element.271), channel_id=1, source_target_pairs={{0,32},{32,0},{1,33},{33,1},{2,34},{34,2},{3,35},{35,3},{4,36},{36... | collective-permute-start | bytes 1179656 | tf_op jit(solution)/shard_map/ppermute | solution.py:31
  155.8 51.3 %collective-permute-start.35 = (f32[384,256]{1,0:T(8,128)S(1)}, f32[384,256]{1,0:T(8,128)S(1)}, u32[]{:S(2)}, u32[]{:S(2)}) collective-permute-start(f32[384,256]{1,0:T(8,128)S(1)} %get-tuple-element.278), channel_id=1, source_target_pairs={{0,64},{64,0},{1,65},{65,1},{2,66},{66,2},{3,67},{67,3},{4,68},{68... | collective-permute-start | bytes 1179656 | tf_op jit(solution)/shard_map/ppermute | solution.py:31
  171.8 42.5 %collective-permute-start.36 = (f32[384,256]{1,0:T(8,128)S(1)}, f32[384,256]{1,0:T(8,128)S(1)}, u32[]{:S(2)}, u32[]{:S(2)}) collective-permute-start(f32[384,256]{1,0:T(8,128)S(1)} %get-tuple-element.281), channel_id=1, source_target_pairs={{0,64},{64,0},{1,65},{65,1},{2,66},{66,2},{3,67},{67,3},{4,68},{68... | collective-permute-start | bytes 1179656 | tf_op jit(solution)/shard_map/ppermute | solution.py:31
  208.2 28.4 %collective-permute-start.38 = (f32[384,256]{1,0:T(8,128)S(1)}, f32[384,256]{1,0:T(8,128)S(1)}, u32[]{:S(2)}, u32[]{:S(2)}) collective-permute-start(f32[384,256]{1,0:T(8,128)S(1)} %get-tuple-element.288), channel_id=1, source_target_pairs={{0,128},{128,0},{1,129},{129,1},{2,130},{130,2},{3,131},{131,3},{4... | collective-permute-start | bytes 1179656 | tf_op jit(solution)/shard_map/ppermute | solution.py:31
  215.4 25.5 %collective-permute-start.39 = (f32[384,256]{1,0:T(8,128)S(1)}, f32[384,256]{1,0:T(8,128)S(1)}, u32[]{:S(2)}, u32[]{:S(2)}) collective-permute-start(f32[384,256]{1,0:T(8,128)S(1)} %get-tuple-element.292), channel_id=1, source_target_pairs={{0,128},{128,0},{1,129},{129,1},{2,130},{130,2},{3,131},{131,3},{4... | collective-permute-start | bytes 1179656 | tf_op jit(solution)/shard_map/ppermute | solution.py:31

commit v2 on v1

--- a/solution.py
+++ b/solution.py
@@ -11,8 +11,8 @@
 ORDER = (
     (3, 0), (3, 1), (0, 0), (3, 2), (1, 0), (2, 0), (0, 1), (3, 3), (0, 2), (1, 1), (3, 4), (4, 0),
     (1, 2), (0, 3), (3, 5), (0, 4), (1, 3), (4, 1), (3, 6), (0, 5), (1, 4), (4, 2), (1, 5), (0, 6),
-    (4, 3), (3, 7), (2, 1), (4, 4), (2, 2), (4, 5), (1, 6), (2, 3), (1, 7), (2, 4), (0, 7), (1, 8),
-    (2, 5), (4, 6), (2, 6), (3, 8), (4, 7), (2, 7), (0, 8), (4, 8), (2, 8),
+    (4, 3), (3, 7), (2, 1), (4, 4), (2, 2), (4, 5), (1, 6), (2, 3), (1, 7), (2, 4), (0, 7), (2, 5),
+    (3, 8), (4, 6), (0, 8), (2, 6), (1, 8), (4, 7), (2, 7), (4, 8), (2, 8),
 )
 ANY = pl.BlockSpec(memory_space=pl.ANY)
 VMEM = pl.BlockSpec(memory_space=pltpu.VMEM)
@@ -104,10 +104,8 @@
             send_ref[pl.ds(pl.multiple_of((i - blocks) * rows, rows), rows)] = product
 
 
-def first_kernel(start, token_ref, t_ref, c_ref, send_ref, keep_ref, next_ref, stacked, block, sem):
-    copy = pltpu.make_async_copy(c_ref.at[0, :, pl.ds(start, block.shape[1])], block, sem)
-    copy.start()
-    copy.wait()
+def first_kernel(start, token_ref, t_ref, c_ref, send_ref, keep_ref, next_ref, stacked):
+    block = c_ref.at[0, :, pl.ds(start, stacked.shape[1])]
     multiply(2, t_ref, (block,), send_ref, keep_ref, stacked)
     next_ref[...] = jnp.zeros_like(next_ref)
 
@@ -117,7 +115,7 @@
     next_ref[...] = jnp.zeros_like(next_ref)
 
 
-def stage(name, kernel, operands, specs, width, scratch=()):
+def stage(name, kernel, operands, specs, width):
     rank = operands[1].shape[0] // 2
     block = pltpu.VMEM((rank, width), jnp.float32)
     return pl.pallas_call(
@@ -125,7 +123,7 @@
         out_shape=(block, block, TOKEN),
         in_specs=specs,
         out_specs=(VMEM, VMEM, VMEM),
-        scratch_shapes=[pltpu.VMEM((3 * rank, width), jnp.bfloat16), *scratch],
+        scratch_shapes=[pltpu.VMEM((3 * rank, width), jnp.bfloat16)],
         cost_estimate=COST,
         compiler_params=PARAMS,
         name=name,
@@ -133,10 +131,8 @@
 
 
 def first_level(token, matrices, coeffs, start, width):
-    scratch = (pltpu.VMEM((coeffs.shape[1], width), jnp.float32), pltpu.SemaphoreType.DMA)
-    operands = (on_chip(token), on_chip(matrices), in_hbm(coeffs))
-    kernel = functools.partial(first_kernel, start)
-    return stage("first_level", kernel, operands, [VMEM, VMEM, ANY], width, scratch)
+    operands = tuple(map(on_chip, (token, matrices, coeffs)))
+    return stage("first_level", functools.partial(first_kernel, start), operands, [VMEM] * 3, width)
 
 
 def next_level(token, matrices, kept, arrived):

time: 243 us -> 239 us (0.984)
  the two profiles are of different devices: /device:TPU:18 before, /device:TPU:10 now
where the time goes in v2:
time: 239 us
  starting transfers between devices  90.1 us (38%)
  waiting for transfers between devices  86.2 us (36%)
  Pallas kernels  61.7 us (26%)
    ppermute x40, starting transfers between devices, partner(): return lax.ppermute(block, axis, route)  90.1 us
    ppermute x40, waiting for transfers between devices, partner(): return lax.ppermute(block, axis, route)  86.2 us
    pallas_call x40, Pallas kernels, stage(): pl.pallas_call(kernel, out_shape=(block, block, TOKEN), in_specs=specs, o...  43.3 us
    pallas_call x8, Pallas kernels, split_matrices(): pl.pallas_call(split_kernel, grid=(1,), out_shape=(pltpu.VMEM((2 * rank,...  13.9 us
  transfers between devices with their start and end apart: 40, of which 14 were waited for; matrix products, arithmetic and copies ran while one was open for 0% of the time, Pallas kernels for 23%

profile of v2, /device:TPU:10, one launch (start us, length us, event | category | flops | bytes accessed | tf_op | source)
XLA Modules:
  0.0 238.8 jit_solution(10187295317632355531)
XLA Ops:
  0.0 1.8 split_matrices.8
  1.9 1.4 first_level.5
  3.4 1.7 split_matrices.9
  5.1 1.0 next_level.35
  6.7 1.7 split_matrices.10
  8.5 1.2 first_level.6
  10.0 7.8 %collective-permute-done.1.arrived_ref = f32[384,256]{1,0:T(8,128)S(1)} collective-permute-done((f32[384,256]{1,0:T(8,128)S(1)}, f32[384,256]{1,0:T(8,128)S(1)}, u32[]{:S(2)}, u32[]{:S(2)}) %collective-permute-start.1) | collective-permute-done | bytes 393248 | tf_op jit(solution)/shard_map/ppermute | solution.py:31
  18.8 2.4 %collective-permute-start.3 = (f32[384,256]{1,0:T(8,128)S(1)}, f32[384,256]{1,0:T(8,128)S(1)}, u32[]{:S(2)}, u32[]{:S(2)}) collective-permute-start(f32[384,256]{1,0:T(8,128)S(1)} %get-tuple-element.172), channel_id=1, source_target_pairs={{0,4},{4,0},{1,5},{5,1},{2,6},{6,2},{3,7},{7,3},{8,12},{12,8},{9,1... | collective-permute-start | bytes 1179656 | tf_op jit(solution)/shard_map/ppermute | solution.py:31
  21.2 1.7 split_matrices.11
  23.0 1.2 first_level.7
  24.3 2.2 first_level.8
  27.4 1.4 collective-permute-start.4
  29.1 3.1 %collective-permute-done.3.arrived_ref = f32[384,256]{1,0:T(8,128)S(1)} collective-permute-done((f32[384,256]{1,0:T(8,128)S(1)}, f32[384,256]{1,0:T(8,128)S(1)}, u32[]{:S(2)}, u32[]{:S(2)}) %collective-permute-start.3) | collective-permute-done | bytes 393248 | tf_op jit(solution)/shard_map/ppermute | solution.py:31
  33.9 1.7 split_matrices.12
  37.5 1.6 collective-permute-start.7
  39.1 1.1 collective-permute-start.8
  40.2 1.9 collective-permute-done.6.arrived_ref
  43.2 2.3 collective-permute-start.9
  45.4 1.7 split_matrices.13
  47.2 1.4 first_level.9
  50.5 1.5 collective-permute-start.10
  51.9 2.3 collective-permute-start.11
  55.5 2.3 collective-permute-start.13
  57.8 1.7 split_matrices.14
  61.9 2.6 %collective-permute-start.14 = (f32[384,128]{1,0:T(8,128)S(1)}, f32[384,128]{1,0:T(8,128)S(1)}, u32[]{:S(2)}, u32[]{:S(2)}) collective-permute-start(f32[384,128]{1,0:T(8,128)S(1)} %get-tuple-element.213), channel_id=1, source_target_pairs={{0,16},{16,0},{1,17},{17,1},{2,18},{18,2},{3,19},{19,3},{4,20},{20... | collective-permute-start | bytes 589832 | tf_op jit(solution)/shard_map/ppermute | solution.py:31
  64.5 1.0 next_level.47
  65.6 1.6 collective-permute-start.16
  67.1 1.0 next_level.48
  68.2 3.3 %collective-permute-start.20 = (f32[384,256]{1,0:T(8,128)S(1)}, f32[384,256]{1,0:T(8,128)S(1)}, u32[]{:S(2)}, u32[]{:S(2)}) collective-permute-start(f32[384,256]{1,0:T(8,128)S(1)} %get-tuple-element.232), channel_id=1, source_target_pairs={{0,64},{64,0},{1,65},{65,1},{2,66},{66,2},{3,67},{67,3},{4,68},{68... | collective-permute-start | bytes 1179656 | tf_op jit(solution)/shard_map/ppermute | solution.py:31
  71.5 1.7 split_matrices.15
  75.1 1.2 collective-permute-start.17
  77.1 1.0 next_level.51
  78.1 2.2 collective-permute-start.19
  80.3 2.3 collective-permute-done.17.arrived_ref
  83.5 1.7 collective-permute-start.25
  85.1 7.0 %collective-permute-done.18.arrived_ref = f32[384,128]{1,0:T(8,128)S(1)} collective-permute-done((f32[384,128]{1,0:T(8,128)S(1)}, f32[384,128]{1,0:T(8,128)S(1)}, u32[]{:S(2)}, u32[]{:S(2)}) %collective-permute-start.18) | collective-permute-done | bytes 196640 | tf_op jit(solution)/shard_map/ppermute | solution.py:31
  94.0 1.0 next_level.54
  95.1 3.0 %collective-permute-start.22 = (f32[384,256]{1,0:T(8,128)S(1)}, f32[384,256]{1,0:T(8,128)S(1)}, u32[]{:S(2)}, u32[]{:S(2)}) collective-permute-start(f32[384,256]{1,0:T(8,128)S(1)} %get-tuple-element.238), channel_id=1, source_target_pairs={{0,8},{8,0},{1,9},{9,1},{2,10},{10,2},{3,11},{11,3},{4,12},{12,4},... | collective-permute-start | bytes 1179656 | tf_op jit(solution)/shard_map/ppermute | solution.py:31
  99.2 2.0 next_level.56
  101.3 5.9 %collective-permute-start.31 = (f32[384,256]{1,0:T(8,128)S(1)}, f32[384,256]{1,0:T(8,128)S(1)}, u32[]{:S(2)}, u32[]{:S(2)}) collective-permute-start(f32[384,256]{1,0:T(8,128)S(1)} %get-tuple-element.265), channel_id=1, source_target_pairs={{0,128},{128,0},{1,129},{129,1},{2,130},{130,2},{3,131},{131,3},{4... | collective-permute-start | bytes 1179656 | tf_op jit(solution)/shard_map/ppermute | solution.py:31
  107.2 1.0 next_level.57
  108.4 3.2 %collective-permute-done.23.arrived_ref = f32[384,256]{1,0:T(8,128)S(1)} collective-permute-done((f32[384,256]{1,0:T(8,128)S(1)}, f32[384,256]{1,0:T(8,128)S(1)}, u32[]{:S(2)}, u32[]{:S(2)}) %collective-permute-start.23) | collective-permute-done | bytes 393248 | tf_op jit(solution)/shard_map/ppermute | solution.py:31
  112.7 4.9 %collective-permute-done.24.arrived_ref = f32[384,256]{1,0:T(8,128)S(1)} collective-permute-done((f32[384,256]{1,0:T(8,128)S(1)}, f32[384,256]{1,0:T(8,128)S(1)}, u32[]{:S(2)}, u32[]{:S(2)}) %collective-permute-start.24) | collective-permute-done | bytes 393248 | tf_op jit(solution)/shard_map/ppermute | solution.py:31
  119.6 3.0 %collective-permute-start.27 = (f32[384,128]{1,0:T(8,128)S(1)}, f32[384,128]{1,0:T(8,128)S(1)}, u32[]{:S(2)}, u32[]{:S(2)}) collective-permute-start(f32[384,128]{1,0:T(8,128)S(1)} %get-tuple-element.253), channel_id=1, source_target_pairs={{0,64},{64,0},{1,65},{65,1},{2,66},{66,2},{3,67},{67,3},{4,68},{68... | collective-permute-start | bytes 589832 | tf_op jit(solution)/shard_map/ppermute | solution.py:31
  122.6 1.0 next_level.61
  124.1 2.8 %collective-permute-start.32 = (f32[384,256]{1,0:T(8,128)S(1)}, f32[384,256]{1,0:T(8,128)S(1)}, u32[]{:S(2)}, u32[]{:S(2)}) collective-permute-start(f32[384,256]{1,0:T(8,128)S(1)} %get-tuple-element.268), channel_id=1, source_target_pairs={{0,32},{32,0},{1,33},{33,1},{2,34},{34,2},{3,35},{35,3},{4,36},{36... | collective-permute-start | bytes 1179656 | tf_op jit(solution)/shard_map/ppermute | solution.py:31
  126.9 4.0 %collective-permute-done.27.arrived_ref = f32[384,128]{1,0:T(8,128)S(1)} collective-permute-done((f32[384,128]{1,0:T(8,128)S(1)}, f32[384,128]{1,0:T(8,128)S(1)}, u32[]{:S(2)}, u32[]{:S(2)}) %collective-permute-start.27) | collective-permute-done | bytes 196640 | tf_op jit(solution)/shard_map/ppermute | solution.py:31
  131.9 3.1 %collective-permute-start.35 = (f32[384,128]{1,0:T(8,128)S(1)}, f32[384,128]{1,0:T(8,128)S(1)}, u32[]{:S(2)}, u32[]{:S(2)}) collective-permute-start(f32[384,128]{1,0:T(8,128)S(1)} %get-tuple-element.278), channel_id=1, source_target_pairs={{0,128},{128,0},{1,129},{129,1},{2,130},{130,2},{3,131},{131,3},{4... | collective-permute-start | bytes 589832 | tf_op jit(solution)/shard_map/ppermute | solution.py:31
  135.0 1.0 next_level.63
  136.0 1.9 collective-permute-start.30
  138.9 2.1 collective-permute-start.33
  141.0 5.5 %collective-permute-done.30.arrived_ref = f32[384,256]{1,0:T(8,128)S(1)} collective-permute-done((f32[384,256]{1,0:T(8,128)S(1)}, f32[384,256]{1,0:T(8,128)S(1)}, u32[]{:S(2)}, u32[]{:S(2)}) %collective-permute-start.30) | collective-permute-done | bytes 393248 | tf_op jit(solution)/shard_map/ppermute | solution.py:31
  146.5 1.0 next_level.65
  148.5 1.0 next_level.66
  149.5 1.9 collective-permute-start.36
  151.4 3.4 %collective-permute-done.33.arrived_ref = f32[384,128]{1,0:T(8,128)S(1)} collective-permute-done((f32[384,128]{1,0:T(8,128)S(1)}, f32[384,128]{1,0:T(8,128)S(1)}, u32[]{:S(2)}, u32[]{:S(2)}) %collective-permute-start.33) | collective-permute-done | bytes 196640 | tf_op jit(solution)/shard_map/ppermute | solution.py:31
  155.5 12.4 %collective-permute-done.34.arrived_ref = f32[384,256]{1,0:T(8,128)S(1)} collective-permute-done((f32[384,256]{1,0:T(8,128)S(1)}, f32[384,256]{1,0:T(8,128)S(1)}, u32[]{:S(2)}, u32[]{:S(2)}) %collective-permute-start.34) | collective-permute-done | bytes 393248 | tf_op jit(solution)/shard_map/ppermute | solution.py:31
  169.8 1.0 next_level.68
  170.9 29.9 %collective-permute-start.38 = (f32[384,256]{1,0:T(8,128)S(1)}, f32[384,256]{1,0:T(8,128)S(1)}, u32[]{:S(2)}, u32[]{:S(2)}) collective-permute-start(f32[384,256]{1,0:T(8,128)S(1)} %get-tuple-element.288), channel_id=1, source_target_pairs={{0,128},{128,0},{1,129},{129,1},{2,130},{130,2},{3,131},{131,3},{4... | collective-permute-start | bytes 1179656 | tf_op jit(solution)/shard_map/ppermute | solution.py:31
  200.8 11.9 %collective-permute-done.37.arrived_ref = f32[384,256]{1,0:T(8,128)S(1)} collective-permute-done((f32[384,256]{1,0:T(8,128)S(1)}, f32[384,256]{1,0:T(8,128)S(1)}, u32[]{:S(2)}, u32[]{:S(2)}) %collective-permute-start.37) | collective-permute-done | bytes 393248 | tf_op jit(solution)/shard_map/ppermute | solution.py:31
  212.7 1.0 next_level.69
  213.7 4.0 %collective-permute-start.39 = (f32[384,256]{1,0:T(8,128)S(1)}, f32[384,256]{1,0:T(8,128)S(1)}, u32[]{:S(2)}, u32[]{:S(2)}) collective-permute-start(f32[384,256]{1,0:T(8,128)S(1)} %get-tuple-element.292), channel_id=1, source_target_pairs={{0,128},{128,0},{1,129},{129,1},{2,130},{130,2},{3,131},{131,3},{4... | collective-permute-start | bytes 1179656 | tf_op jit(solution)/shard_map/ppermute | solution.py:31
  218.6 18.6 %collective-permute-done.39.arrived_ref = f32[384,256]{1,0:T(8,128)S(1)} collective-permute-done((f32[384,256]{1,0:T(8,128)S(1)}, f32[384,256]{1,0:T(8,128)S(1)}, u32[]{:S(2)}, u32[]{:S(2)}) %collective-permute-start.39) | collective-permute-done | bytes 393248 | tf_op jit(solution)/shard_map/ppermute | solution.py:31
  237.2 1.4 write_result.9
  (72 shorter events, 29.5 us)
Async XLA Ops:
  0.0 1.9 copy-start
  3.3 1.8 collective-permute-start
  6.2 11.6 %collective-permute-start.1 = (f32[384,256]{1,0:T(8,128)S(1)}, f32[384,256]{1,0:T(8,128)S(1)}, u32[]{:S(2)}, u32[]{:S(2)}) collective-permute-start(f32[384,256]{1,0:T(8,128)S(1)} %get-tuple-element.162), channel_id=1, source_target_pairs={{0,2},{2,0},{1,3},{3,1},{4,6},{6,4},{5,7},{7,5},{8,10},{10,8},{9,1... | collective-permute-start | bytes 1179656 | tf_op jit(solution)/shard_map/ppermute | solution.py:31
  9.7 16.8 %collective-permute-start.2 = (f32[384,128]{1,0:T(8,128)S(1)}, f32[384,128]{1,0:T(8,128)S(1)}, u32[]{:S(2)}, u32[]{:S(2)}) collective-permute-start(f32[384,128]{1,0:T(8,128)S(1)} %get-tuple-element.168), channel_id=1, source_target_pairs={{0,1},{1,0},{2,3},{3,2},{4,5},{5,4},{6,7},{7,6},{8,9},{9,8},{10,11... | collective-permute-start | bytes 589832 | tf_op jit(solution)/shard_map/ppermute | solution.py:31
  18.8 13.4 %collective-permute-start.3 = (f32[384,256]{1,0:T(8,128)S(1)}, f32[384,256]{1,0:T(8,128)S(1)}, u32[]{:S(2)}, u32[]{:S(2)}) collective-permute-start(f32[384,256]{1,0:T(8,128)S(1)} %get-tuple-element.172), channel_id=1, source_target_pairs={{0,4},{4,0},{1,5},{5,1},{2,6},{6,2},{3,7},{7,3},{8,12},{12,8},{9,1... | collective-permute-start | bytes 1179656 | tf_op jit(solution)/shard_map/ppermute | solution.py:31
  24.2 12.3 %collective-permute-start.5 = (f32[384,128]{1,0:T(8,128)S(1)}, f32[384,128]{1,0:T(8,128)S(1)}, u32[]{:S(2)}, u32[]{:S(2)}) collective-permute-start(f32[384,128]{1,0:T(8,128)S(1)} %get-tuple-element.179), channel_id=1, source_target_pairs={{0,1},{1,0},{2,3},{3,2},{4,5},{5,4},{6,7},{7,6},{8,9},{9,8},{10,11... | collective-permute-start | bytes 589832 | tf_op jit(solution)/shard_map/ppermute | solution.py:31
  27.4 8.2 %collective-permute-start.4 = (f32[384,128]{1,0:T(8,128)S(1)}, f32[384,128]{1,0:T(8,128)S(1)}, u32[]{:S(2)}, u32[]{:S(2)}) collective-permute-start(f32[384,128]{1,0:T(8,128)S(1)} %get-tuple-element.176), channel_id=1, source_target_pairs={{0,2},{2,0},{1,3},{3,1},{4,6},{6,4},{5,7},{7,5},{8,10},{10,8},{9,1... | collective-permute-start | bytes 589832 | tf_op jit(solution)/shard_map/ppermute | solution.py:31
  28.8 70.3 %collective-permute-start.21 = (f32[384,256]{1,0:T(8,128)}, f32[384,256]{1,0:T(8,128)}, u32[]{:S(2)}, u32[]{:S(2)}) collective-permute-start(f32[384,256]{1,0:T(8,128)} %get-tuple-element.235), channel_id=1, source_target_pairs={{0,1},{1,0},{2,3},{3,2},{4,5},{5,4},{6,7},{7,6},{8,9},{9,8},{10,11... | collective-permute-start | bytes 1179656 | tf_op jit(solution)/shard_map/ppermute | solution.py:31
  33.2 8.9 %collective-permute-start.6 = (f32[384,256]{1,0:T(8,128)S(1)}, f32[384,256]{1,0:T(8,128)S(1)}, u32[]{:S(2)}, u32[]{:S(2)}) collective-permute-start(f32[384,256]{1,0:T(8,128)S(1)} %get-tuple-element.183), channel_id=1, source_target_pairs={{0,8},{8,0},{1,9},{9,1},{2,10},{10,2},{3,11},{11,3},{4,12},{12,4},... | collective-permute-start | bytes 1179656 | tf_op jit(solution)/shard_map/ppermute | solution.py:31
  37.5 11.1 %collective-permute-start.7 = (f32[384,128]{1,0:T(8,128)S(1)}, f32[384,128]{1,0:T(8,128)S(1)}, u32[]{:S(2)}, u32[]{:S(2)}) collective-permute-start(f32[384,128]{1,0:T(8,128)S(1)} %get-tuple-element.188), channel_id=1, source_target_pairs={{0,2},{2,0},{1,3},{3,1},{4,6},{6,4},{5,7},{7,5},{8,10},{10,8},{9,1... | collective-permute-start | bytes 589832 | tf_op jit(solution)/shard_map/ppermute | solution.py:31
  39.1 10.4 %collective-permute-start.8 = (f32[384,128]{1,0:T(8,128)S(1)}, f32[384,128]{1,0:T(8,128)S(1)}, u32[]{:S(2)}, u32[]{:S(2)}) collective-permute-start(f32[384,128]{1,0:T(8,128)S(1)} %get-tuple-element.191), channel_id=1, source_target_pairs={{0,4},{4,0},{1,5},{5,1},{2,6},{6,2},{3,7},{7,3},{8,12},{12,8},{9,1... | collective-permute-start | bytes 589832 | tf_op jit(solution)/shard_map/ppermute | solution.py:31
  43.2 11.3 %collective-permute-start.9 = (f32[384,256]{1,0:T(8,128)S(1)}, f32[384,256]{1,0:T(8,128)S(1)}, u32[]{:S(2)}, u32[]{:S(2)}) collective-permute-start(f32[384,256]{1,0:T(8,128)S(1)} %get-tuple-element.195), channel_id=1, source_target_pairs={{0,16},{16,0},{1,17},{17,1},{2,18},{18,2},{3,19},{19,3},{4,20},{20... | collective-permute-start | bytes 1179656 | tf_op jit(solution)/shard_map/ppermute | solution.py:31
  50.5 9.1 %collective-permute-start.10 = (f32[384,128]{1,0:T(8,128)S(1)}, f32[384,128]{1,0:T(8,128)S(1)}, u32[]{:S(2)}, u32[]{:S(2)}) collective-permute-start(f32[384,128]{1,0:T(8,128)S(1)} %get-tuple-element.199), channel_id=1, source_target_pairs={{0,8},{8,0},{1,9},{9,1},{2,10},{10,2},{3,11},{11,3},{4,12},{12,4},... | collective-permute-start | bytes 589832 | tf_op jit(solution)/shard_map/ppermute | solution.py:31
  51.9 8.6 %collective-permute-start.11 = (f32[384,128]{1,0:T(8,128)S(1)}, f32[384,128]{1,0:T(8,128)S(1)}, u32[]{:S(2)}, u32[]{:S(2)}) collective-permute-start(f32[384,128]{1,0:T(8,128)S(1)} %get-tuple-element.202), channel_id=1, source_target_pairs={{0,4},{4,0},{1,5},{5,1},{2,6},{6,2},{3,7},{7,3},{8,12},{12,8},{9,1... | collective-permute-start | bytes 589832 | tf_op jit(solution)/shard_map/ppermute | solution.py:31
  54.3 10.2 %collective-permute-start.12 = (f32[384,256]{1,0:T(8,128)S(1)}, f32[384,256]{1,0:T(8,128)S(1)}, u32[]{:S(2)}, u32[]{:S(2)}) collective-permute-start(f32[384,256]{1,0:T(8,128)S(1)} %get-tuple-element.205), channel_id=1, source_target_pairs={{0,1},{1,0},{2,3},{3,2},{4,5},{5,4},{6,7},{7,6},{8,9},{9,8},{10,11... | collective-permute-start | bytes 1179656 | tf_op jit(solution)/shard_map/ppermute | solution.py:31
  55.5 11.6 %collective-permute-start.13 = (f32[384,256]{1,0:T(8,128)S(1)}, f32[384,256]{1,0:T(8,128)S(1)}, u32[]{:S(2)}, u32[]{:S(2)}) collective-permute-start(f32[384,256]{1,0:T(8,128)S(1)} %get-tuple-element.209), channel_id=1, source_target_pairs={{0,32},{32,0},{1,33},{33,1},{2,34},{34,2},{3,35},{35,3},{4,36},{36... | collective-permute-start | bytes 1179656 | tf_op jit(solution)/shard_map/ppermute | solution.py:31
  61.4 12.8 %collective-permute-start.15 = (f32[384,128]{1,0:T(8,128)S(1)}, f32[384,128]{1,0:T(8,128)S(1)}, u32[]{:S(2)}, u32[]{:S(2)}) collective-permute-start(f32[384,128]{1,0:T(8,128)S(1)} %get-tuple-element.216), channel_id=1, source_target_pairs={{0,8},{8,0},{1,9},{9,1},{2,10},{10,2},{3,11},{11,3},{4,12},{12,4},... | collective-permute-start | bytes 589832 | tf_op jit(solution)/shard_map/ppermute | solution.py:31
  61.9 11.3 %collective-permute-start.14 = (f32[384,128]{1,0:T(8,128)S(1)}, f32[384,128]{1,0:T(8,128)S(1)}, u32[]{:S(2)}, u32[]{:S(2)}) collective-permute-start(f32[384,128]{1,0:T(8,128)S(1)} %get-tuple-element.213), channel_id=1, source_target_pairs={{0,16},{16,0},{1,17},{17,1},{2,18},{18,2},{3,19},{19,3},{4,20},{20... | collective-permute-start | bytes 589832 | tf_op jit(solution)/shard_map/ppermute | solution.py:31
  65.6 11.5 %collective-permute-start.16 = (f32[384,256]{1,0:T(8,128)S(1)}, f32[384,256]{1,0:T(8,128)S(1)}, u32[]{:S(2)}, u32[]{:S(2)}) collective-permute-start(f32[384,256]{1,0:T(8,128)S(1)} %get-tuple-element.219), channel_id=1, source_target_pairs={{0,2},{2,0},{1,3},{3,1},{4,6},{6,4},{5,7},{7,5},{8,10},{10,8},{9,1... | collective-permute-start | bytes 1179656 | tf_op jit(solution)/shard_map/ppermute | solution.py:31
  68.2 29.9 %collective-permute-start.20 = (f32[384,256]{1,0:T(8,128)S(1)}, f32[384,256]{1,0:T(8,128)S(1)}, u32[]{:S(2)}, u32[]{:S(2)}) collective-permute-start(f32[384,256]{1,0:T(8,128)S(1)} %get-tuple-element.232), channel_id=1, source_target_pairs={{0,64},{64,0},{1,65},{65,1},{2,66},{66,2},{3,67},{67,3},{4,68},{68... | collective-permute-start | bytes 1179656 | tf_op jit(solution)/shard_map/ppermute | solution.py:31
  75.1 7.4 %collective-permute-start.17 = (f32[384,128]{1,0:T(8,128)S(1)}, f32[384,128]{1,0:T(8,128)S(1)}, u32[]{:S(2)}, u32[]{:S(2)}) collective-permute-start(f32[384,128]{1,0:T(8,128)S(1)} %get-tuple-element.222), channel_id=1, source_target_pairs={{0,16},{16,0},{1,17},{17,1},{2,18},{18,2},{3,19},{19,3},{4,20},{20... | collective-permute-start | bytes 589832 | tf_op jit(solution)/shard_map/ppermute | solution.py:31
  76.4 15.8 %collective-permute-start.18 = (f32[384,128]{1,0:T(8,128)S(1)}, f32[384,128]{1,0:T(8,128)S(1)}, u32[]{:S(2)}, u32[]{:S(2)}) collective-permute-start(f32[384,128]{1,0:T(8,128)S(1)} %get-tuple-element.225), channel_id=1, source_target_pairs={{0,32},{32,0},{1,33},{33,1},{2,34},{34,2},{3,35},{35,3},{4,36},{36... | collective-permute-start | bytes 589832 | tf_op jit(solution)/shard_map/ppermute | solution.py:31
  78.1 15.9 %collective-permute-start.19 = (f32[384,256]{1,0:T(8,128)S(1)}, f32[384,256]{1,0:T(8,128)S(1)}, u32[]{:S(2)}, u32[]{:S(2)}) collective-permute-start(f32[384,256]{1,0:T(8,128)S(1)} %get-tuple-element.228), channel_id=1, source_target_pairs={{0,4},{4,0},{1,5},{5,1},{2,6},{6,2},{3,7},{7,3},{8,12},{12,8},{9,1... | collective-permute-start | bytes 1179656 | tf_op jit(solution)/shard_map/ppermute | solution.py:31
  83.5 35.2 %collective-permute-start.25 = (f32[384,128]{1,0:T(8,128)S(1)}, f32[384,128]{1,0:T(8,128)S(1)}, u32[]{:S(2)}, u32[]{:S(2)}) collective-permute-start(f32[384,128]{1,0:T(8,128)S(1)} %get-tuple-element.247), channel_id=1, source_target_pairs={{0,32},{32,0},{1,33},{33,1},{2,34},{34,2},{3,35},{35,3},{4,36},{36... | collective-permute-start | bytes 589832 | tf_op jit(solution)/shard_map/ppermute | solution.py:31
  93.1 44.9 %collective-permute-start.29 = (f32[384,128]{1,0:T(8,128)S(1)}, f32[384,128]{1,0:T(8,128)S(1)}, u32[]{:S(2)}, u32[]{:S(2)}) collective-permute-start(f32[384,128]{1,0:T(8,128)S(1)} %get-tuple-element.259), channel_id=1, source_target_pairs={{0,64},{64,0},{1,65},{65,1},{2,66},{66,2},{3,67},{67,3},{4,68},{68... | collective-permute-start | bytes 589832 | tf_op jit(solution)/shard_map/ppermute | solution.py:31
  95.1 12.1 %collective-permute-start.22 = (f32[384,256]{1,0:T(8,128)S(1)}, f32[384,256]{1,0:T(8,128)S(1)}, u32[]{:S(2)}, u32[]{:S(2)}) collective-permute-start(f32[384,256]{1,0:T(8,128)S(1)} %get-tuple-element.238), channel_id=1, source_target_pairs={{0,8},{8,0},{1,9},{9,1},{2,10},{10,2},{3,11},{11,3},{4,12},{12,4},... | collective-permute-start | bytes 1179656 | tf_op jit(solution)/shard_map/ppermute | solution.py:31
  101.2 10.4 %collective-permute-start.23 = (f32[384,256]{1,0:T(8,128)S(1)}, f32[384,256]{1,0:T(8,128)S(1)}, u32[]{:S(2)}, u32[]{:S(2)}) collective-permute-start(f32[384,256]{1,0:T(8,128)S(1)} %get-tuple-element.241), channel_id=1, source_target_pairs={{0,2},{2,0},{1,3},{3,1},{4,6},{6,4},{5,7},{7,5},{8,10},{10,8},{9,1... | collective-permute-start | bytes 1179656 | tf_op jit(solution)/shard_map/ppermute | solution.py:31
  101.3 46.3 %collective-permute-start.31 = (f32[384,256]{1,0:T(8,128)S(1)}, f32[384,256]{1,0:T(8,128)S(1)}, u32[]{:S(2)}, u32[]{:S(2)}) collective-permute-start(f32[384,256]{1,0:T(8,128)S(1)} %get-tuple-element.265), channel_id=1, source_target_pairs={{0,128},{128,0},{1,129},{129,1},{2,130},{130,2},{3,131},{131,3},{4... | collective-permute-start | bytes 1179656 | tf_op jit(solution)/shard_map/ppermute | solution.py:31
  108.3 9.4 %collective-permute-start.24 = (f32[384,256]{1,0:T(8,128)S(1)}, f32[384,256]{1,0:T(8,128)S(1)}, u32[]{:S(2)}, u32[]{:S(2)}) collective-permute-start(f32[384,256]{1,0:T(8,128)S(1)} %get-tuple-element.244), channel_id=1, source_target_pairs={{0,16},{16,0},{1,17},{17,1},{2,18},{18,2},{3,19},{19,3},{4,20},{20... | collective-permute-start | bytes 1179656 | tf_op jit(solution)/shard_map/ppermute | solution.py:31
  112.6 10.0 %collective-permute-start.26 = (f32[384,256]{1,0:T(8,128)S(1)}, f32[384,256]{1,0:T(8,128)S(1)}, u32[]{:S(2)}, u32[]{:S(2)}) collective-permute-start(f32[384,256]{1,0:T(8,128)S(1)} %get-tuple-element.250), channel_id=1, source_target_pairs={{0,4},{4,0},{1,5},{5,1},{2,6},{6,2},{3,7},{7,3},{8,12},{12,8},{9,1... | collective-permute-start | bytes 1179656 | tf_op jit(solution)/shard_map/ppermute | solution.py:31
  119.6 11.3 %collective-permute-start.27 = (f32[384,128]{1,0:T(8,128)S(1)}, f32[384,128]{1,0:T(8,128)S(1)}, u32[]{:S(2)}, u32[]{:S(2)}) collective-permute-start(f32[384,128]{1,0:T(8,128)S(1)} %get-tuple-element.253), channel_id=1, source_target_pairs={{0,64},{64,0},{1,65},{65,1},{2,66},{66,2},{3,67},{67,3},{4,68},{68... | collective-permute-start | bytes 589832 | tf_op jit(solution)/shard_map/ppermute | solution.py:31
  123.7 11.3 %collective-permute-start.28 = (f32[384,256]{1,0:T(8,128)S(1)}, f32[384,256]{1,0:T(8,128)S(1)}, u32[]{:S(2)}, u32[]{:S(2)}) collective-permute-start(f32[384,256]{1,0:T(8,128)S(1)} %get-tuple-element.256), channel_id=1, source_target_pairs={{0,8},{8,0},{1,9},{9,1},{2,10},{10,2},{3,11},{11,3},{4,12},{12,4},... | collective-permute-start | bytes 1179656 | tf_op jit(solution)/shard_map/ppermute | solution.py:31
  124.1 24.4 %collective-permute-start.32 = (f32[384,256]{1,0:T(8,128)S(1)}, f32[384,256]{1,0:T(8,128)S(1)}, u32[]{:S(2)}, u32[]{:S(2)}) collective-permute-start(f32[384,256]{1,0:T(8,128)S(1)} %get-tuple-element.268), channel_id=1, source_target_pairs={{0,32},{32,0},{1,33},{33,1},{2,34},{34,2},{3,35},{35,3},{4,36},{36... | collective-permute-start | bytes 1179656 | tf_op jit(solution)/shard_map/ppermute | solution.py:31
  131.9 37.2 %collective-permute-start.35 = (f32[384,128]{1,0:T(8,128)S(1)}, f32[384,128]{1,0:T(8,128)S(1)}, u32[]{:S(2)}, u32[]{:S(2)}) collective-permute-start(f32[384,128]{1,0:T(8,128)S(1)} %get-tuple-element.278), channel_id=1, source_target_pairs={{0,128},{128,0},{1,129},{129,1},{2,130},{130,2},{3,131},{131,3},{4... | collective-permute-start | bytes 589832 | tf_op jit(solution)/shard_map/ppermute | solution.py:31
  136.0 10.5 %collective-permute-start.30 = (f32[384,256]{1,0:T(8,128)S(1)}, f32[384,256]{1,0:T(8,128)S(1)}, u32[]{:S(2)}, u32[]{:S(2)}) collective-permute-start(f32[384,256]{1,0:T(8,128)S(1)} %get-tuple-element.262), channel_id=1, source_target_pairs={{0,16},{16,0},{1,17},{17,1},{2,18},{18,2},{3,19},{19,3},{4,20},{20... | collective-permute-start | bytes 1179656 | tf_op jit(solution)/shard_map/ppermute | solution.py:31
  138.9 15.9 %collective-permute-start.33 = (f32[384,128]{1,0:T(8,128)S(1)}, f32[384,128]{1,0:T(8,128)S(1)}, u32[]{:S(2)}, u32[]{:S(2)}) collective-permute-start(f32[384,128]{1,0:T(8,128)S(1)} %get-tuple-element.271), channel_id=1, source_target_pairs={{0,128},{128,0},{1,129},{129,1},{2,130},{130,2},{3,131},{131,3},{4... | collective-permute-start | bytes 589832 | tf_op jit(solution)/shard_map/ppermute | solution.py:31
  147.5 20.4 %collective-permute-start.34 = (f32[384,256]{1,0:T(8,128)S(1)}, f32[384,256]{1,0:T(8,128)S(1)}, u32[]{:S(2)}, u32[]{:S(2)}) collective-permute-start(f32[384,256]{1,0:T(8,128)S(1)} %get-tuple-element.275), channel_id=1, source_target_pairs={{0,32},{32,0},{1,33},{33,1},{2,34},{34,2},{3,35},{35,3},{4,36},{36... | collective-permute-start | bytes 1179656 | tf_op jit(solution)/shard_map/ppermute | solution.py:31
  149.5 20.3 %collective-permute-start.36 = (f32[384,256]{1,0:T(8,128)S(1)}, f32[384,256]{1,0:T(8,128)S(1)}, u32[]{:S(2)}, u32[]{:S(2)}) collective-permute-start(f32[384,256]{1,0:T(8,128)S(1)} %get-tuple-element.282), channel_id=1, source_target_pairs={{0,64},{64,0},{1,65},{65,1},{2,66},{66,2},{3,67},{67,3},{4,68},{68... | collective-permute-start | bytes 1179656 | tf_op jit(solution)/shard_map/ppermute | solution.py:31
  169.0 43.7 %collective-permute-start.37 = (f32[384,256]{1,0:T(8,128)S(1)}, f32[384,256]{1,0:T(8,128)S(1)}, u32[]{:S(2)}, u32[]{:S(2)}) collective-permute-start(f32[384,256]{1,0:T(8,128)S(1)} %get-tuple-element.285), channel_id=1, source_target_pairs={{0,64},{64,0},{1,65},{65,1},{2,66},{66,2},{3,67},{67,3},{4,68},{68... | collective-permute-start | bytes 1179656 | tf_op jit(solution)/shard_map/ppermute | solution.py:31
  170.9 46.8 %collective-permute-start.38 = (f32[384,256]{1,0:T(8,128)S(1)}, f32[384,256]{1,0:T(8,128)S(1)}, u32[]{:S(2)}, u32[]{:S(2)}) collective-permute-start(f32[384,256]{1,0:T(8,128)S(1)} %get-tuple-element.288), channel_id=1, source_target_pairs={{0,128},{128,0},{1,129},{129,1},{2,130},{130,2},{3,131},{131,3},{4... | collective-permute-start | bytes 1179656 | tf_op jit(solution)/shard_map/ppermute | solution.py:31
  213.7 23.5 %collective-permute-start.39 = (f32[384,256]{1,0:T(8,128)S(1)}, f32[384,256]{1,0:T(8,128)S(1)}, u32[]{:S(2)}, u32[]{:S(2)}) collective-permute-start(f32[384,256]{1,0:T(8,128)S(1)} %get-tuple-element.292), channel_id=1, source_target_pairs={{0,128},{128,0},{1,129},{129,1},{2,130},{130,2},{3,131},{131,3},{4... | collective-permute-start | bytes 1179656 | tf_op jit(solution)/shard_map/ppermute | solution.py:31

commit v3 on v2

--- a/solution.py
+++ b/solution.py
@@ -7,13 +7,14 @@
 from jax.sharding import PartitionSpec as P
 
 LEVELS = 8
-WIDTHS = (128, 128, 256, 256, 256)
+WIDTHS = (256, 128, 128, 256, 256)
 ORDER = (
-    (3, 0), (3, 1), (0, 0), (3, 2), (1, 0), (2, 0), (0, 1), (3, 3), (0, 2), (1, 1), (3, 4), (4, 0),
-    (1, 2), (0, 3), (3, 5), (0, 4), (1, 3), (4, 1), (3, 6), (0, 5), (1, 4), (4, 2), (1, 5), (0, 6),
-    (4, 3), (3, 7), (2, 1), (4, 4), (2, 2), (4, 5), (1, 6), (2, 3), (1, 7), (2, 4), (0, 7), (2, 5),
-    (3, 8), (4, 6), (0, 8), (2, 6), (1, 8), (4, 7), (2, 7), (4, 8), (2, 8),
+    (0, 0), (0, 1), (0, 2), (1, 0), (0, 3), (1, 1), (2, 1), (0, 4), (1, 2), (2, 2), (1, 3), (0, 5),
+    (2, 3), (4, 1), (1, 4), (0, 6), (1, 5), (4, 2), (2, 4), (1, 6), (2, 5), (4, 3), (0, 7), (3, 1),
+    (4, 4), (3, 2), (4, 5), (2, 6), (3, 3), (2, 7), (3, 4), (1, 7), (3, 5), (4, 6), (0, 8), (2, 8),
+    (3, 6), (1, 8), (4, 7), (3, 7), (4, 8), (3, 8),
 )
+LAST = {0: 0, 1: 4}
 ANY = pl.BlockSpec(memory_space=pl.ANY)
 VMEM = pl.BlockSpec(memory_space=pltpu.VMEM)
 PARAMS = pltpu.CompilerParams(vmem_limit_bytes=12 << 20)
@@ -106,12 +107,14 @@
 
 def first_kernel(start, token_ref, t_ref, c_ref, send_ref, keep_ref, next_ref, stacked):
     block = c_ref.at[0, :, pl.ds(start, stacked.shape[1])]
-    multiply(2, t_ref, (block,), send_ref, keep_ref, stacked)
-    next_ref[...] = jnp.zeros_like(next_ref)
-
-
-def level_kernel(token_ref, t_ref, kept_ref, arrived_ref, send_ref, keep_ref, next_ref, stacked):
-    multiply(1, t_ref, (kept_ref, arrived_ref), send_ref, keep_ref, stacked)
+    multiply(1, t_ref, (block,), send_ref, keep_ref, stacked)
+    next_ref[...] = jnp.zeros_like(next_ref)
+
+
+def level_kernel(start, token_ref, t_ref, kept_ref, arrived_ref, send_ref, keep_ref, next_ref, stacked):
+    columns = pl.ds(start, stacked.shape[1])
+    parts = (kept_ref.at[:, columns], arrived_ref.at[:, columns])
+    multiply(1, t_ref, parts, send_ref, keep_ref, stacked)
     next_ref[...] = jnp.zeros_like(next_ref)
 
 
@@ -135,9 +138,9 @@
     return stage("first_level", functools.partial(first_kernel, start), operands, [VMEM] * 3, width)
 
 
-def next_level(token, matrices, kept, arrived):
+def next_level(token, matrices, kept, arrived, start, width):
     operands = tuple(map(on_chip, (token, matrices, kept, arrived)))
-    return stage("next_level", level_kernel, operands, [VMEM] * 4, kept.shape[1])
+    return stage("next_level", functools.partial(level_kernel, start), operands, [VMEM] * 4, width)
 
 
 def write_kernel(start, token_ref, kept_ref, arrived_ref, *refs):
@@ -179,15 +182,21 @@
     matrices = [first]
     result = None
     for chunk, level in ORDER:
+        start, width = starts[chunk], WIDTHS[chunk]
         if level == LEVELS:
-            result, token = write_result(token, *parts[chunk], starts[chunk], coeffs.shape, result)
+            result, token = write_result(token, *parts[chunk][:2], start, coeffs.shape, result)
             continue
         if level == 0:
-            stepped = first_level(token, matrices[0], coeffs, starts[chunk], WIDTHS[chunk])
+            last = LAST[chunk]
+            width = starts[last] + WIDTHS[last] - start
+            stepped = first_level(token, matrices[0], coeffs, start, width)
         else:
-            stepped = next_level(token, matrices[level], *parts[chunk])
+            kept, arrived, base = parts[chunk]
+            stepped = next_level(token, matrices[level], kept, arrived, start - base, width)
         outgoing, kept, token = stepped
-        parts[chunk] = (kept, partner(outgoing, "bfly", level % bit_count))
+        arrived = partner(outgoing, "bfly", level % bit_count)
+        for member in range(chunk, LAST[chunk] + 1) if level == 0 else (chunk,):
+            parts[member] = (kept, arrived, start)
         if len(matrices) == level + 1 < LEVELS:
             following, token = split_matrices(token, transfers, level + 1)
             matrices.append(following)

time: 239 us -> 227 us (0.950)
  starting transfers between devices: 90.1 us -> 62.5 us
  waiting for transfers between devices: 86.2 us -> 106 us
  Pallas kernels: 61.7 us -> 56.6 us
    ppermute x40 -> x37, starting transfers between devices: 90.1 us -> 62.5 us  [partner(): return lax.ppermute(block, axis, route)]
    ppermute x40 -> x37, waiting for transfers between devices: 86.2 us -> 106 us  [partner(): return lax.ppermute(block, axis, route)]
    pallas_call x40 -> x37, Pallas kernels: 43.3 us -> 38.1 us  [stage(): pl.pallas_call(kernel, out_shape=(block, block, TOKEN), in_specs=specs, o...]
  transfers between devices with their start and end apart: 40 -> 37, of which waited for: 14 -> 14; matrix products, arithmetic and copies ran while one was open for 0% -> 0% of each run, Pallas kernels for 23% -> 22%
where the time goes in v3:
time: 227 us; the launch traced here: 226 us
  waiting for transfers between devices  106 us (47%)
  starting transfers between devices  62.5 us (28%)
  Pallas kernels  56.6 us (25%)
    ppermute x37, waiting for transfers between devices, partner(): return lax.ppermute(block, axis, route)  106 us
    ppermute x37, starting transfers between devices, partner(): return lax.ppermute(block, axis, route)  62.5 us
    pallas_call x37, Pallas kernels, stage(): pl.pallas_call(kernel, out_shape=(block, block, TOKEN), in_specs=specs, o...  38.1 us
    pallas_call x8, Pallas kernels, split_matrices(): pl.pallas_call(split_kernel, grid=(1,), out_shape=(pltpu.VMEM((2 * rank,...  13.9 us
  transfers between devices with their start and end apart: 37, of which 14 were waited for; matrix products, arithmetic and copies ran while one was open for 0% of the time, Pallas kernels for 22%

profile of v3, /device:TPU:10, one launch (start us, length us, event | category | flops | bytes accessed | tf_op | source)
XLA Modules:
  0.0 225.7 jit_solution(11872222335327481532)
XLA Ops:
  0.0 1.8 split_matrices.8
  3.0 1.7 split_matrices.9
  4.7 1.1 next_level.35
  6.3 1.7 split_matrices.10
  8.1 9.3 %collective-permute-done.1.arrived_ref = f32[384,256]{1,0:T(8,128)S(1)} collective-permute-done((f32[384,256]{1,0:T(8,128)S(1)}, f32[384,256]{1,0:T(8,128)S(1)}, u32[]{:S(2)}, u32[]{:S(2)}) %collective-permute-start.1) | collective-permute-done | bytes 393248 | tf_op jit(solution)/shard_map/ppermute | solution.py:32
  17.4 1.0 next_level.36
  18.5 2.4 %collective-permute-start.2 = (f32[384,256]{1,0:T(8,128)S(1)}, f32[384,256]{1,0:T(8,128)S(1)}, u32[]{:S(2)}, u32[]{:S(2)}) collective-permute-start(f32[384,256]{1,0:T(8,128)S(1)} %get-tuple-element.158), channel_id=1, source_target_pairs={{0,4},{4,0},{1,5},{5,1},{2,6},{6,2},{3,7},{7,3},{8,12},{12,8},{9,1... | collective-permute-start | bytes 1179656 | tf_op jit(solution)/shard_map/ppermute | solution.py:32
  20.8 1.7 split_matrices.11
  22.6 2.3 first_level.3
  24.9 5.8 %collective-permute-done.2.arrived_ref = f32[384,256]{1,0:T(8,128)S(1)} collective-permute-done((f32[384,256]{1,0:T(8,128)S(1)}, f32[384,256]{1,0:T(8,128)S(1)}, u32[]{:S(2)}, u32[]{:S(2)}) %collective-permute-start.2) | collective-permute-done | bytes 393248 | tf_op jit(solution)/shard_map/ppermute | solution.py:32
  30.8 1.0 next_level.37
  31.8 1.3 collective-permute-start.4
  33.1 1.7 split_matrices.12
  35.8 1.6 collective-permute-start.5
  38.9 2.8 %collective-permute-done.4.arrived_ref = f32[384,256]{1,0:T(8,128)S(1)} collective-permute-done((f32[384,256]{1,0:T(8,128)S(1)}, f32[384,256]{1,0:T(8,128)S(1)}, u32[]{:S(2)}, u32[]{:S(2)}) %collective-permute-start.4) | collective-permute-done | bytes 393248 | tf_op jit(solution)/shard_map/ppermute | solution.py:32
  41.7 1.0 next_level.40
  42.8 2.2 collective-permute-start.8
  45.0 1.7 split_matrices.13
  47.7 2.4 %collective-permute-start.7 = (f32[384,128]{1,0:T(8,128)S(1)}, f32[384,128]{1,0:T(8,128)S(1)}, u32[]{:S(2)}, u32[]{:S(2)}) collective-permute-start(f32[384,128]{1,0:T(8,128)S(1)} %get-tuple-element.177), channel_id=1, source_target_pairs={{0,4},{4,0},{1,5},{5,1},{2,6},{6,2},{3,7},{7,3},{8,12},{12,8},{9,1... | collective-permute-start | bytes 589832 | tf_op jit(solution)/shard_map/ppermute | solution.py:32
  51.0 1.3 collective-permute-start.9
  52.3 4.4 %collective-permute-done.7.arrived_ref = f32[384,128]{1,0:T(8,128)S(1)} collective-permute-done((f32[384,128]{1,0:T(8,128)S(1)}, f32[384,128]{1,0:T(8,128)S(1)}, u32[]{:S(2)}, u32[]{:S(2)}) %collective-permute-start.7) | collective-permute-done | bytes 196640 | tf_op jit(solution)/shard_map/ppermute | solution.py:32
  57.7 1.5 collective-permute-start.10
  59.2 1.0 next_level.44
  60.2 2.0 collective-permute-start.11
  62.3 1.7 split_matrices.14
  65.7 1.0 next_level.46
  68.1 1.5 collective-permute-start.12
  69.6 1.0 next_level.48
  70.7 3.9 %collective-permute-start.18 = (f32[384,256]{1,0:T(8,128)S(1)}, f32[384,256]{1,0:T(8,128)S(1)}, u32[]{:S(2)}, u32[]{:S(2)}) collective-permute-start(f32[384,256]{1,0:T(8,128)S(1)} %get-tuple-element.216), channel_id=1, source_target_pairs={{0,64},{64,0},{1,65},{65,1},{2,66},{66,2},{3,67},{67,3},{4,68},{68... | collective-permute-start | bytes 1179656 | tf_op jit(solution)/shard_map/ppermute | solution.py:32
  74.6 1.7 split_matrices.15
  78.3 1.0 next_level.50
  81.1 1.8 collective-permute-start.17
  82.9 7.7 %collective-permute-done.15.arrived_ref = f32[384,128]{1,0:T(8,128)S(1)} collective-permute-done((f32[384,128]{1,0:T(8,128)S(1)}, f32[384,128]{1,0:T(8,128)S(1)}, u32[]{:S(2)}, u32[]{:S(2)}) %collective-permute-start.15) | collective-permute-done | bytes 196640 | tf_op jit(solution)/shard_map/ppermute | solution.py:32
  92.7 1.0 next_level.54
  93.8 6.1 %collective-permute-start.19 = (f32[384,256]{1,0:T(8,128)S(1)}, f32[384,256]{1,0:T(8,128)S(1)}, u32[]{:S(2)}, u32[]{:S(2)}) collective-permute-start(f32[384,256]{1,0:T(8,128)S(1)} %get-tuple-element.220), channel_id=1, source_target_pairs={{0,8},{8,0},{1,9},{9,1},{2,10},{10,2},{3,11},{11,3},{4,12},{12,4},... | collective-permute-start | bytes 1179656 | tf_op jit(solution)/shard_map/ppermute | solution.py:32
  99.9 1.0 next_level.55
  100.9 1.1 next_level.56
  102.0 1.1 collective-permute-start.20
  103.1 5.3 %collective-permute-start.29 = (f32[384,256]{1,0:T(8,128)S(1)}, f32[384,256]{1,0:T(8,128)S(1)}, u32[]{:S(2)}, u32[]{:S(2)}) collective-permute-start(f32[384,256]{1,0:T(8,128)S(1)} %get-tuple-element.250), channel_id=1, source_target_pairs={{0,128},{128,0},{1,129},{129,1},{2,130},{130,2},{3,131},{131,3},{4... | collective-permute-start | bytes 1179656 | tf_op jit(solution)/shard_map/ppermute | solution.py:32
  108.4 1.0 next_level.57
  109.5 1.9 collective-permute-done.20.arrived_ref
  111.4 1.0 next_level.58
  112.8 9.9 %collective-permute-done.21.arrived_ref = f32[384,256]{1,0:T(8,128)S(1)} collective-permute-done((f32[384,256]{1,0:T(8,128)S(1)}, f32[384,256]{1,0:T(8,128)S(1)}, u32[]{:S(2)}, u32[]{:S(2)}) %collective-permute-start.21) | collective-permute-done | bytes 393248 | tf_op jit(solution)/shard_map/ppermute | solution.py:32
  124.7 1.4 collective-permute-start.24
  127.1 2.3 %collective-permute-start.25 = (f32[384,256]{1,0:T(8,128)S(1)}, f32[384,256]{1,0:T(8,128)S(1)}, u32[]{:S(2)}, u32[]{:S(2)}) collective-permute-start(f32[384,256]{1,0:T(8,128)S(1)} %get-tuple-element.238), channel_id=1, source_target_pairs={{0,8},{8,0},{1,9},{9,1},{2,10},{10,2},{3,11},{11,3},{4,12},{12,4},... | collective-permute-start | bytes 1179656 | tf_op jit(solution)/shard_map/ppermute | solution.py:32
  129.4 1.9 collective-permute-start.28
  131.3 9.7 %collective-permute-done.24.arrived_ref = f32[384,128]{1,0:T(8,128)S(1)} collective-permute-done((f32[384,128]{1,0:T(8,128)S(1)}, f32[384,128]{1,0:T(8,128)S(1)}, u32[]{:S(2)}, u32[]{:S(2)}) %collective-permute-start.24) | collective-permute-done | bytes 196640 | tf_op jit(solution)/shard_map/ppermute | solution.py:32
  141.9 1.6 collective-permute-start.30
  143.5 1.0 next_level.63
  145.6 4.5 %collective-permute-start.32 = (f32[384,128]{1,0:T(8,128)S(1)}, f32[384,128]{1,0:T(8,128)S(1)}, u32[]{:S(2)}, u32[]{:S(2)}) collective-permute-start(f32[384,128]{1,0:T(8,128)S(1)} %get-tuple-element.260), channel_id=1, source_target_pairs={{0,128},{128,0},{1,129},{129,1},{2,130},{130,2},{3,131},{131,3},{4... | collective-permute-start | bytes 589832 | tf_op jit(solution)/shard_map/ppermute | solution.py:32
  150.1 3.8 %collective-permute-done.27.arrived_ref = f32[384,256]{1,0:T(8,128)S(1)} collective-permute-done((f32[384,256]{1,0:T(8,128)S(1)}, f32[384,256]{1,0:T(8,128)S(1)}, u32[]{:S(2)}, u32[]{:S(2)}) %collective-permute-start.27) | collective-permute-done | bytes 393248 | tf_op jit(solution)/shard_map/ppermute | solution.py:32
  153.9 1.0 next_level.65
  155.1 1.0 next_level.66
  156.1 2.9 %collective-permute-start.33 = (f32[384,256]{1,0:T(8,128)S(1)}, f32[384,256]{1,0:T(8,128)S(1)}, u32[]{:S(2)}, u32[]{:S(2)}) collective-permute-start(f32[384,256]{1,0:T(8,128)S(1)} %get-tuple-element.264), channel_id=1, source_target_pairs={{0,64},{64,0},{1,65},{65,1},{2,66},{66,2},{3,67},{67,3},{4,68},{68... | collective-permute-start | bytes 1179656 | tf_op jit(solution)/shard_map/ppermute | solution.py:32
  160.7 6.6 %collective-permute-done.31.arrived_ref = f32[384,256]{1,0:T(8,128)S(1)} collective-permute-done((f32[384,256]{1,0:T(8,128)S(1)}, f32[384,256]{1,0:T(8,128)S(1)}, u32[]{:S(2)}, u32[]{:S(2)}) %collective-permute-start.31) | collective-permute-done | bytes 393248 | tf_op jit(solution)/shard_map/ppermute | solution.py:32
  167.3 1.0 next_level.67
  169.2 21.1 %collective-permute-done.33.arrived_ref = f32[384,256]{1,0:T(8,128)S(1)} collective-permute-done((f32[384,256]{1,0:T(8,128)S(1)}, f32[384,256]{1,0:T(8,128)S(1)}, u32[]{:S(2)}, u32[]{:S(2)}) %collective-permute-start.33) | collective-permute-done | bytes 393248 | tf_op jit(solution)/shard_map/ppermute | solution.py:32
  190.2 1.0 next_level.68
  191.3 3.8 %collective-permute-start.35 = (f32[384,256]{1,0:T(8,128)S(1)}, f32[384,256]{1,0:T(8,128)S(1)}, u32[]{:S(2)}, u32[]{:S(2)}) collective-permute-start(f32[384,256]{1,0:T(8,128)S(1)} %get-tuple-element.270), channel_id=1, source_target_pairs={{0,128},{128,0},{1,129},{129,1},{2,130},{130,2},{3,131},{131,3},{4... | collective-permute-start | bytes 1179656 | tf_op jit(solution)/shard_map/ppermute | solution.py:32
  195.5 1.0 next_level.69
  196.6 4.3 %collective-permute-start.36 = (f32[384,256]{1,0:T(8,128)S(1)}, f32[384,256]{1,0:T(8,128)S(1)}, u32[]{:S(2)}, u32[]{:S(2)}) collective-permute-start(f32[384,256]{1,0:T(8,128)S(1)} %get-tuple-element.274), channel_id=1, source_target_pairs={{0,128},{128,0},{1,129},{129,1},{2,130},{130,2},{3,131},{131,3},{4... | collective-permute-start | bytes 1179656 | tf_op jit(solution)/shard_map/ppermute | solution.py:32
  200.9 18.5 %collective-permute-done.35.arrived_ref = f32[384,256]{1,0:T(8,128)S(1)} collective-permute-done((f32[384,256]{1,0:T(8,128)S(1)}, f32[384,256]{1,0:T(8,128)S(1)}, u32[]{:S(2)}, u32[]{:S(2)}) %collective-permute-start.35) | collective-permute-done | bytes 393248 | tf_op jit(solution)/shard_map/ppermute | solution.py:32
  220.2 3.9 %collective-permute-done.36.arrived_ref = f32[384,256]{1,0:T(8,128)S(1)} collective-permute-done((f32[384,256]{1,0:T(8,128)S(1)}, f32[384,256]{1,0:T(8,128)S(1)}, u32[]{:S(2)}, u32[]{:S(2)}) %collective-permute-start.36) | collective-permute-done | bytes 393248 | tf_op jit(solution)/shard_map/ppermute | solution.py:32
  224.1 1.4 write_result.9
  (63 shorter events, 24.8 us)
Async XLA Ops:
  0.0 1.9 copy-start
  2.9 1.8 collective-permute-start
  5.8 11.6 %collective-permute-start.1 = (f32[384,256]{1,0:T(8,128)S(1)}, f32[384,256]{1,0:T(8,128)S(1)}, u32[]{:S(2)}, u32[]{:S(2)}) collective-permute-start(f32[384,256]{1,0:T(8,128)S(1)} %get-tuple-element.152), channel_id=1, source_target_pairs={{0,2},{2,0},{1,3},{3,1},{4,6},{6,4},{5,7},{7,5},{8,10},{10,8},{9,1... | collective-permute-start | bytes 1179656 | tf_op jit(solution)/shard_map/ppermute | solution.py:32
  18.5 12.3 %collective-permute-start.2 = (f32[384,256]{1,0:T(8,128)S(1)}, f32[384,256]{1,0:T(8,128)S(1)}, u32[]{:S(2)}, u32[]{:S(2)}) collective-permute-start(f32[384,256]{1,0:T(8,128)S(1)} %get-tuple-element.158), channel_id=1, source_target_pairs={{0,4},{4,0},{1,5},{5,1},{2,6},{6,2},{3,7},{7,3},{8,12},{12,8},{9,1... | collective-permute-start | bytes 1179656 | tf_op jit(solution)/shard_map/ppermute | solution.py:32
  24.8 10.0 %collective-permute-start.3 = (f32[384,768]{1,0:T(8,128)S(1)}, f32[384,768]{1,0:T(8,128)S(1)}, u32[]{:S(2)}, u32[]{:S(2)}) collective-permute-start(f32[384,768]{1,0:T(8,128)S(1)} %get-tuple-element.162), channel_id=1, source_target_pairs={{0,1},{1,0},{2,3},{3,2},{4,5},{5,4},{6,7},{7,6},{8,9},{9,8},{10,11... | collective-permute-start | bytes 3538952 | tf_op jit(solution)/shard_map/ppermute | solution.py:32
  31.8 9.9 %collective-permute-start.4 = (f32[384,256]{1,0:T(8,128)S(1)}, f32[384,256]{1,0:T(8,128)S(1)}, u32[]{:S(2)}, u32[]{:S(2)}) collective-permute-start(f32[384,256]{1,0:T(8,128)S(1)} %get-tuple-element.167), channel_id=1, source_target_pairs={{0,8},{8,0},{1,9},{9,1},{2,10},{10,2},{3,11},{11,3},{4,12},{12,4},... | collective-permute-start | bytes 1179656 | tf_op jit(solution)/shard_map/ppermute | solution.py:32
  35.8 10.9 %collective-permute-start.5 = (f32[384,128]{1,0:T(8,128)S(1)}, f32[384,128]{1,0:T(8,128)S(1)}, u32[]{:S(2)}, u32[]{:S(2)}) collective-permute-start(f32[384,128]{1,0:T(8,128)S(1)} %get-tuple-element.171), channel_id=1, source_target_pairs={{0,2},{2,0},{1,3},{3,1},{4,6},{6,4},{5,7},{7,5},{8,10},{10,8},{9,1... | collective-permute-start | bytes 589832 | tf_op jit(solution)/shard_map/ppermute | solution.py:32
  38.4 11.7 %collective-permute-start.6 = (f32[384,128]{1,0:T(8,128)S(1)}, f32[384,128]{1,0:T(8,128)S(1)}, u32[]{:S(2)}, u32[]{:S(2)}) collective-permute-start(f32[384,128]{1,0:T(8,128)S(1)} %get-tuple-element.174), channel_id=1, source_target_pairs={{0,2},{2,0},{1,3},{3,1},{4,6},{6,4},{5,7},{7,5},{8,10},{10,8},{9,1... | collective-permute-start | bytes 589832 | tf_op jit(solution)/shard_map/ppermute | solution.py:32
  42.8 16.4 %collective-permute-start.8 = (f32[384,256]{1,0:T(8,128)S(1)}, f32[384,256]{1,0:T(8,128)S(1)}, u32[]{:S(2)}, u32[]{:S(2)}) collective-permute-start(f32[384,256]{1,0:T(8,128)S(1)} %get-tuple-element.181), channel_id=1, source_target_pairs={{0,16},{16,0},{1,17},{17,1},{2,18},{18,2},{3,19},{19,3},{4,20},{20... | collective-permute-start | bytes 1179656 | tf_op jit(solution)/shard_map/ppermute | solution.py:32
  47.7 9.1 %collective-permute-start.7 = (f32[384,128]{1,0:T(8,128)S(1)}, f32[384,128]{1,0:T(8,128)S(1)}, u32[]{:S(2)}, u32[]{:S(2)}) collective-permute-start(f32[384,128]{1,0:T(8,128)S(1)} %get-tuple-element.177), channel_id=1, source_target_pairs={{0,4},{4,0},{1,5},{5,1},{2,6},{6,2},{3,7},{7,3},{8,12},{12,8},{9,1... | collective-permute-start | bytes 589832 | tf_op jit(solution)/shard_map/ppermute | solution.py:32
  51.0 13.0 %collective-permute-start.9 = (f32[384,128]{1,0:T(8,128)S(1)}, f32[384,128]{1,0:T(8,128)S(1)}, u32[]{:S(2)}, u32[]{:S(2)}) collective-permute-start(f32[384,128]{1,0:T(8,128)S(1)} %get-tuple-element.185), channel_id=1, source_target_pairs={{0,4},{4,0},{1,5},{5,1},{2,6},{6,2},{3,7},{7,3},{8,12},{12,8},{9,1... | collective-permute-start | bytes 589832 | tf_op jit(solution)/shard_map/ppermute | solution.py:32
  57.7 9.5 %collective-permute-start.10 = (f32[384,128]{1,0:T(8,128)S(1)}, f32[384,128]{1,0:T(8,128)S(1)}, u32[]{:S(2)}, u32[]{:S(2)}) collective-permute-start(f32[384,128]{1,0:T(8,128)S(1)} %get-tuple-element.189), channel_id=1, source_target_pairs={{0,8},{8,0},{1,9},{9,1},{2,10},{10,2},{3,11},{11,3},{4,12},{12,4},... | collective-permute-start | bytes 589832 | tf_op jit(solution)/shard_map/ppermute | solution.py:32
  60.2 9.4 %collective-permute-start.11 = (f32[384,256]{1,0:T(8,128)S(1)}, f32[384,256]{1,0:T(8,128)S(1)}, u32[]{:S(2)}, u32[]{:S(2)}) collective-permute-start(f32[384,256]{1,0:T(8,128)S(1)} %get-tuple-element.193), channel_id=1, source_target_pairs={{0,32},{32,0},{1,33},{33,1},{2,34},{34,2},{3,35},{35,3},{4,36},{36... | collective-permute-start | bytes 1179656 | tf_op jit(solution)/shard_map/ppermute | solution.py:32
  64.9 14.4 %collective-permute-start.14 = (f32[384,128]{1,0:T(8,128)S(1)}, f32[384,128]{1,0:T(8,128)S(1)}, u32[]{:S(2)}, u32[]{:S(2)}) collective-permute-start(f32[384,128]{1,0:T(8,128)S(1)} %get-tuple-element.203), channel_id=1, source_target_pairs={{0,8},{8,0},{1,9},{9,1},{2,10},{10,2},{3,11},{11,3},{4,12},{12,4},... | collective-permute-start | bytes 589832 | tf_op jit(solution)/shard_map/ppermute | solution.py:32
  66.8 11.5 %collective-permute-start.13 = (f32[384,256]{1,0:T(8,128)S(1)}, f32[384,256]{1,0:T(8,128)S(1)}, u32[]{:S(2)}, u32[]{:S(2)}) collective-permute-start(f32[384,256]{1,0:T(8,128)S(1)} %get-tuple-element.200), channel_id=1, source_target_pairs={{0,2},{2,0},{1,3},{3,1},{4,6},{6,4},{5,7},{7,5},{8,10},{10,8},{9,1... | collective-permute-start | bytes 1179656 | tf_op jit(solution)/shard_map/ppermute | solution.py:32
  68.1 8.3 %collective-permute-start.12 = (f32[384,128]{1,0:T(8,128)S(1)}, f32[384,128]{1,0:T(8,128)S(1)}, u32[]{:S(2)}, u32[]{:S(2)}) collective-permute-start(f32[384,128]{1,0:T(8,128)S(1)} %get-tuple-element.197), channel_id=1, source_target_pairs={{0,16},{16,0},{1,17},{17,1},{2,18},{18,2},{3,19},{19,3},{4,20},{20... | collective-permute-start | bytes 589832 | tf_op jit(solution)/shard_map/ppermute | solution.py:32
  70.7 29.2 %collective-permute-start.18 = (f32[384,256]{1,0:T(8,128)S(1)}, f32[384,256]{1,0:T(8,128)S(1)}, u32[]{:S(2)}, u32[]{:S(2)}) collective-permute-start(f32[384,256]{1,0:T(8,128)S(1)} %get-tuple-element.216), channel_id=1, source_target_pairs={{0,64},{64,0},{1,65},{65,1},{2,66},{66,2},{3,67},{67,3},{4,68},{68... | collective-permute-start | bytes 1179656 | tf_op jit(solution)/shard_map/ppermute | solution.py:32
  77.3 13.3 %collective-permute-start.15 = (f32[384,128]{1,0:T(8,128)S(1)}, f32[384,128]{1,0:T(8,128)S(1)}, u32[]{:S(2)}, u32[]{:S(2)}) collective-permute-start(f32[384,128]{1,0:T(8,128)S(1)} %get-tuple-element.206), channel_id=1, source_target_pairs={{0,32},{32,0},{1,33},{33,1},{2,34},{34,2},{3,35},{35,3},{4,36},{36... | collective-permute-start | bytes 589832 | tf_op jit(solution)/shard_map/ppermute | solution.py:32
  80.3 11.3 %collective-permute-start.16 = (f32[384,128]{1,0:T(8,128)S(1)}, f32[384,128]{1,0:T(8,128)S(1)}, u32[]{:S(2)}, u32[]{:S(2)}) collective-permute-start(f32[384,128]{1,0:T(8,128)S(1)} %get-tuple-element.209), channel_id=1, source_target_pairs={{0,16},{16,0},{1,17},{17,1},{2,18},{18,2},{3,19},{19,3},{4,20},{20... | collective-permute-start | bytes 589832 | tf_op jit(solution)/shard_map/ppermute | solution.py:32
  81.1 11.6 %collective-permute-start.17 = (f32[384,256]{1,0:T(8,128)S(1)}, f32[384,256]{1,0:T(8,128)S(1)}, u32[]{:S(2)}, u32[]{:S(2)}) collective-permute-start(f32[384,256]{1,0:T(8,128)S(1)} %get-tuple-element.212), channel_id=1, source_target_pairs={{0,4},{4,0},{1,5},{5,1},{2,6},{6,2},{3,7},{7,3},{8,12},{12,8},{9,1... | collective-permute-start | bytes 1179656 | tf_op jit(solution)/shard_map/ppermute | solution.py:32
  92.5 31.2 %collective-permute-start.22 = (f32[384,128]{1,0:T(8,128)S(1)}, f32[384,128]{1,0:T(8,128)S(1)}, u32[]{:S(2)}, u32[]{:S(2)}) collective-permute-start(f32[384,128]{1,0:T(8,128)S(1)} %get-tuple-element.229), channel_id=1, source_target_pairs={{0,32},{32,0},{1,33},{33,1},{2,34},{34,2},{3,35},{35,3},{4,36},{36... | collective-permute-start | bytes 589832 | tf_op jit(solution)/shard_map/ppermute | solution.py:32
  92.6 52.1 %collective-permute-start.26 = (f32[384,128]{1,0:T(8,128)S(1)}, f32[384,128]{1,0:T(8,128)S(1)}, u32[]{:S(2)}, u32[]{:S(2)}) collective-permute-start(f32[384,128]{1,0:T(8,128)S(1)} %get-tuple-element.241), channel_id=1, source_target_pairs={{0,64},{64,0},{1,65},{65,1},{2,66},{66,2},{3,67},{67,3},{4,68},{68... | collective-permute-start | bytes 589832 | tf_op jit(solution)/shard_map/ppermute | solution.py:32
  93.8 14.6 %collective-permute-start.19 = (f32[384,256]{1,0:T(8,128)S(1)}, f32[384,256]{1,0:T(8,128)S(1)}, u32[]{:S(2)}, u32[]{:S(2)}) collective-permute-start(f32[384,256]{1,0:T(8,128)S(1)} %get-tuple-element.220), channel_id=1, source_target_pairs={{0,8},{8,0},{1,9},{9,1},{2,10},{10,2},{3,11},{11,3},{4,12},{12,4},... | collective-permute-start | bytes 1179656 | tf_op jit(solution)/shard_map/ppermute | solution.py:32
  102.0 9.4 %collective-permute-start.20 = (f32[384,256]{1,0:T(8,128)S(1)}, f32[384,256]{1,0:T(8,128)S(1)}, u32[]{:S(2)}, u32[]{:S(2)}) collective-permute-start(f32[384,256]{1,0:T(8,128)S(1)} %get-tuple-element.223), channel_id=1, source_target_pairs={{0,2},{2,0},{1,3},{3,1},{4,6},{6,4},{5,7},{7,5},{8,10},{10,8},{9,1... | collective-permute-start | bytes 1179656 | tf_op jit(solution)/shard_map/ppermute | solution.py:32
  103.1 56.0 %collective-permute-start.29 = (f32[384,256]{1,0:T(8,128)S(1)}, f32[384,256]{1,0:T(8,128)S(1)}, u32[]{:S(2)}, u32[]{:S(2)}) collective-permute-start(f32[384,256]{1,0:T(8,128)S(1)} %get-tuple-element.250), channel_id=1, source_target_pairs={{0,128},{128,0},{1,129},{129,1},{2,130},{130,2},{3,131},{131,3},{4... | collective-permute-start | bytes 1179656 | tf_op jit(solution)/shard_map/ppermute | solution.py:32
  109.4 13.3 %collective-permute-start.21 = (f32[384,256]{1,0:T(8,128)S(1)}, f32[384,256]{1,0:T(8,128)S(1)}, u32[]{:S(2)}, u32[]{:S(2)}) collective-permute-start(f32[384,256]{1,0:T(8,128)S(1)} %get-tuple-element.226), channel_id=1, source_target_pairs={{0,16},{16,0},{1,17},{17,1},{2,18},{18,2},{3,19},{19,3},{4,20},{20... | collective-permute-start | bytes 1179656 | tf_op jit(solution)/shard_map/ppermute | solution.py:32
  112.4 13.6 %collective-permute-start.23 = (f32[384,256]{1,0:T(8,128)S(1)}, f32[384,256]{1,0:T(8,128)S(1)}, u32[]{:S(2)}, u32[]{:S(2)}) collective-permute-start(f32[384,256]{1,0:T(8,128)S(1)} %get-tuple-element.232), channel_id=1, source_target_pairs={{0,4},{4,0},{1,5},{5,1},{2,6},{6,2},{3,7},{7,3},{8,12},{12,8},{9,1... | collective-permute-start | bytes 1179656 | tf_op jit(solution)/shard_map/ppermute | solution.py:32
  124.7 16.3 %collective-permute-start.24 = (f32[384,128]{1,0:T(8,128)S(1)}, f32[384,128]{1,0:T(8,128)S(1)}, u32[]{:S(2)}, u32[]{:S(2)}) collective-permute-start(f32[384,128]{1,0:T(8,128)S(1)} %get-tuple-element.235), channel_id=1, source_target_pairs={{0,64},{64,0},{1,65},{65,1},{2,66},{66,2},{3,67},{67,3},{4,68},{68... | collective-permute-start | bytes 589832 | tf_op jit(solution)/shard_map/ppermute | solution.py:32
  127.1 16.5 %collective-permute-start.25 = (f32[384,256]{1,0:T(8,128)S(1)}, f32[384,256]{1,0:T(8,128)S(1)}, u32[]{:S(2)}, u32[]{:S(2)}) collective-permute-start(f32[384,256]{1,0:T(8,128)S(1)} %get-tuple-element.238), channel_id=1, source_target_pairs={{0,8},{8,0},{1,9},{9,1},{2,10},{10,2},{3,11},{11,3},{4,12},{12,4},... | collective-permute-start | bytes 1179656 | tf_op jit(solution)/shard_map/ppermute | solution.py:32
  129.4 25.7 %collective-permute-start.28 = (f32[384,256]{1,0:T(8,128)S(1)}, f32[384,256]{1,0:T(8,128)S(1)}, u32[]{:S(2)}, u32[]{:S(2)}) collective-permute-start(f32[384,256]{1,0:T(8,128)S(1)} %get-tuple-element.247), channel_id=1, source_target_pairs={{0,32},{32,0},{1,33},{33,1},{2,34},{34,2},{3,35},{35,3},{4,36},{36... | collective-permute-start | bytes 1179656 | tf_op jit(solution)/shard_map/ppermute | solution.py:32
  141.9 18.0 %collective-permute-start.30 = (f32[384,128]{1,0:T(8,128)S(1)}, f32[384,128]{1,0:T(8,128)S(1)}, u32[]{:S(2)}, u32[]{:S(2)}) collective-permute-start(f32[384,128]{1,0:T(8,128)S(1)} %get-tuple-element.253), channel_id=1, source_target_pairs={{0,128},{128,0},{1,129},{129,1},{2,130},{130,2},{3,131},{131,3},{4... | collective-permute-start | bytes 589832 | tf_op jit(solution)/shard_map/ppermute | solution.py:32
  144.6 9.4 %collective-permute-start.27 = (f32[384,256]{1,0:T(8,128)S(1)}, f32[384,256]{1,0:T(8,128)S(1)}, u32[]{:S(2)}, u32[]{:S(2)}) collective-permute-start(f32[384,256]{1,0:T(8,128)S(1)} %get-tuple-element.244), channel_id=1, source_target_pairs={{0,16},{16,0},{1,17},{17,1},{2,18},{18,2},{3,19},{19,3},{4,20},{20... | collective-permute-start | bytes 1179656 | tf_op jit(solution)/shard_map/ppermute | solution.py:32
  145.6 22.8 %collective-permute-start.32 = (f32[384,128]{1,0:T(8,128)S(1)}, f32[384,128]{1,0:T(8,128)S(1)}, u32[]{:S(2)}, u32[]{:S(2)}) collective-permute-start(f32[384,128]{1,0:T(8,128)S(1)} %get-tuple-element.260), channel_id=1, source_target_pairs={{0,128},{128,0},{1,129},{129,1},{2,130},{130,2},{3,131},{131,3},{4... | collective-permute-start | bytes 589832 | tf_op jit(solution)/shard_map/ppermute | solution.py:32
  155.0 12.3 %collective-permute-start.31 = (f32[384,256]{1,0:T(8,128)S(1)}, f32[384,256]{1,0:T(8,128)S(1)}, u32[]{:S(2)}, u32[]{:S(2)}) collective-permute-start(f32[384,256]{1,0:T(8,128)S(1)} %get-tuple-element.257), channel_id=1, source_target_pairs={{0,32},{32,0},{1,33},{33,1},{2,34},{34,2},{3,35},{35,3},{4,36},{36... | collective-permute-start | bytes 1179656 | tf_op jit(solution)/shard_map/ppermute | solution.py:32
  156.1 34.1 %collective-permute-start.33 = (f32[384,256]{1,0:T(8,128)S(1)}, f32[384,256]{1,0:T(8,128)S(1)}, u32[]{:S(2)}, u32[]{:S(2)}) collective-permute-start(f32[384,256]{1,0:T(8,128)S(1)} %get-tuple-element.264), channel_id=1, source_target_pairs={{0,64},{64,0},{1,65},{65,1},{2,66},{66,2},{3,67},{67,3},{4,68},{68... | collective-permute-start | bytes 1179656 | tf_op jit(solution)/shard_map/ppermute | solution.py:32
  168.3 27.2 %collective-permute-start.34 = (f32[384,256]{1,0:T(8,128)S(1)}, f32[384,256]{1,0:T(8,128)S(1)}, u32[]{:S(2)}, u32[]{:S(2)}) collective-permute-start(f32[384,256]{1,0:T(8,128)S(1)} %get-tuple-element.267), channel_id=1, source_target_pairs={{0,64},{64,0},{1,65},{65,1},{2,66},{66,2},{3,67},{67,3},{4,68},{68... | collective-permute-start | bytes 1179656 | tf_op jit(solution)/shard_map/ppermute | solution.py:32
  191.3 28.1 %collective-permute-start.35 = (f32[384,256]{1,0:T(8,128)S(1)}, f32[384,256]{1,0:T(8,128)S(1)}, u32[]{:S(2)}, u32[]{:S(2)}) collective-permute-start(f32[384,256]{1,0:T(8,128)S(1)} %get-tuple-element.270), channel_id=1, source_target_pairs={{0,128},{128,0},{1,129},{129,1},{2,130},{130,2},{3,131},{131,3},{4... | collective-permute-start | bytes 1179656 | tf_op jit(solution)/shard_map/ppermute | solution.py:32
  196.6 27.6 %collective-permute-start.36 = (f32[384,256]{1,0:T(8,128)S(1)}, f32[384,256]{1,0:T(8,128)S(1)}, u32[]{:S(2)}, u32[]{:S(2)}) collective-permute-start(f32[384,256]{1,0:T(8,128)S(1)} %get-tuple-element.274), channel_id=1, source_target_pairs={{0,128},{128,0},{1,129},{129,1},{2,130},{130,2},{3,131},{131,3},{4... | collective-permute-start | bytes 1179656 | tf_op jit(solution)/shard_map/ppermute | solution.py:32

commit v4 on v3

--- a/solution.py
+++ b/solution.py
@@ -76,7 +76,7 @@
 
 def multiply(blocks, t_ref, part_refs, send_ref, keep_ref, stacked):
     rank = send_ref.shape[0]
-    step = 48
+    step = 128
 
     @pl.loop(0, rank // step)
     def _(i):
@@ -145,7 +145,7 @@
 
 def write_kernel(start, token_ref, kept_ref, arrived_ref, *refs):
     out_ref, next_ref, block, sem = refs[-4:]
-    step = 48
+    step = 128
 
     @pl.loop(0, block.shape[0] // step)
     def _(i):

time: 227 us -> 237 us (1.044)
  starting transfers between devices: 62.5 us -> 76 us
    ppermute x37, starting transfers between devices: 62.5 us -> 76 us  [partner(): return lax.ppermute(block, axis, route)]
  transfers between devices with their start and end apart: 37 -> 37, of which waited for: 14 -> 14; matrix products, arithmetic and copies ran while one was open for 0% -> 0% of each run, Pallas kernels for 22% -> 21%
where the time goes in v4:
time: 237 us
  waiting for transfers between devices  105 us (44%)
  starting transfers between devices  76 us (32%)
  Pallas kernels  55.3 us (23%)
    ppermute x37, waiting for transfers between devices, partner(): return lax.ppermute(block, axis, route)  105 us
    ppermute x37, starting transfers between devices, partner(): return lax.ppermute(block, axis, route)  76 us
    pallas_call x37, Pallas kernels, stage(): pl.pallas_call(kernel, out_shape=(block, block, TOKEN), in_specs=specs, o...  36.9 us
    pallas_call x8, Pallas kernels, split_matrices(): pl.pallas_call(split_kernel, grid=(1,), out_shape=(pltpu.VMEM((2 * rank,...  13.9 us
  transfers between devices with their start and end apart: 37, of which 14 were waited for; matrix products, arithmetic and copies ran while one was open for 0% of the time, Pallas kernels for 21%

profile of v4, /device:TPU:10, one launch (start us, length us, event | category | flops | bytes accessed | tf_op | source)
XLA Modules:
  0.0 236.6 jit_solution(16191562113391675346)
XLA Ops:
  0.0 1.8 split_matrices.8
  3.0 1.7 split_matrices.9
  4.7 1.0 next_level.35
  6.3 1.7 split_matrices.10
  8.0 9.3 %collective-permute-done.1.arrived_ref = f32[384,256]{1,0:T(8,128)S(1)} collective-permute-done((f32[384,256]{1,0:T(8,128)S(1)}, f32[384,256]{1,0:T(8,128)S(1)}, u32[]{:S(2)}, u32[]{:S(2)}) %collective-permute-start.1) | collective-permute-done | bytes 393248 | tf_op jit(solution)/shard_map/ppermute | solution.py:32
  17.4 1.0 next_level.36
  18.4 2.4 %collective-permute-start.2 = (f32[384,256]{1,0:T(8,128)S(1)}, f32[384,256]{1,0:T(8,128)S(1)}, u32[]{:S(2)}, u32[]{:S(2)}) collective-permute-start(f32[384,256]{1,0:T(8,128)S(1)} %get-tuple-element.158), channel_id=1, source_target_pairs={{0,4},{4,0},{1,5},{5,1},{2,6},{6,2},{3,7},{7,3},{8,12},{12,8},{9,1... | collective-permute-start | bytes 1179656 | tf_op jit(solution)/shard_map/ppermute | solution.py:32
  20.7 1.7 split_matrices.11
  22.5 2.2 first_level.3
  24.8 5.9 %collective-permute-done.2.arrived_ref = f32[384,256]{1,0:T(8,128)S(1)} collective-permute-done((f32[384,256]{1,0:T(8,128)S(1)}, f32[384,256]{1,0:T(8,128)S(1)}, u32[]{:S(2)}, u32[]{:S(2)}) %collective-permute-start.2) | collective-permute-done | bytes 393248 | tf_op jit(solution)/shard_map/ppermute | solution.py:32
  30.7 1.0 next_level.37
  31.7 1.3 collective-permute-start.4
  33.0 1.7 split_matrices.12
  35.6 1.6 collective-permute-start.5
  38.7 2.9 %collective-permute-done.4.arrived_ref = f32[384,256]{1,0:T(8,128)S(1)} collective-permute-done((f32[384,256]{1,0:T(8,128)S(1)}, f32[384,256]{1,0:T(8,128)S(1)}, u32[]{:S(2)}, u32[]{:S(2)}) %collective-permute-start.4) | collective-permute-done | bytes 393248 | tf_op jit(solution)/shard_map/ppermute | solution.py:32
  41.6 1.0 next_level.40
  42.7 2.2 collective-permute-start.8
  44.9 1.7 split_matrices.13
  47.5 2.4 %collective-permute-start.7 = (f32[384,128]{1,0:T(8,128)S(1)}, f32[384,128]{1,0:T(8,128)S(1)}, u32[]{:S(2)}, u32[]{:S(2)}) collective-permute-start(f32[384,128]{1,0:T(8,128)S(1)} %get-tuple-element.177), channel_id=1, source_target_pairs={{0,4},{4,0},{1,5},{5,1},{2,6},{6,2},{3,7},{7,3},{8,12},{12,8},{9,1... | collective-permute-start | bytes 589832 | tf_op jit(solution)/shard_map/ppermute | solution.py:32
  50.8 1.3 collective-permute-start.9
  52.1 4.4 %collective-permute-done.7.arrived_ref = f32[384,128]{1,0:T(8,128)S(1)} collective-permute-done((f32[384,128]{1,0:T(8,128)S(1)}, f32[384,128]{1,0:T(8,128)S(1)}, u32[]{:S(2)}, u32[]{:S(2)}) %collective-permute-start.7) | collective-permute-done | bytes 196640 | tf_op jit(solution)/shard_map/ppermute | solution.py:32
  57.5 1.5 collective-permute-start.10
  59.0 1.0 next_level.44
  60.0 2.2 collective-permute-start.11
  62.2 1.7 split_matrices.14
  65.5 1.0 next_level.46
  67.8 1.6 collective-permute-start.12
  69.3 1.0 next_level.48
  70.3 4.3 %collective-permute-start.18 = (f32[384,256]{1,0:T(8,128)S(1)}, f32[384,256]{1,0:T(8,128)S(1)}, u32[]{:S(2)}, u32[]{:S(2)}) collective-permute-start(f32[384,256]{1,0:T(8,128)S(1)} %get-tuple-element.216), channel_id=1, source_target_pairs={{0,64},{64,0},{1,65},{65,1},{2,66},{66,2},{3,67},{67,3},{4,68},{68... | collective-permute-start | bytes 1179656 | tf_op jit(solution)/shard_map/ppermute | solution.py:32
  74.7 1.7 split_matrices.15
  77.8 1.0 next_level.50
  80.7 1.8 collective-permute-start.17
  82.5 7.9 %collective-permute-done.15.arrived_ref = f32[384,128]{1,0:T(8,128)S(1)} collective-permute-done((f32[384,128]{1,0:T(8,128)S(1)}, f32[384,128]{1,0:T(8,128)S(1)}, u32[]{:S(2)}, u32[]{:S(2)}) %collective-permute-start.15) | collective-permute-done | bytes 196640 | tf_op jit(solution)/shard_map/ppermute | solution.py:32
  92.4 1.0 next_level.54
  93.4 5.9 %collective-permute-start.19 = (f32[384,256]{1,0:T(8,128)S(1)}, f32[384,256]{1,0:T(8,128)S(1)}, u32[]{:S(2)}, u32[]{:S(2)}) collective-permute-start(f32[384,256]{1,0:T(8,128)S(1)} %get-tuple-element.220), channel_id=1, source_target_pairs={{0,8},{8,0},{1,9},{9,1},{2,10},{10,2},{3,11},{11,3},{4,12},{12,4},... | collective-permute-start | bytes 1179656 | tf_op jit(solution)/shard_map/ppermute | solution.py:32
  99.3 1.0 next_level.55
  100.3 1.0 next_level.56
  101.4 1.1 collective-permute-start.20
  102.5 5.6 %collective-permute-start.29 = (f32[384,256]{1,0:T(8,128)S(1)}, f32[384,256]{1,0:T(8,128)S(1)}, u32[]{:S(2)}, u32[]{:S(2)}) collective-permute-start(f32[384,256]{1,0:T(8,128)S(1)} %get-tuple-element.250), channel_id=1, source_target_pairs={{0,128},{128,0},{1,129},{129,1},{2,130},{130,2},{3,131},{131,3},{4... | collective-permute-start | bytes 1179656 | tf_op jit(solution)/shard_map/ppermute | solution.py:32
  108.1 1.0 next_level.57
  109.4 1.4 collective-permute-done.20.arrived_ref
  110.9 1.0 next_level.58
  112.4 10.4 %collective-permute-done.21.arrived_ref = f32[384,256]{1,0:T(8,128)S(1)} collective-permute-done((f32[384,256]{1,0:T(8,128)S(1)}, f32[384,256]{1,0:T(8,128)S(1)}, u32[]{:S(2)}, u32[]{:S(2)}) %collective-permute-start.21) | collective-permute-done | bytes 393248 | tf_op jit(solution)/shard_map/ppermute | solution.py:32
  125.2 1.0 next_level.61
  126.2 2.3 collective-permute-start.25
  128.4 2.2 collective-permute-start.28
  130.6 8.8 %collective-permute-done.24.arrived_ref = f32[384,128]{1,0:T(8,128)S(1)} collective-permute-done((f32[384,128]{1,0:T(8,128)S(1)}, f32[384,128]{1,0:T(8,128)S(1)}, u32[]{:S(2)}, u32[]{:S(2)}) %collective-permute-start.24) | collective-permute-done | bytes 196640 | tf_op jit(solution)/shard_map/ppermute | solution.py:32
  140.3 2.1 collective-permute-start.30
  142.3 1.0 next_level.63
  144.4 4.0 %collective-permute-start.32 = (f32[384,128]{1,0:T(8,128)S(1)}, f32[384,128]{1,0:T(8,128)S(1)}, u32[]{:S(2)}, u32[]{:S(2)}) collective-permute-start(f32[384,128]{1,0:T(8,128)S(1)} %get-tuple-element.260), channel_id=1, source_target_pairs={{0,128},{128,0},{1,129},{129,1},{2,130},{130,2},{3,131},{131,3},{4... | collective-permute-start | bytes 589832 | tf_op jit(solution)/shard_map/ppermute | solution.py:32
  148.4 4.3 %collective-permute-done.27.arrived_ref = f32[384,256]{1,0:T(8,128)S(1)} collective-permute-done((f32[384,256]{1,0:T(8,128)S(1)}, f32[384,256]{1,0:T(8,128)S(1)}, u32[]{:S(2)}, u32[]{:S(2)}) %collective-permute-start.27) | collective-permute-done | bytes 393248 | tf_op jit(solution)/shard_map/ppermute | solution.py:32
  152.7 1.0 next_level.65
  153.9 1.0 next_level.66
  154.9 3.5 %collective-permute-start.33 = (f32[384,256]{1,0:T(8,128)S(1)}, f32[384,256]{1,0:T(8,128)S(1)}, u32[]{:S(2)}, u32[]{:S(2)}) collective-permute-start(f32[384,256]{1,0:T(8,128)S(1)} %get-tuple-element.264), channel_id=1, source_target_pairs={{0,64},{64,0},{1,65},{65,1},{2,66},{66,2},{3,67},{67,3},{4,68},{68... | collective-permute-start | bytes 1179656 | tf_op jit(solution)/shard_map/ppermute | solution.py:32
  159.9 6.1 %collective-permute-done.31.arrived_ref = f32[384,256]{1,0:T(8,128)S(1)} collective-permute-done((f32[384,256]{1,0:T(8,128)S(1)}, f32[384,256]{1,0:T(8,128)S(1)}, u32[]{:S(2)}, u32[]{:S(2)}) %collective-permute-start.31) | collective-permute-done | bytes 393248 | tf_op jit(solution)/shard_map/ppermute | solution.py:32
  166.0 1.0 next_level.67
  167.0 1.4 collective-permute-start.34
  169.1 20.4 %collective-permute-done.33.arrived_ref = f32[384,256]{1,0:T(8,128)S(1)} collective-permute-done((f32[384,256]{1,0:T(8,128)S(1)}, f32[384,256]{1,0:T(8,128)S(1)}, u32[]{:S(2)}, u32[]{:S(2)}) %collective-permute-start.33) | collective-permute-done | bytes 393248 | tf_op jit(solution)/shard_map/ppermute | solution.py:32
  189.5 1.0 next_level.68
  190.5 17.4 %collective-permute-start.35 = (f32[384,256]{1,0:T(8,128)S(1)}, f32[384,256]{1,0:T(8,128)S(1)}, u32[]{:S(2)}, u32[]{:S(2)}) collective-permute-start(f32[384,256]{1,0:T(8,128)S(1)} %get-tuple-element.270), channel_id=1, source_target_pairs={{0,128},{128,0},{1,129},{129,1},{2,130},{130,2},{3,131},{131,3},{4... | collective-permute-start | bytes 1179656 | tf_op jit(solution)/shard_map/ppermute | solution.py:32
  209.9 2.6 %collective-permute-start.36 = (f32[384,256]{1,0:T(8,128)S(1)}, f32[384,256]{1,0:T(8,128)S(1)}, u32[]{:S(2)}, u32[]{:S(2)}) collective-permute-start(f32[384,256]{1,0:T(8,128)S(1)} %get-tuple-element.274), channel_id=1, source_target_pairs={{0,128},{128,0},{1,129},{129,1},{2,130},{130,2},{3,131},{131,3},{4... | collective-permute-start | bytes 1179656 | tf_op jit(solution)/shard_map/ppermute | solution.py:32
  212.4 13.8 %collective-permute-done.35.arrived_ref = f32[384,256]{1,0:T(8,128)S(1)} collective-permute-done((f32[384,256]{1,0:T(8,128)S(1)}, f32[384,256]{1,0:T(8,128)S(1)}, u32[]{:S(2)}, u32[]{:S(2)}) %collective-permute-start.35) | collective-permute-done | bytes 393248 | tf_op jit(solution)/shard_map/ppermute | solution.py:32
  227.1 7.9 %collective-permute-done.36.arrived_ref = f32[384,256]{1,0:T(8,128)S(1)} collective-permute-done((f32[384,256]{1,0:T(8,128)S(1)}, f32[384,256]{1,0:T(8,128)S(1)}, u32[]{:S(2)}, u32[]{:S(2)}) %collective-permute-start.36) | collective-permute-done | bytes 393248 | tf_op jit(solution)/shard_map/ppermute | solution.py:32
  235.0 1.4 write_result.9
  (63 shorter events, 24.9 us)
Async XLA Ops:
  0.0 1.9 copy-start
  2.9 1.8 collective-permute-start
  5.7 11.6 %collective-permute-start.1 = (f32[384,256]{1,0:T(8,128)S(1)}, f32[384,256]{1,0:T(8,128)S(1)}, u32[]{:S(2)}, u32[]{:S(2)}) collective-permute-start(f32[384,256]{1,0:T(8,128)S(1)} %get-tuple-element.152), channel_id=1, source_target_pairs={{0,2},{2,0},{1,3},{3,1},{4,6},{6,4},{5,7},{7,5},{8,10},{10,8},{9,1... | collective-permute-start | bytes 1179656 | tf_op jit(solution)/shard_map/ppermute | solution.py:32
  18.4 12.3 %collective-permute-start.2 = (f32[384,256]{1,0:T(8,128)S(1)}, f32[384,256]{1,0:T(8,128)S(1)}, u32[]{:S(2)}, u32[]{:S(2)}) collective-permute-start(f32[384,256]{1,0:T(8,128)S(1)} %get-tuple-element.158), channel_id=1, source_target_pairs={{0,4},{4,0},{1,5},{5,1},{2,6},{6,2},{3,7},{7,3},{8,12},{12,8},{9,1... | collective-permute-start | bytes 1179656 | tf_op jit(solution)/shard_map/ppermute | solution.py:32
  24.7 10.0 %collective-permute-start.3 = (f32[384,768]{1,0:T(8,128)S(1)}, f32[384,768]{1,0:T(8,128)S(1)}, u32[]{:S(2)}, u32[]{:S(2)}) collective-permute-start(f32[384,768]{1,0:T(8,128)S(1)} %get-tuple-element.162), channel_id=1, source_target_pairs={{0,1},{1,0},{2,3},{3,2},{4,5},{5,4},{6,7},{7,6},{8,9},{9,8},{10,11... | collective-permute-start | bytes 3538952 | tf_op jit(solution)/shard_map/ppermute | solution.py:32
  31.7 9.9 %collective-permute-start.4 = (f32[384,256]{1,0:T(8,128)S(1)}, f32[384,256]{1,0:T(8,128)S(1)}, u32[]{:S(2)}, u32[]{:S(2)}) collective-permute-start(f32[384,256]{1,0:T(8,128)S(1)} %get-tuple-element.167), channel_id=1, source_target_pairs={{0,8},{8,0},{1,9},{9,1},{2,10},{10,2},{3,11},{11,3},{4,12},{12,4},... | collective-permute-start | bytes 1179656 | tf_op jit(solution)/shard_map/ppermute | solution.py:32
  35.6 11.0 %collective-permute-start.5 = (f32[384,128]{1,0:T(8,128)S(1)}, f32[384,128]{1,0:T(8,128)S(1)}, u32[]{:S(2)}, u32[]{:S(2)}) collective-permute-start(f32[384,128]{1,0:T(8,128)S(1)} %get-tuple-element.171), channel_id=1, source_target_pairs={{0,2},{2,0},{1,3},{3,1},{4,6},{6,4},{5,7},{7,5},{8,10},{10,8},{9,1... | collective-permute-start | bytes 589832 | tf_op jit(solution)/shard_map/ppermute | solution.py:32
  38.1 11.8 %collective-permute-start.6 = (f32[384,128]{1,0:T(8,128)S(1)}, f32[384,128]{1,0:T(8,128)S(1)}, u32[]{:S(2)}, u32[]{:S(2)}) collective-permute-start(f32[384,128]{1,0:T(8,128)S(1)} %get-tuple-element.174), channel_id=1, source_target_pairs={{0,2},{2,0},{1,3},{3,1},{4,6},{6,4},{5,7},{7,5},{8,10},{10,8},{9,1... | collective-permute-start | bytes 589832 | tf_op jit(solution)/shard_map/ppermute | solution.py:32
  42.7 16.3 %collective-permute-start.8 = (f32[384,256]{1,0:T(8,128)S(1)}, f32[384,256]{1,0:T(8,128)S(1)}, u32[]{:S(2)}, u32[]{:S(2)}) collective-permute-start(f32[384,256]{1,0:T(8,128)S(1)} %get-tuple-element.181), channel_id=1, source_target_pairs={{0,16},{16,0},{1,17},{17,1},{2,18},{18,2},{3,19},{19,3},{4,20},{20... | collective-permute-start | bytes 1179656 | tf_op jit(solution)/shard_map/ppermute | solution.py:32
  47.5 9.0 %collective-permute-start.7 = (f32[384,128]{1,0:T(8,128)S(1)}, f32[384,128]{1,0:T(8,128)S(1)}, u32[]{:S(2)}, u32[]{:S(2)}) collective-permute-start(f32[384,128]{1,0:T(8,128)S(1)} %get-tuple-element.177), channel_id=1, source_target_pairs={{0,4},{4,0},{1,5},{5,1},{2,6},{6,2},{3,7},{7,3},{8,12},{12,8},{9,1... | collective-permute-start | bytes 589832 | tf_op jit(solution)/shard_map/ppermute | solution.py:32
  50.8 13.1 %collective-permute-start.9 = (f32[384,128]{1,0:T(8,128)S(1)}, f32[384,128]{1,0:T(8,128)S(1)}, u32[]{:S(2)}, u32[]{:S(2)}) collective-permute-start(f32[384,128]{1,0:T(8,128)S(1)} %get-tuple-element.185), channel_id=1, source_target_pairs={{0,4},{4,0},{1,5},{5,1},{2,6},{6,2},{3,7},{7,3},{8,12},{12,8},{9,1... | collective-permute-start | bytes 589832 | tf_op jit(solution)/shard_map/ppermute | solution.py:32
  57.5 9.4 %collective-permute-start.10 = (f32[384,128]{1,0:T(8,128)S(1)}, f32[384,128]{1,0:T(8,128)S(1)}, u32[]{:S(2)}, u32[]{:S(2)}) collective-permute-start(f32[384,128]{1,0:T(8,128)S(1)} %get-tuple-element.189), channel_id=1, source_target_pairs={{0,8},{8,0},{1,9},{9,1},{2,10},{10,2},{3,11},{11,3},{4,12},{12,4},... | collective-permute-start | bytes 589832 | tf_op jit(solution)/shard_map/ppermute | solution.py:32
  60.0 9.3 %collective-permute-start.11 = (f32[384,256]{1,0:T(8,128)S(1)}, f32[384,256]{1,0:T(8,128)S(1)}, u32[]{:S(2)}, u32[]{:S(2)}) collective-permute-start(f32[384,256]{1,0:T(8,128)S(1)} %get-tuple-element.193), channel_id=1, source_target_pairs={{0,32},{32,0},{1,33},{33,1},{2,34},{34,2},{3,35},{35,3},{4,36},{36... | collective-permute-start | bytes 1179656 | tf_op jit(solution)/shard_map/ppermute | solution.py:32
  64.8 14.0 %collective-permute-start.14 = (f32[384,128]{1,0:T(8,128)S(1)}, f32[384,128]{1,0:T(8,128)S(1)}, u32[]{:S(2)}, u32[]{:S(2)}) collective-permute-start(f32[384,128]{1,0:T(8,128)S(1)} %get-tuple-element.203), channel_id=1, source_target_pairs={{0,8},{8,0},{1,9},{9,1},{2,10},{10,2},{3,11},{11,3},{4,12},{12,4},... | collective-permute-start | bytes 589832 | tf_op jit(solution)/shard_map/ppermute | solution.py:32
  66.5 11.3 %collective-permute-start.13 = (f32[384,256]{1,0:T(8,128)S(1)}, f32[384,256]{1,0:T(8,128)S(1)}, u32[]{:S(2)}, u32[]{:S(2)}) collective-permute-start(f32[384,256]{1,0:T(8,128)S(1)} %get-tuple-element.200), channel_id=1, source_target_pairs={{0,2},{2,0},{1,3},{3,1},{4,6},{6,4},{5,7},{7,5},{8,10},{10,8},{9,1... | collective-permute-start | bytes 1179656 | tf_op jit(solution)/shard_map/ppermute | solution.py:32
  67.8 8.6 %collective-permute-start.12 = (f32[384,128]{1,0:T(8,128)S(1)}, f32[384,128]{1,0:T(8,128)S(1)}, u32[]{:S(2)}, u32[]{:S(2)}) collective-permute-start(f32[384,128]{1,0:T(8,128)S(1)} %get-tuple-element.197), channel_id=1, source_target_pairs={{0,16},{16,0},{1,17},{17,1},{2,18},{18,2},{3,19},{19,3},{4,20},{20... | collective-permute-start | bytes 589832 | tf_op jit(solution)/shard_map/ppermute | solution.py:32
  70.3 29.0 %collective-permute-start.18 = (f32[384,256]{1,0:T(8,128)S(1)}, f32[384,256]{1,0:T(8,128)S(1)}, u32[]{:S(2)}, u32[]{:S(2)}) collective-permute-start(f32[384,256]{1,0:T(8,128)S(1)} %get-tuple-element.216), channel_id=1, source_target_pairs={{0,64},{64,0},{1,65},{65,1},{2,66},{66,2},{3,67},{67,3},{4,68},{68... | collective-permute-start | bytes 1179656 | tf_op jit(solution)/shard_map/ppermute | solution.py:32
  77.3 13.0 %collective-permute-start.15 = (f32[384,128]{1,0:T(8,128)S(1)}, f32[384,128]{1,0:T(8,128)S(1)}, u32[]{:S(2)}, u32[]{:S(2)}) collective-permute-start(f32[384,128]{1,0:T(8,128)S(1)} %get-tuple-element.206), channel_id=1, source_target_pairs={{0,32},{32,0},{1,33},{33,1},{2,34},{34,2},{3,35},{35,3},{4,36},{36... | collective-permute-start | bytes 589832 | tf_op jit(solution)/shard_map/ppermute | solution.py:32
  79.8 11.5 %collective-permute-start.16 = (f32[384,128]{1,0:T(8,128)S(1)}, f32[384,128]{1,0:T(8,128)S(1)}, u32[]{:S(2)}, u32[]{:S(2)}) collective-permute-start(f32[384,128]{1,0:T(8,128)S(1)} %get-tuple-element.209), channel_id=1, source_target_pairs={{0,16},{16,0},{1,17},{17,1},{2,18},{18,2},{3,19},{19,3},{4,20},{20... | collective-permute-start | bytes 589832 | tf_op jit(solution)/shard_map/ppermute | solution.py:32
  80.7 11.7 %collective-permute-start.17 = (f32[384,256]{1,0:T(8,128)S(1)}, f32[384,256]{1,0:T(8,128)S(1)}, u32[]{:S(2)}, u32[]{:S(2)}) collective-permute-start(f32[384,256]{1,0:T(8,128)S(1)} %get-tuple-element.212), channel_id=1, source_target_pairs={{0,4},{4,0},{1,5},{5,1},{2,6},{6,2},{3,7},{7,3},{8,12},{12,8},{9,1... | collective-permute-start | bytes 1179656 | tf_op jit(solution)/shard_map/ppermute | solution.py:32
  92.1 31.7 %collective-permute-start.22 = (f32[384,128]{1,0:T(8,128)S(1)}, f32[384,128]{1,0:T(8,128)S(1)}, u32[]{:S(2)}, u32[]{:S(2)}) collective-permute-start(f32[384,128]{1,0:T(8,128)S(1)} %get-tuple-element.229), channel_id=1, source_target_pairs={{0,32},{32,0},{1,33},{33,1},{2,34},{34,2},{3,35},{35,3},{4,36},{36... | collective-permute-start | bytes 589832 | tf_op jit(solution)/shard_map/ppermute | solution.py:32
  92.2 51.2 %collective-permute-start.26 = (f32[384,128]{1,0:T(8,128)S(1)}, f32[384,128]{1,0:T(8,128)S(1)}, u32[]{:S(2)}, u32[]{:S(2)}) collective-permute-start(f32[384,128]{1,0:T(8,128)S(1)} %get-tuple-element.241), channel_id=1, source_target_pairs={{0,64},{64,0},{1,65},{65,1},{2,66},{66,2},{3,67},{67,3},{4,68},{68... | collective-permute-start | bytes 589832 | tf_op jit(solution)/shard_map/ppermute | solution.py:32
  93.4 14.7 %collective-permute-start.19 = (f32[384,256]{1,0:T(8,128)S(1)}, f32[384,256]{1,0:T(8,128)S(1)}, u32[]{:S(2)}, u32[]{:S(2)}) collective-permute-start(f32[384,256]{1,0:T(8,128)S(1)} %get-tuple-element.220), channel_id=1, source_target_pairs={{0,8},{8,0},{1,9},{9,1},{2,10},{10,2},{3,11},{11,3},{4,12},{12,4},... | collective-permute-start | bytes 1179656 | tf_op jit(solution)/shard_map/ppermute | solution.py:32
  101.4 9.5 %collective-permute-start.20 = (f32[384,256]{1,0:T(8,128)S(1)}, f32[384,256]{1,0:T(8,128)S(1)}, u32[]{:S(2)}, u32[]{:S(2)}) collective-permute-start(f32[384,256]{1,0:T(8,128)S(1)} %get-tuple-element.223), channel_id=1, source_target_pairs={{0,2},{2,0},{1,3},{3,1},{4,6},{6,4},{5,7},{7,5},{8,10},{10,8},{9,1... | collective-permute-start | bytes 1179656 | tf_op jit(solution)/shard_map/ppermute | solution.py:32
  102.5 55.9 %collective-permute-start.29 = (f32[384,256]{1,0:T(8,128)S(1)}, f32[384,256]{1,0:T(8,128)S(1)}, u32[]{:S(2)}, u32[]{:S(2)}) collective-permute-start(f32[384,256]{1,0:T(8,128)S(1)} %get-tuple-element.250), channel_id=1, source_target_pairs={{0,128},{128,0},{1,129},{129,1},{2,130},{130,2},{3,131},{131,3},{4... | collective-permute-start | bytes 1179656 | tf_op jit(solution)/shard_map/ppermute | solution.py:32
  109.1 13.7 %collective-permute-start.21 = (f32[384,256]{1,0:T(8,128)S(1)}, f32[384,256]{1,0:T(8,128)S(1)}, u32[]{:S(2)}, u32[]{:S(2)}) collective-permute-start(f32[384,256]{1,0:T(8,128)S(1)} %get-tuple-element.226), channel_id=1, source_target_pairs={{0,16},{16,0},{1,17},{17,1},{2,18},{18,2},{3,19},{19,3},{4,20},{20... | collective-permute-start | bytes 1179656 | tf_op jit(solution)/shard_map/ppermute | solution.py:32
  111.9 13.3 %collective-permute-start.23 = (f32[384,256]{1,0:T(8,128)S(1)}, f32[384,256]{1,0:T(8,128)S(1)}, u32[]{:S(2)}, u32[]{:S(2)}) collective-permute-start(f32[384,256]{1,0:T(8,128)S(1)} %get-tuple-element.232), channel_id=1, source_target_pairs={{0,4},{4,0},{1,5},{5,1},{2,6},{6,2},{3,7},{7,3},{8,12},{12,8},{9,1... | collective-permute-start | bytes 1179656 | tf_op jit(solution)/shard_map/ppermute | solution.py:32
  124.8 14.6 %collective-permute-start.24 = (f32[384,128]{1,0:T(8,128)S(1)}, f32[384,128]{1,0:T(8,128)S(1)}, u32[]{:S(2)}, u32[]{:S(2)}) collective-permute-start(f32[384,128]{1,0:T(8,128)S(1)} %get-tuple-element.235), channel_id=1, source_target_pairs={{0,64},{64,0},{1,65},{65,1},{2,66},{66,2},{3,67},{67,3},{4,68},{68... | collective-permute-start | bytes 589832 | tf_op jit(solution)/shard_map/ppermute | solution.py:32
  126.2 16.2 %collective-permute-start.25 = (f32[384,256]{1,0:T(8,128)S(1)}, f32[384,256]{1,0:T(8,128)S(1)}, u32[]{:S(2)}, u32[]{:S(2)}) collective-permute-start(f32[384,256]{1,0:T(8,128)S(1)} %get-tuple-element.238), channel_id=1, source_target_pairs={{0,8},{8,0},{1,9},{9,1},{2,10},{10,2},{3,11},{11,3},{4,12},{12,4},... | collective-permute-start | bytes 1179656 | tf_op jit(solution)/shard_map/ppermute | solution.py:32
  128.4 25.4 %collective-permute-start.28 = (f32[384,256]{1,0:T(8,128)S(1)}, f32[384,256]{1,0:T(8,128)S(1)}, u32[]{:S(2)}, u32[]{:S(2)}) collective-permute-start(f32[384,256]{1,0:T(8,128)S(1)} %get-tuple-element.247), channel_id=1, source_target_pairs={{0,32},{32,0},{1,33},{33,1},{2,34},{34,2},{3,35},{35,3},{4,36},{36... | collective-permute-start | bytes 1179656 | tf_op jit(solution)/shard_map/ppermute | solution.py:32
  140.3 18.9 %collective-permute-start.30 = (f32[384,128]{1,0:T(8,128)S(1)}, f32[384,128]{1,0:T(8,128)S(1)}, u32[]{:S(2)}, u32[]{:S(2)}) collective-permute-start(f32[384,128]{1,0:T(8,128)S(1)} %get-tuple-element.253), channel_id=1, source_target_pairs={{0,128},{128,0},{1,129},{129,1},{2,130},{130,2},{3,131},{131,3},{4... | collective-permute-start | bytes 589832 | tf_op jit(solution)/shard_map/ppermute | solution.py:32
  143.3 9.4 %collective-permute-start.27 = (f32[384,256]{1,0:T(8,128)S(1)}, f32[384,256]{1,0:T(8,128)S(1)}, u32[]{:S(2)}, u32[]{:S(2)}) collective-permute-start(f32[384,256]{1,0:T(8,128)S(1)} %get-tuple-element.244), channel_id=1, source_target_pairs={{0,16},{16,0},{1,17},{17,1},{2,18},{18,2},{3,19},{19,3},{4,20},{20... | collective-permute-start | bytes 1179656 | tf_op jit(solution)/shard_map/ppermute | solution.py:32
  144.4 24.0 %collective-permute-start.32 = (f32[384,128]{1,0:T(8,128)S(1)}, f32[384,128]{1,0:T(8,128)S(1)}, u32[]{:S(2)}, u32[]{:S(2)}) collective-permute-start(f32[384,128]{1,0:T(8,128)S(1)} %get-tuple-element.260), channel_id=1, source_target_pairs={{0,128},{128,0},{1,129},{129,1},{2,130},{130,2},{3,131},{131,3},{4... | collective-permute-start | bytes 589832 | tf_op jit(solution)/shard_map/ppermute | solution.py:32
  153.7 12.3 %collective-permute-start.31 = (f32[384,256]{1,0:T(8,128)S(1)}, f32[384,256]{1,0:T(8,128)S(1)}, u32[]{:S(2)}, u32[]{:S(2)}) collective-permute-start(f32[384,256]{1,0:T(8,128)S(1)} %get-tuple-element.257), channel_id=1, source_target_pairs={{0,32},{32,0},{1,33},{33,1},{2,34},{34,2},{3,35},{35,3},{4,36},{36... | collective-permute-start | bytes 1179656 | tf_op jit(solution)/shard_map/ppermute | solution.py:32
  154.9 34.7 %collective-permute-start.33 = (f32[384,256]{1,0:T(8,128)S(1)}, f32[384,256]{1,0:T(8,128)S(1)}, u32[]{:S(2)}, u32[]{:S(2)}) collective-permute-start(f32[384,256]{1,0:T(8,128)S(1)} %get-tuple-element.264), channel_id=1, source_target_pairs={{0,64},{64,0},{1,65},{65,1},{2,66},{66,2},{3,67},{67,3},{4,68},{68... | collective-permute-start | bytes 1179656 | tf_op jit(solution)/shard_map/ppermute | solution.py:32
  167.0 41.8 %collective-permute-start.34 = (f32[384,256]{1,0:T(8,128)S(1)}, f32[384,256]{1,0:T(8,128)S(1)}, u32[]{:S(2)}, u32[]{:S(2)}) collective-permute-start(f32[384,256]{1,0:T(8,128)S(1)} %get-tuple-element.267), channel_id=1, source_target_pairs={{0,64},{64,0},{1,65},{65,1},{2,66},{66,2},{3,67},{67,3},{4,68},{68... | collective-permute-start | bytes 1179656 | tf_op jit(solution)/shard_map/ppermute | solution.py:32
  190.5 35.7 %collective-permute-start.35 = (f32[384,256]{1,0:T(8,128)S(1)}, f32[384,256]{1,0:T(8,128)S(1)}, u32[]{:S(2)}, u32[]{:S(2)}) collective-permute-start(f32[384,256]{1,0:T(8,128)S(1)} %get-tuple-element.270), channel_id=1, source_target_pairs={{0,128},{128,0},{1,129},{129,1},{2,130},{130,2},{3,131},{131,3},{4... | collective-permute-start | bytes 1179656 | tf_op jit(solution)/shard_map/ppermute | solution.py:32
  209.9 25.1 %collective-permute-start.36 = (f32[384,256]{1,0:T(8,128)S(1)}, f32[384,256]{1,0:T(8,128)S(1)}, u32[]{:S(2)}, u32[]{:S(2)}) collective-permute-start(f32[384,256]{1,0:T(8,128)S(1)} %get-tuple-element.274), channel_id=1, source_target_pairs={{0,128},{128,0},{1,129},{129,1},{2,130},{130,2},{3,131},{131,3},{4... | collective-permute-start | bytes 1179656 | tf_op jit(solution)/shard_map/ppermute | solution.py:32
